TPU v7x, 32 devices: a whole 2x2x4 slice. The times are simulated.
32 devices in a mesh: dp: 16 (over z, x, core), tensor: 2 (over y).
Axes of the slice: x: 2, y: 2, z: 4, core: 2. Of those that a mesh axis runs over, the one named last changes fastest.
Arguments:
- inputs: bfloat16 [640, 64, 1024], P('tensor', 'dp'), may hold values from -6 to 6
- pad_mask: int32 [64, 640], P('dp'), may hold values from 0 to 1, as said below
- norm1_gain: bfloat16 [2, 512], P('tensor', 'dp'), may hold values from 0.099609375 to 1.8984375
- norm1_shift: bfloat16 [2, 512], P('tensor', 'dp'), may hold values from -3 to 3
- qkv_weight: bfloat16 [1024, 3, 1024], P('dp', None, 'tensor'), may hold values from -0.1875 to 0.1875
- qv_bias: bfloat16 [2, 2, 512], P(None, 'tensor', 'dp'), may hold values from -3 to 3
- out_weight: bfloat16 [1024, 1024], P('tensor', 'dp'), may hold values from -3 to 3
- out_bias: bfloat16 [2, 512], P('tensor', 'dp'), may hold values from -3 to 3
- norm2_gain: bfloat16 [2, 512], P('tensor', 'dp'), may hold values from 0.099609375 to 1.8984375
- norm2_shift: bfloat16 [2, 512], P('tensor', 'dp'), may hold values from -3 to 3
- up_weight: bfloat16 [1024, 4096], P('dp', 'tensor'), may hold values from -0.1875 to 0.1875
- up_bias: bfloat16 [2, 2048], P('tensor', 'dp'), may hold values from -3 to 3
- down_weight: bfloat16 [4096, 1024], P('tensor', 'dp'), may hold values from -0.09375 to 0.09375
- down_bias: bfloat16 [2, 512], P('tensor', 'dp'), may hold values from -3 to 3
- cotangent: float32 [640, 64, 1024], P('tensor', 'dp'), may hold values from -6 to 6
Outputs:
- block_output: float32 [640, 64, 1024], P('tensor', 'dp')
- input_grad: float32 [640, 64, 1024], P('tensor', 'dp')
- gain_one_grad: float32 [2, 512], P('tensor', 'dp')
- shift_one_grad: float32 [2, 512], P('tensor', 'dp')
- qkv_weight_grad: float32 [1024, 3, 1024], P('dp', None, 'tensor')
- qv_bias_grad: float32 [2, 2, 512], P(None, 'tensor', 'dp')
- out_weight_grad: float32 [1024, 1024], P('tensor', 'dp')
- out_bias_grad: float32 [2, 512], P('tensor', 'dp')
- gain_two_grad: float32 [2, 512], P('tensor', 'dp')
- shift_two_grad: float32 [2, 512], P('tensor', 'dp')
- up_weight_grad: float32 [1024, 4096], P('dp', 'tensor')
- up_bias_grad: float32 [2, 2048], P('tensor', 'dp')
- down_weight_grad: float32 [4096, 1024], P('tensor', 'dp')
- down_bias_grad: float32 [2, 512], P('tensor', 'dp')
Inputs may be any that keep to these rules, and one draw needn't show every extreme that they name: `pad_mask`: each image's row holds ones on its first slots and zeros after them; it has between 289 and 577 ones, and image 0 has exactly 577.
All inputs are finite; a program needn't handle non-finite values.
Results may differ from a plain program's by a relative error of at most 0.0085.
The roundings to bfloat16 on the way count: a program that leaves them out, or rounds other values in their place, can miss the bound.
Values may be sent and summed in bfloat16 or wider, within the bound.
No kernel may reach another device: no remote copies, remote signals or barrier semaphores. Data moves between devices by JAX's collectives and lax.ppermute only.
A program may use at most 256 MiB of HBM per device.

v0:
```python
import jax
import jax.numpy as jnp
from jax import lax
from jax.sharding import PartitionSpec as P

HD = 64


epsilon = 1e-06
masked_score = -1e30


def layer_norm(values, gain, shift):
    row_mean = jnp.mean(values, axis=-1, keepdims=True)
    centred = values - row_mean
    spread = jnp.mean(centred * centred, axis=-1, keepdims=True)
    return centred * lax.rsqrt(spread + epsilon) * gain + shift


def gelu_exact(values):
    return jax.nn.gelu(values, approximate=False)


def image_scores(queries, key_rows, kept_row):
    scores = jnp.einsum(
        "qhe,khe->hqk", queries, key_rows, preferred_element_type=jnp.float32
    ) * HD ** (-0.5)
    return jnp.where(kept_row[None, None, :], scores, masked_score)


def forward_image(operands):
    queries, key_rows, value_rows, kept_row = operands
    scores = image_scores(queries, key_rows, kept_row)
    row_max = jnp.max(scores, axis=-1, keepdims=True)
    exps = jnp.exp(scores - row_max)
    row_total = jnp.sum(exps, axis=-1, keepdims=True)
    soft_weights = (exps / row_total).astype(jnp.bfloat16)
    attended = jnp.einsum(
        "hqk,khe->qhe", soft_weights, value_rows, preferred_element_type=jnp.float32
    )
    return (attended.astype(jnp.bfloat16), (row_max + jnp.log(row_total))[..., 0])


def backward_image(operands):
    queries, key_rows, value_rows, kept_row, log_total, attended_grad = operands
    seq_length = queries.shape[0]
    scores = image_scores(queries, key_rows, kept_row)
    soft_float = jnp.exp(scores - log_total[..., None])
    soft_weights = soft_float.astype(jnp.bfloat16)
    value_grad = jnp.einsum(
        "hqk,qhe->khe", soft_weights, attended_grad, preferred_element_type=jnp.float32
    )
    prob_grad = jnp.einsum(
        "qhe,khe->hqk", attended_grad, value_rows, preferred_element_type=jnp.float32
    )
    score_grad = soft_float * (prob_grad - jnp.sum(prob_grad * soft_float, axis=-1, keepdims=True))
    score_grad = score_grad.astype(jnp.bfloat16)
    query_grad = jnp.einsum(
        "hqk,khe->qhe", score_grad, key_rows, preferred_element_type=jnp.float32
    ) * HD ** (-0.5)
    key_grad = jnp.einsum(
        "hqk,qhe->khe", score_grad, queries, preferred_element_type=jnp.float32
    ) * HD ** (-0.5)
    joined = jnp.concatenate(
        [
            query_grad.reshape(seq_length, -1),
            key_grad.reshape(seq_length, -1),
            value_grad.reshape(seq_length, -1),
        ],
        axis=-1,
    )
    return joined.astype(jnp.bfloat16)


def on_device(
    inputs,
    pad_mask,
    norm1_gain,
    norm1_shift,
    qkv_weight,
    qv_bias,
    out_weight,
    out_bias,
    norm2_gain,
    norm2_shift,
    up_weight,
    up_bias,
    down_weight,
    down_bias,
    cotangent,
):
    local_rows = inputs.shape[0]
    image_count = inputs.shape[1]
    model_width = inputs.shape[2]
    seq_length = pad_mask.shape[1]
    tensor_count = lax.axis_size("tensor")
    vector_stack = jnp.stack(
        [norm1_gain, norm1_shift, out_bias, norm2_gain, norm2_shift, down_bias], axis=0
    )
    gathered = (
        lax.all_gather(qkv_weight, "dp", axis=0, tiled=True),
        lax.all_gather(out_weight, "dp", axis=1, tiled=True),
        lax.all_gather(up_weight, "dp", axis=0, tiled=True),
        lax.all_gather(down_weight, "dp", axis=1, tiled=True),
        lax.all_gather(qv_bias, "dp", axis=2, tiled=True),
        lax.all_gather(up_bias, "dp", axis=1, tiled=True),
        lax.all_gather(vector_stack, "dp", axis=2, tiled=True),
    )
    qkv_full, out_full, up_full, down_full, bias_pair, bias_hidden, vector_part = gathered
    local_width = qkv_full.shape[2]
    head_count = local_width // HD
    vector_rows = (
        lax.all_gather(vector_part, "tensor", axis=1, tiled=True)
        .reshape(6, model_width)
        .astype(jnp.float32)
    )
    gain_one, shift_one, out_shift, gain_two, shift_two, down_shift = [
        vector_rows[index] for index in range(6)
    ]
    qkv_matrix = qkv_full.reshape(model_width, 3 * local_width)
    bias_row = jnp.concatenate(
        [
            bias_pair[0, 0].astype(jnp.float32),
            jnp.zeros((local_width,), jnp.float32),
            bias_pair[1, 0].astype(jnp.float32),
        ]
    )
    up_row = bias_hidden.reshape(-1).astype(jnp.float32)
    kept_all = pad_mask > 0
    first_row = lax.axis_index("tensor") * local_rows
    kept_float = jnp.transpose(lax.dynamic_slice_in_dim(kept_all, first_row, local_rows, 1)).astype(
        jnp.float32
    )[:, :, None]
    input_float = inputs.astype(jnp.float32)
    normed_one = layer_norm(input_float, gain_one, shift_one).astype(jnp.bfloat16)
    normed_all = lax.all_gather(normed_one, "tensor", axis=0, tiled=True)
    qkv_rows = (
        jnp.einsum("sbd,dc->sbc", normed_all, qkv_matrix, preferred_element_type=jnp.float32)
        + bias_row
    )
    qkv_rows = qkv_rows.astype(jnp.bfloat16)
    qkv_images = jnp.swapaxes(qkv_rows, 0, 1).reshape(image_count, seq_length, 3, head_count, HD)
    query_all = qkv_images[:, :, 0]
    key_all = qkv_images[:, :, 1]
    value_all = qkv_images[:, :, 2]
    attended_img, log_totals = lax.map(forward_image, (query_all, key_all, value_all, kept_all))
    attended_rows = jnp.swapaxes(attended_img.reshape(image_count, seq_length, local_width), 0, 1)
    row_block = attended_rows
    projected = lax.psum_scatter(
        jnp.einsum("sbc,cd->sbd", row_block, out_full, preferred_element_type=jnp.float32),
        "tensor",
        scatter_dimension=0,
        tiled=True,
    )
    after_attn = input_float + projected + out_shift
    normed_two = layer_norm(after_attn, gain_two, shift_two).astype(jnp.bfloat16)
    normed_all_two = lax.all_gather(normed_two, "tensor", axis=0, tiled=True)
    up_values = (
        jnp.einsum("sbd,df->sbf", normed_all_two, up_full, preferred_element_type=jnp.float32)
        + up_row
    )
    activated = gelu_exact(up_values).astype(jnp.bfloat16)
    row_block = activated
    mlp_out = lax.psum_scatter(
        jnp.einsum("sbf,fd->sbd", row_block, down_full, preferred_element_type=jnp.float32),
        "tensor",
        scatter_dimension=0,
        tiled=True,
    )
    block_output = (after_attn + mlp_out + down_shift) * kept_float
    qkv_back, out_back, up_back, down_back = (qkv_matrix, out_full, up_full, down_full)
    out_grad = cotangent * kept_float
    down_shift_grad = jnp.sum(out_grad, axis=(0, 1))
    out_low = out_grad.astype(jnp.bfloat16)
    out_low_all = lax.all_gather(out_low, "tensor", axis=0, tiled=True)
    down_weight_grad = jnp.einsum(
        "sbf,sbd->fd", activated, out_low_all, preferred_element_type=jnp.float32
    )
    act_grad = jnp.einsum("sbd,fd->sbf", out_low_all, down_back, preferred_element_type=jnp.float32)
    _, gelu_back = jax.vjp(gelu_exact, up_values)
    up_grad = gelu_back(act_grad)[0].astype(jnp.bfloat16)
    up_shift_grad = jnp.sum(up_grad.astype(jnp.float32), axis=(0, 1))
    up_weight_grad = jnp.einsum(
        "sbd,sbf->df", normed_all_two, up_grad, preferred_element_type=jnp.float32
    )
    row_block = up_grad
    normed_two_grad = lax.psum_scatter(
        jnp.einsum("sbf,df->sbd", row_block, up_back, preferred_element_type=jnp.float32),
        "tensor",
        scatter_dimension=0,
        tiled=True,
    )
    _, norm_two_back = jax.vjp(layer_norm, after_attn, gain_two, shift_two)
    attn_side, gain_two_grad, shift_two_grad = norm_two_back(normed_two_grad)
    after_attn_grad = out_grad + attn_side
    out_shift_grad = jnp.sum(after_attn_grad, axis=(0, 1))
    proj_low = after_attn_grad.astype(jnp.bfloat16)
    proj_low_all = lax.all_gather(proj_low, "tensor", axis=0, tiled=True)
    out_weight_grad = jnp.einsum(
        "sbc,sbd->cd", attended_rows, proj_low_all, preferred_element_type=jnp.float32
    )
    attended_grad = jnp.einsum(
        "sbd,cd->sbc", proj_low_all, out_back, preferred_element_type=jnp.float32
    )
    attended_grad = attended_grad.astype(jnp.bfloat16)
    attended_grad_img = jnp.swapaxes(attended_grad, 0, 1).reshape(
        image_count, seq_length, head_count, HD
    )
    qkv_grad_img = lax.map(
        backward_image, (query_all, key_all, value_all, kept_all, log_totals, attended_grad_img)
    )
    qkv_grad = jnp.swapaxes(qkv_grad_img, 0, 1)
    qkv_sums = jnp.sum(qkv_grad.astype(jnp.float32), axis=(0, 1))
    qv_grad = jnp.stack([qkv_sums[:local_width], qkv_sums[2 * local_width :]], axis=0).reshape(
        2, 1, local_width
    )
    qkv_weight_grad = jnp.einsum(
        "sbd,sbc->dc", normed_all, qkv_grad, preferred_element_type=jnp.float32
    )
    qkv_weight_grad = qkv_weight_grad.reshape(model_width, 3, local_width)
    row_block = qkv_grad
    normed_one_grad = lax.psum_scatter(
        jnp.einsum("sbc,dc->sbd", row_block, qkv_back, preferred_element_type=jnp.float32),
        "tensor",
        scatter_dimension=0,
        tiled=True,
    )
    _, norm_one_back = jax.vjp(layer_norm, input_float, gain_one, shift_one)
    input_side, gain_one_grad, shift_one_grad = norm_one_back(normed_one_grad)
    input_grad = after_attn_grad + input_side
    vector_grads = jnp.stack(
        [
            gain_one_grad,
            shift_one_grad,
            out_shift_grad,
            gain_two_grad,
            shift_two_grad,
            down_shift_grad,
        ],
        axis=0,
    ).reshape(6, tensor_count, model_width // tensor_count)
    vector_local = lax.psum_scatter(vector_grads, "tensor", scatter_dimension=1, tiled=True)
    owned = (
        lax.psum_scatter(qkv_weight_grad, "dp", scatter_dimension=0, tiled=True),
        lax.psum_scatter(out_weight_grad, "dp", scatter_dimension=1, tiled=True),
        lax.psum_scatter(up_weight_grad, "dp", scatter_dimension=0, tiled=True),
        lax.psum_scatter(down_weight_grad, "dp", scatter_dimension=1, tiled=True),
        lax.psum_scatter(qv_grad, "dp", scatter_dimension=2, tiled=True),
        lax.psum_scatter(up_shift_grad.reshape(1, -1), "dp", scatter_dimension=1, tiled=True),
        lax.psum_scatter(vector_local, "dp", scatter_dimension=2, tiled=True),
    )
    qkv_owned, out_owned, up_owned, down_owned, qv_owned, hidden_owned, vector_owned = owned
    return (
        block_output,
        input_grad,
        vector_owned[0],
        vector_owned[1],
        qkv_owned,
        qv_owned,
        out_owned,
        vector_owned[2],
        vector_owned[3],
        vector_owned[4],
        up_owned,
        hidden_owned,
        down_owned,
        vector_owned[5],
    )


def solution(mesh):
    in_specs = (
        P("tensor", "dp", None),
        P("dp", None),
        P("tensor", "dp"),
        P("tensor", "dp"),
        P("dp", None, "tensor"),
        P(None, "tensor", "dp"),
        P("tensor", "dp"),
        P("tensor", "dp"),
        P("tensor", "dp"),
        P("tensor", "dp"),
        P("dp", "tensor"),
        P("tensor", "dp"),
        P("tensor", "dp"),
        P("tensor", "dp"),
        P("tensor", "dp", None),
    )
    out_specs = (
        P("tensor", "dp", None),
        P("tensor", "dp", None),
        P("tensor", "dp"),
        P("tensor", "dp"),
        P("dp", None, "tensor"),
        P(None, "tensor", "dp"),
        P("tensor", "dp"),
        P("tensor", "dp"),
        P("tensor", "dp"),
        P("tensor", "dp"),
        P("dp", "tensor"),
        P("tensor", "dp"),
        P("tensor", "dp"),
        P("tensor", "dp"),
    )
    return jax.shard_map(
        on_device, mesh=mesh, in_specs=in_specs, out_specs=out_specs, check_vma=False
    )
```

profile of v0, /device:TPU:0, one launch (start us, length us, event | category | flops | bytes accessed | tf_op | source)
XLA Modules:
  0.0 1861.0 jit_solution(15390352596484088534)
XLA Ops:
  12.1 23.8 %all_gather.36 = bf16[6,1,512]{0,1,2:T(2,128)(2,1)S(1)} all-gather(bf16[6,1,32]{0,1,2:T(2,128)(2,1)S(1)} %copy.88), channel_id=1, replica_groups=mesh['dp'=16,'tensor'=2] {'dp'}, dimensions={2}, use_global_device_ids=true | all-gather | bytes 6528 | tf_op jit(solution)/shard_map/all_gather | solution.py:107
  49.8 18.0 all_gather.40
  73.5 54.6 %all-gather.9.cloned.1.call-done = bf16[640,4,1024]{2,0,1:T(8,128)(2,1)} async-done(((bf16[320,4,1024]{2,0,1:T(8,128)(2,1)}), bf16[640,4,1024]{2,0,1:T(8,128)(2,1)}) %all-gather.9.cloned.1.call-update) | async-done | bytes 5242896 | tf_op jit(solution)/shard_map/all_gather | solution.py:136
  128.1 12.9 fusion.50
  141.0 10.6 copy.93
  157.0 51.6 %while.22 = (s32[]{:T(128)}, bf16[4,640,8,64]{1,3,2,0:T(8,128)(2,1)}, f32[4,8,640]{2,1,0:T(8,128)}, bf16[4,640,8,64]{1,3,2,0:T(8,128)(2,1)}, pred[4,640]{1,0:T(4...) while((s32[]{:T(128)}, ...), condition=%wide.region_5.6_spmd, body=%wide.region_2.5_spmd.sunk | while | flops 878504960 | bytes 42113112 | solution.py:146
  213.6 8.9 fusion.80
  223.1 12.6 all-gather.15.cloned.1.call-start
  235.7 108.8 %reduce-scatter.18.cloned.1.call-done = f32[320,4,1024]{2,0,1:T(8,128)} async-done(((f32[640,4,1024]{2,0,1:T(8,128)}), f32[320,4,1024]{2,0,1:T(8,128)}) %reduce-scatter.18.cloned.1.call-update) | async-done | bytes 5242896 | tf_op jit(solution)/shard_map/reduce_scatter | solution.py:149
  353.2 7.3 fusion.77
  361.4 21.3 %all_gather.44 = bf16[1,2048]{1,0:T(2,128)(2,1)S(1)} all-gather(bf16[1,128]{1,0:T(2,128)(2,1)S(1)} %copy-done.29), channel_id=1, replica_groups=mesh['dp'=16,'tensor'=2] {'dp'}, dimensions={1}, use_global_device_ids=true | all-gather | bytes 4352 | tf_op jit(solution)/shard_map/all_gather | solution.py:106
  382.8 14.3 all-gather.17.cloned.1.call-done
  397.1 68.5 %all-gather.15.cloned.1.call-done = bf16[640,4,1024]{2,0,1:T(8,128)(2,1)} async-done(((bf16[320,4,1024]{2,0,1:T(8,128)(2,1)}), bf16[640,4,1024]{2,0,1:T(8,128)(2,1)}) %all-gather.15.cloned.1.call-update) | async-done | bytes 5242896 | tf_op jit(solution)/shard_map/all_gather | solution.py:157
  465.6 24.9 %fusion.68 = (u8[640,2048]{1,0:T(8,128)(4,1)S(1)}, u8[640,2048]{1,0:T(8,128)(4,1)S(1)}, f32[640,4,2048]{2,0,1:T(8,128)}) fusion(f32[2048]{0:T(1024)S(1)} %bitcast.227, bf16[640,4,1024]{2,0,1:T(8,128)(2,1)} %all-gather.15.cloned.1.call-done, bf16[1024,2048]{1,0:T(8,128)(2,1)} %all-gather.17.cloned.1.call-done), kind=kOutput, calls=%fused_computation.110 | convolution fusion | flops 10808197120 | bytes 33038336 | tf_op jit(solution)/shard_map/sbd,df->sbf/dot_general | solution.py:159
  490.5 51.1 %multiply_convert_fusion.1 = (bf16[640,4,2048]{2,0,1:T(8,128)(2,1)}, f32[640,4,2048]{2,0,1:T(8,128)}) fusion(f32[640,4,2048]{2,0,1:T(8,128)} %get-tuple-element.224, f32[2048]{0:T(1024)S(1)} %bitcast.228, u8[640,2048]{1,0:T(8,128)(4,1)S(1)} %get-tuple-element.154, u8[640,2048]{1,0:T(8,128)(4,1)S(1)} %get-tuple-element.153), kind=kLoop, calls=%fused_computation.64 | loop fusion | flops 372244480 | bytes 55058432 | tf_op jit(solution)/shard_map/convert_element_type | solution.py:162
  541.6 47.0 %all-gather.19.cloned.1.call-done = bf16[2048,1024]{0,1:T(8,128)(2,1)} async-done(((bf16[2048,64]{0,1:T(8,128)(2,1)}), bf16[2048,1024]{0,1:T(8,128)(2,1)}) %all-gather.19.cloned.1.call-update) | async-done | bytes 4194320 | tf_op jit(solution)/shard_map/all_gather | solution.py:104
  588.7 28.1 %convert_reduce_fusion = (f32[2048]{0:T(1024)}, bf16[640,4,2048]{2,0,1:T(8,128)(2,1)}) fusion(f32[640,4,2048]{2,0,1:T(8,128)} %get-tuple-element.198, bf16[640,4,1024]{2,0,1:T(8,128)(2,1)} %all-gather.21.cloned.1.call-done, bf16[2048,1024]{0,1:T(8,128)(2,1)} %all-gather.19.cloned.1.call-done, f32[640,4,2048]{2,0,1:T(8,128)} %get-tuple-element.224, ...), kind=kOutput, calls=%fused_computation.62 | convolution fusion | flops 10826545152 | bytes 61882368 | tf_op jit(solution)/shard_map/sbd,fd->sbf/dot_general | solution.py:179
  616.8 17.4 fusion.72
  634.2 17.5 fusion.70
  651.8 102.9 %reduce-scatter.22.cloned.1.call-done = f32[320,4,1024]{2,0,1:T(8,128)} async-done(((f32[640,4,1024]{2,0,1:T(8,128)}), f32[320,4,1024]{2,0,1:T(8,128)}) %reduce-scatter.22.cloned.1.call-update) | async-done | bytes 5242896 | tf_op jit(solution)/shard_map/reduce_scatter | solution.py:187
  754.7 6.0 fusion.93
  765.5 113.3 %reduce-scatter.20.cloned.1.call-done = f32[320,4,1024]{2,0,1:T(8,128)} async-done(((f32[640,4,1024]{2,0,1:T(8,128)}), f32[320,4,1024]{2,0,1:T(8,128)}) %reduce-scatter.20.cloned.1.call-update) | async-done | bytes 5242896 | tf_op jit(solution)/shard_map/reduce_scatter | solution.py:164
  878.7 11.7 fusion.95
  894.9 68.5 %all-gather.23.cloned.1.call-done = bf16[640,4,1024]{2,0,1:T(8,128)(2,1)} async-done(((bf16[320,4,1024]{2,0,1:T(8,128)(2,1)}), bf16[640,4,1024]{2,0,1:T(8,128)(2,1)}) %all-gather.23.cloned.1.call-update) | async-done | bytes 5242896 | tf_op jit(solution)/shard_map/all_gather | solution.py:198
  963.4 7.2 convolution_convert_fusion
  970.6 113.1 %while.23 = (s32[]{:T(128)}, bf16[4,640,1536]{1,2,0:T(8,128)(2,1)}, bf16[4,640,8,64]{1,3,2,0:T(8,128)(2,1)S(1)}, pred[4,640]{1,0:T(4,128)(4,1)S(1)}, bf16[4,640,...) while((s32[]{:T(128)}, bf16[4,640,1536]{1,2,0:T(8,128)(2,1)}, ...), condition=%wide.region_15.16_spmd, body=%wide.region_13.15_spmd.sunk | while | flops 2134174720 | bytes 108898144 | solution.py:209
  975.9 7.9 multiply_reduce_fusion.5
  983.7 5.9 multiply_convert_fusion.3
  1004.2 7.9 multiply_reduce_fusion.5
  1012.0 5.9 multiply_convert_fusion.3
  1032.4 7.9 multiply_reduce_fusion.5
  1040.3 5.9 multiply_convert_fusion.3
  1060.7 7.9 multiply_reduce_fusion.5
  1083.7 14.4 fusion.53
  1106.3 13.3 fusion.51
  1119.6 9.5 copy.100
  1130.5 89.7 %reduce-scatter.24.cloned.1.call-done = f32[320,4,1024]{2,0,1:T(8,128)} async-done(((f32[640,4,1024]{2,0,1:T(8,128)}), f32[320,4,1024]{2,0,1:T(8,128)}) %reduce-scatter.24.cloned.1.call-update) | async-done | bytes 5242896 | tf_op jit(solution)/shard_map/reduce_scatter | solution.py:222
  1228.3 7.3 all-reduce
  1241.2 17.4 convolution_bitcast_fusion.1
  1258.6 17.5 convolution_bitcast_fusion
  1276.4 7.6 fusion.83
  1286.7 8.2 copy.101
  1295.0 45.0 %reduce-scatter.34.cloned.1.call-done = f32[32,2]{1,0:T(8,128)} async-done(((f32[512,2]{1,0:T(8,128)}), f32[32,2]{1,0:T(8,128)}) %reduce-scatter.34.cloned.1.call-update) | async-done | bytes 272
  1341.4 171.6 %all-reduce.4.cloned.1.call-done = f32[1024,3,512]{2,1,0:T(4,128)} async-done(((f32[1024,3,512]{2,1,0:T(4,128)}), f32[1024,3,512]{2,1,0:T(4,128)}) %all-reduce.4.cloned.1.call-update) | async-done | bytes 6291472
  1526.0 45.6 %reduce-scatter.32.cloned.1.call-done = f32[32,6]{1,0:T(8,128)} async-done(((f32[512,6]{1,0:T(8,128)}), f32[32,6]{1,0:T(8,128)}) %reduce-scatter.32.cloned.1.call-update) | async-done | bytes 784
  1575.9 103.8 %reduce-scatter.28.cloned.1.call-done = f32[64,2048]{1,0:T(8,128)} async-done(((f32[1024,2048]{1,0:T(8,128)}), f32[64,2048]{1,0:T(8,128)}) %reduce-scatter.28.cloned.1.call-update) | async-done | bytes 524304 | tf_op jit(solution)/shard_map/reduce_scatter | solution.py:246
  1679.7 108.9 %reduce-scatter.30.cloned.1.call-done = f32[2048,64]{0,1:T(8,128)} async-done(((f32[2048,1024]{0,1:T(8,128)}), f32[2048,64]{0,1:T(8,128)}) %reduce-scatter.30.cloned.1.call-update) | async-done | bytes 524304 | tf_op jit(solution)/shard_map/reduce_scatter | solution.py:247
  1788.6 65.7 %reduce-scatter.26.cloned.1.call-done = f32[512,64]{0,1:T(8,128)} async-done(((f32[512,1024]{0,1:T(8,128)}), f32[512,64]{0,1:T(8,128)}) %reduce-scatter.26.cloned.1.call-update) | async-done | bytes 131088 | tf_op jit(solution)/shard_map/reduce_scatter | solution.py:245
  (234 shorter events, 213.4 us)
Async XLA Ops:
  7.2 36.4 %copy-start.1 = (bf16[320,4,1024]{2,1,0:T(4,128)(2,1)S(1)}, bf16[320,4,1024]{2,1,0:T(4,128)(2,1)}, u32[]{:S(2)}) copy-start(bf16[320,4,1024]{2,1,0:T(4,128)(2,1)} %param.19) | copy-start | bytes 7864324
  7.2 63.0 %all-gather.11.cloned.1.call-start = ((), (), s32[]{:S(2)}) async-start(), calls=%async_computation.11 | async-start | bytes 3342336 | tf_op jit(solution)/shard_map/all_gather | solution.py:101
  7.9 120.2 %all-gather.9.cloned.1.call-start = ((), (), s32[]{:S(2)}) async-start(), calls=%async_computation.10 | async-start | bytes 7864320 | tf_op jit(solution)/shard_map/all_gather | solution.py:136
  43.6 2.2 copy-start.10
  43.6 6.1 copy-start.28
  43.6 26.5 %copy-start.26 = (s32[4,640]{1,0:T(4,128)S(1)}, s32[4,640]{1,0:T(4,128)}, u32[]{:S(2)}) copy-start(s32[4,640]{1,0:T(4,128)} %param.20) | copy-start | bytes 30724
  48.9 164.7 %all-gather.13.cloned.1.call-start = ((), (), s32[]{:S(2)}) async-start(), calls=%async_computation.12 | async-start | bytes 1114112 | tf_op jit(solution)/shard_map/all_gather | solution.py:102
  49.6 294.9 %reduce-scatter.18.cloned.1.call-start = ((), (), s32[]{:S(2)}) async-start(), calls=%async_computation.13 | async-start | bytes 15728640 | tf_op jit(solution)/shard_map/reduce_scatter | solution.py:149
  73.5 67.5 %copy-start.9 = (bf16[1024,3,512]{0,2,1:T(8,128)(2,1)}, bf16[1024,3,512]{0,2,1:T(8,128)(2,1)S(1)}, u32[]{:S(2)}) copy-start(bf16[1024,3,512]{0,2,1:T(8,128)(2,1)S(1)} %copy.90) | copy-start | bytes 9437188
  208.6 13.9 copy-start.7
  222.5 122.0 %copy-start.2 = (bf16[320,4,1024]{2,1,0:T(4,128)(2,1)S(1)}, bf16[320,4,1024]{2,1,0:T(4,128)(2,1)}, u32[]{:S(2)}) copy-start(bf16[320,4,1024]{2,1,0:T(4,128)(2,1)} %param.19) | copy-start | bytes 7864324
  222.5 122.0 %copy-start.22 = (f32[1,2,512]{2,0,1:T(1,128)S(1)}, f32[1,2,512]{2,0,1:T(1,128)}, u32[]{:S(2)}) copy-start(f32[1,2,512]{2,0,1:T(1,128)} %get-tuple-element.219) | copy-start | bytes 12292
  222.5 174.6 %all-gather.17.cloned.1.call-start = ((), (), s32[]{:S(2)}) async-start(), calls=%async_computation.15 | async-start | bytes 4456448 | tf_op jit(solution)/shard_map/all_gather | solution.py:103
  223.1 242.5 %all-gather.15.cloned.1.call-start = ((), (), s32[]{:S(2)}) async-start(), calls=%async_computation.14 | async-start | bytes 7864320 | tf_op jit(solution)/shard_map/all_gather | solution.py:157
  348.6 2.4 copy-start
  348.6 2.4 copy-start.12
  348.6 2.3 copy-start.19
  353.1 188.5 %all-gather.21.cloned.1.call-start = ((), (), s32[]{:S(2)}) async-start(), calls=%async_computation.18 | async-start | bytes 7864320 | tf_op jit(solution)/shard_map/all_gather | solution.py:175
  353.2 8.2 copy-start.29
  360.6 228.0 %all-gather.19.cloned.1.call-start = ((), (), s32[]{:S(2)}) async-start(), calls=%async_computation.16 | async-start | bytes 4456448 | tf_op jit(solution)/shard_map/all_gather | solution.py:104
  361.4 393.3 %reduce-scatter.22.cloned.1.call-start = ((), (), s32[]{:S(2)}) async-start(), calls=%async_computation.19 | async-start | bytes 15728640 | tf_op jit(solution)/shard_map/reduce_scatter | solution.py:187
  634.2 244.5 %reduce-scatter.20.cloned.1.call-start = ((), (), s32[]{:S(2)}) async-start(), calls=%async_computation.17 | async-start | bytes 15728640 | tf_op jit(solution)/shard_map/reduce_scatter | solution.py:164
  651.8 311.6 %all-gather.23.cloned.1.call-start = ((), (), s32[]{:S(2)}) async-start(), calls=%async_computation.20 | async-start | bytes 7864320 | tf_op jit(solution)/shard_map/all_gather | solution.py:198
  754.7 6.0 copy-start.4
  760.7 118.1 %copy-start.21 = (f32[1,2,512]{2,0,1:T(1,128)S(1)}, f32[1,2,512]{2,0,1:T(1,128)}, u32[]{:S(2)}) copy-start(f32[1,2,512]{2,0,1:T(1,128)} %get-tuple-element.216) | copy-start | bytes 12292
  890.4 2.3 copy-start.6
  894.7 325.5 %reduce-scatter.24.cloned.1.call-start = ((), (), s32[]{:S(2)}) async-start(), calls=%async_computation.21 | async-start | bytes 15728640 | tf_op jit(solution)/shard_map/reduce_scatter | solution.py:222
  894.9 75.7 %copy-start.8 = (bf16[4,640,8,64]{1,3,2,0:T(8,128)(2,1)S(1)}, bf16[4,640,8,64]{1,3,2,0:T(8,128)(2,1)}, u32[]{:S(2)}) copy-start(bf16[4,640,8,64]{1,3,2,0:T(8,128)(2,1)} %copy-done.7) | copy-start | bytes 7864324
  1098.1 0.7 copy-start.27
  1098.2 187.2 %reduce-scatter.36.cloned.1.call-start = ((), (), s32[]{:S(2)}) async-start(), calls=%async_computation.27 | async-start | bytes 1114112
  1100.2 239.7 %reduce-scatter.34.cloned.1.call-start = ((), (), s32[]{:S(2)}) async-start(), calls=%async_computation.26 | async-start | bytes 278528
  1106.2 406.7 %all-reduce.4.cloned.1.call-start = ((), (), s32[]{:S(2)}) async-start(), calls=%async_computation.28 | async-start | bytes 16777216
  1129.2 0.7 copy-start.31
  1129.2 1.2 copy-start.25
  1129.2 1.2 copy-start.20
  1129.2 1.3 copy-start.23
  1129.2 1.3 copy-start.24
  1129.2 91.0 %copy-start.3 = (bf16[320,4,1024]{2,1,0:T(4,128)(2,1)S(1)}, bf16[320,4,1024]{2,1,0:T(4,128)(2,1)}, u32[]{:S(2)}) copy-start(bf16[320,4,1024]{2,1,0:T(4,128)(2,1)} %param.19) | copy-start | bytes 7864324
  1129.2 91.0 %copy-start.11 = (f32[320,4]{0,1:T(4,128)S(1)}, f32[320,4]{0,1:T(4,128)}, u32[]{:S(2)}) copy-start(f32[320,4]{0,1:T(4,128)} %copy-done.10) | copy-start | bytes 15364
  1129.2 91.0 %copy-start.14 = (f32[1,2,512]{2,0,1:T(1,128)S(1)}, f32[1,2,512]{2,0,1:T(1,128)}, u32[]{:S(2)}) copy-start(f32[1,2,512]{2,0,1:T(1,128)} %copy-done.13) | copy-start | bytes 12292
  1129.3 95.3 %copy-start.18 = (f32[320,4]{0,1:T(4,128)S(1)}, f32[320,4]{0,1:T(4,128)}, u32[]{:S(2)}) copy-start(f32[320,4]{0,1:T(4,128)} %copy-done.17) | copy-start | bytes 15364
  1129.3 95.4 %copy-start.16 = (f32[320,4]{0,1:T(4,128)S(1)}, f32[320,4]{0,1:T(4,128)}, u32[]{:S(2)}) copy-start(f32[320,4]{0,1:T(4,128)} %copy-done.15) | copy-start | bytes 15364
  1129.3 442.3 %reduce-scatter.32.cloned.1.call-start = ((), (), s32[]{:S(2)}) async-start(), calls=%async_computation.25 | async-start | bytes 278528
  1220.2 4.5 copy-start.5
  1241.1 438.6 %reduce-scatter.28.cloned.1.call-start = ((), (), s32[]{:S(2)}) async-start(), calls=%async_computation.23 | async-start | bytes 8912896 | tf_op jit(solution)/shard_map/reduce_scatter | solution.py:246
  1258.6 530.0 %reduce-scatter.30.cloned.1.call-start = ((), (), s32[]{:S(2)}) async-start(), calls=%async_computation.24 | async-start | bytes 8912896 | tf_op jit(solution)/shard_map/reduce_scatter | solution.py:247
  1276.1 7.9 copy-start.30
  1276.1 578.1 %reduce-scatter.26.cloned.1.call-start = ((), (), s32[]{:S(2)}) async-start(), calls=%async_computation.22 | async-start | bytes 2228224 | tf_op jit(solution)/shard_map/reduce_scatter | solution.py:245
  (3 other events, 1.9 us)
Sparse Core Ops, SparseCore 0:
  10.2 48.9 all-gather.10
  60.8 67.2 all-gather.8
  130.3 37.9 all-gather.12
  222.6 121.7 reduce-scatter.17
  346.5 50.5 all-gather.16
  398.5 67.0 all-gather.14
  467.1 68.5 all-gather.20
  537.9 50.7 all-gather.18
  634.3 120.3 reduce-scatter.21
  756.8 121.8 reduce-scatter.19
  894.8 68.5 all-gather.22
  1098.3 121.8 reduce-scatter.23
  1223.8 57.3 reduce-scatter.35
  1285.5 54.3 reduce-scatter.33
  1344.0 168.9 all-reduce.3
  1516.3 55.1 reduce-scatter.31
  1576.0 103.6 reduce-scatter.27
  1684.2 104.3 reduce-scatter.29
  1792.9 61.2 reduce-scatter.25
where the time goes:
time: 1870 us; the launch traced here: 1860 us
  waiting for transfers between devices  1210 us (65%)
  matrix products  306 us (16%)
  other arithmetic  160 us (9%)
  local copies, waits for them, and re-layouts  80.6 us (4%)
  blocking collectives  74.8 us (4%)
    unnamed x23, waiting for transfers between devices  265 us
    reduce_scatter x1, waiting for transfers between devices, on_device(): lax.psum_scatter(jnp.einsum('sbf,fd->sbd', row_block, down_full, preferre...  113 us
    reduce_scatter x1, waiting for transfers between devices, on_device(): lax.psum_scatter(down_weight_grad, 'dp', scatter_dimension=1, tiled=True)  109 us
    reduce_scatter x1, waiting for transfers between devices, on_device(): lax.psum_scatter(jnp.einsum('sbc,cd->sbd', row_block, out_full, preferred...  109 us
    reduce_scatter x1, waiting for transfers between devices, on_device(): lax.psum_scatter(up_weight_grad, 'dp', scatter_dimension=0, tiled=True)  104 us
    reduce_scatter x1, waiting for transfers between devices, on_device(): lax.psum_scatter(jnp.einsum('sbf,df->sbd', row_block, up_back, preferred_...  103 us
    reduce_scatter x1, waiting for transfers between devices, on_device(): lax.psum_scatter(jnp.einsum('sbc,dc->sbd', row_block, qkv_back, preferred...  89.7 us
    all_gather x1, waiting for transfers between devices, on_device(): normed_all_two = lax.all_gather(normed_two, 'tensor', axis=0, tiled=True)  68.5 us
  transfers between devices with their start and end apart: 19, of which 15 were waited for; matrix products, arithmetic and copies ran while one was open for 18% of the time, Pallas kernels for 0%

commit v1 on v0

--- a/solution.py
+++ b/solution.py
@@ -1,10 +1,17 @@
+import functools
+
 import jax
 import jax.numpy as jnp
 from jax import lax
+from jax.experimental import pallas as pl
+from jax.experimental.pallas import tpu as pltpu
 from jax.sharding import PartitionSpec as P
 
 HD = 64
-
+PAIR = 2 * HD
+VALID = 577
+F32 = jnp.float32
+BF16 = jnp.bfloat16
 
 epsilon = 1e-06
 masked_score = -1e30
@@ -268,6 +275,349 @@
     )
 
 
+BOTH = ("tensor", "dp")
+NT = (((1,), (1,)), ((), ()))
+NN = (((1,), (0,)), ((), ()))
+
+
+def dot_nn(a, b):
+    return lax.dot_general(a, b, NN, preferred_element_type=F32)
+
+
+def dot_nt(a, b):
+    return lax.dot_general(a, b, NT, preferred_element_type=F32)
+
+
+def attention_forward_kernel(lengths, q_ref, k_ref, v_ref, o_ref, lse_ref, *, key_rows):
+    length = lengths[pl.program_id(0)]
+    queries = q_ref[0] * jnp.asarray(HD**-0.5, BF16)
+    keys = k_ref[0, :key_rows]
+    values_t = jnp.transpose(v_ref[0, :key_rows].astype(F32)).astype(BF16)
+    lane = lax.broadcasted_iota(jnp.int32, (key_rows, PAIR), 1)
+    valid = lax.broadcasted_iota(jnp.int32, (key_rows, q_ref.shape[1]), 0) < length
+    outs = []
+    for head in range(2):
+        own = (lane >= head * HD) & (lane < (head + 1) * HD)
+        scores = dot_nt(jnp.where(own, keys, jnp.zeros_like(keys)), queries)
+        scores = jnp.where(valid, scores, masked_score)
+        top = jnp.max(scores, axis=0, keepdims=True)
+        exps = jnp.exp(scores - top)
+        total = jnp.sum(exps, axis=0, keepdims=True)
+        lse_ref[0, 0, head : head + 1, :] = top + jnp.log(total)
+        probs = (exps * (1.0 / total)).astype(BF16)
+        outs.append(dot_nn(values_t[head * HD : (head + 1) * HD], probs))
+    o_ref[0] = jnp.transpose(jnp.concatenate(outs, axis=0)).astype(BF16)
+
+
+def attention_backward_kernel(
+    lengths, q_ref, k_ref, v_ref, lse_ref, g_ref, dq_ref, dk_ref, dv_ref, *, key_rows
+):
+    length = lengths[pl.program_id(0)]
+    slots = q_ref.shape[1]
+    scale = HD**-0.5
+    plain = q_ref[0]
+    queries = plain * jnp.asarray(scale, BF16)
+    keys = k_ref[0, :key_rows]
+    values = v_ref[0, :key_rows]
+    grads = g_ref[0]
+    keys_t = jnp.transpose(keys.astype(F32)).astype(BF16)
+    lane = lax.broadcasted_iota(jnp.int32, (key_rows, PAIR), 1)
+    valid = lax.broadcasted_iota(jnp.int32, (key_rows, slots), 0) < length
+    zero = jnp.zeros_like(keys)
+    dqs, dks, dvs = [], [], []
+    for head in range(2):
+        own = (lane >= head * HD) & (lane < (head + 1) * HD)
+        scores = dot_nt(jnp.where(own, keys, zero), queries)
+        soft = jnp.where(valid, jnp.exp(scores - lse_ref[0, 0, head : head + 1, :]), 0.0)
+        prob_grad = dot_nt(jnp.where(own, values, zero), grads)
+        inner = jnp.sum(prob_grad * soft, axis=0, keepdims=True)
+        score_grad = (soft * (prob_grad - inner)).astype(BF16)
+        dvs.append(dot_nn(soft.astype(BF16), grads))
+        dks.append(dot_nn(score_grad, plain))
+        dqs.append(dot_nn(keys_t[head * HD : (head + 1) * HD], score_grad))
+    first = lane < HD
+    dq_ref[0] = (jnp.transpose(jnp.concatenate(dqs, axis=0)) * scale).astype(BF16)
+    dk_ref[0, :key_rows] = (jnp.where(first, dks[0], dks[1]) * scale).astype(BF16)
+    dv_ref[0, :key_rows] = jnp.where(first, dvs[0], dvs[1]).astype(BF16)
+    if key_rows < slots:
+        rest = jnp.zeros((slots - key_rows, PAIR), BF16)
+        dk_ref[0, key_rows:] = rest
+        dv_ref[0, key_rows:] = rest
+
+
+def key_count(slots):
+    return min(slots, -(-VALID // 16) * 16)
+
+
+def attention_forward(lengths, qkv):
+    images, slots, columns = qkv.shape
+    width = columns // 3
+    pairs = width // PAIR
+    part = lambda offset: pl.BlockSpec((1, slots, PAIR), lambda b, p, ln: (b, 0, offset + p))
+    return pl.pallas_call(
+        functools.partial(attention_forward_kernel, key_rows=key_count(slots)),
+        out_shape=(
+            jax.ShapeDtypeStruct((images, slots, width), BF16),
+            jax.ShapeDtypeStruct((images, pairs, 2, slots), F32),
+        ),
+        grid_spec=pltpu.PrefetchScalarGridSpec(
+            num_scalar_prefetch=1,
+            grid=(images, pairs),
+            in_specs=[part(0), part(pairs), part(2 * pairs)],
+            out_specs=(
+                part(0),
+                pl.BlockSpec((1, 1, 2, slots), lambda b, p, ln: (b, p, 0, 0)),
+            ),
+        ),
+        compiler_params=pltpu.CompilerParams(vmem_limit_bytes=48 << 20),
+        cost_estimate=pl.CostEstimate(
+            flops=images * pairs * 2 * 4 * slots * slots * PAIR,
+            bytes_accessed=images * slots * width * 8,
+            transcendentals=images * pairs * 2 * slots * slots,
+        ),
+        name="attention_forward",
+    )(lengths, qkv, qkv, qkv)
+
+
+def attention_backward(lengths, qkv, lse, grads):
+    images, slots, columns = qkv.shape
+    width = columns // 3
+    pairs = width // PAIR
+    part = lambda offset: pl.BlockSpec((1, slots, PAIR), lambda b, p, ln: (b, 0, offset + p))
+    piece = jax.ShapeDtypeStruct((images, slots, width), BF16)
+    return pl.pallas_call(
+        functools.partial(attention_backward_kernel, key_rows=key_count(slots)),
+        out_shape=(piece, piece, piece),
+        grid_spec=pltpu.PrefetchScalarGridSpec(
+            num_scalar_prefetch=1,
+            grid=(images, pairs),
+            in_specs=[
+                part(0),
+                part(pairs),
+                part(2 * pairs),
+                pl.BlockSpec((1, 1, 2, slots), lambda b, p, ln: (b, p, 0, 0)),
+                part(0),
+            ],
+            out_specs=(part(0), part(0), part(0)),
+        ),
+        compiler_params=pltpu.CompilerParams(vmem_limit_bytes=48 << 20),
+        cost_estimate=pl.CostEstimate(
+            flops=images * pairs * 2 * 10 * slots * slots * PAIR,
+            bytes_accessed=images * slots * width * 14,
+            transcendentals=images * pairs * 2 * slots * slots,
+        ),
+        name="attention_backward",
+    )(lengths, qkv, qkv, qkv, lse, grads)
+
+
+def to_images(rows):
+    count = lax.axis_size("tensor")
+    if count == 1:
+        return rows
+    if count > 2:
+        return lax.all_to_all(rows, "tensor", 0, 1, tiled=True)
+    me = lax.axis_index("tensor")
+    own, part = rows.shape[0] // 2, rows.shape[1]
+    kept = lax.dynamic_slice_in_dim(rows, me * own, own, 0)
+    sent = lax.dynamic_slice_in_dim(rows, (1 - me) * own, own, 0)
+    came = lax.ppermute(sent, "tensor", [(0, 1), (1, 0)])
+    whole = jnp.zeros((own, 2 * part) + rows.shape[2:], rows.dtype)
+    whole = lax.dynamic_update_slice_in_dim(whole, kept, me * part, 1)
+    return lax.dynamic_update_slice_in_dim(whole, came, (1 - me) * part, 1)
+
+
+def to_slots(rows):
+    count = lax.axis_size("tensor")
+    if count == 1:
+        return jnp.swapaxes(rows, 0, 1)
+    if count > 2:
+        return jnp.swapaxes(lax.all_to_all(rows, "tensor", 1, 0, tiled=True), 0, 1)
+    me = lax.axis_index("tensor")
+    own, part = rows.shape[0], rows.shape[1] // 2
+    kept = lax.dynamic_slice_in_dim(rows, me * part, part, 1)
+    sent = lax.dynamic_slice_in_dim(rows, (1 - me) * part, part, 1)
+    came = lax.ppermute(sent, "tensor", [(0, 1), (1, 0)])
+    first = jnp.where(me == 0, kept, came)
+    second = jnp.where(me == 0, came, kept)
+    return jnp.swapaxes(jnp.concatenate([first, second], axis=0), 0, 1)
+
+
+def normalize(values):
+    row_mean = jnp.mean(values, axis=-1, keepdims=True)
+    centred = values - row_mean
+    spread = jnp.mean(centred * centred, axis=-1, keepdims=True)
+    inverse = lax.rsqrt(spread + epsilon)
+    return centred * inverse, inverse
+
+
+def normalize_back(grad, unit, inverse, gain):
+    scaled = grad * gain
+    mean_one = jnp.mean(scaled, axis=-1, keepdims=True)
+    mean_two = jnp.mean(scaled * unit, axis=-1, keepdims=True)
+    return inverse * (scaled - mean_one - unit * mean_two)
+
+
+def gelu_pair(values):
+    area = 0.5 * (1.0 + lax.erf(values * (0.5**0.5)))
+    density = jnp.exp(-0.5 * values * values) * ((2.0 * jnp.pi) ** -0.5)
+    return (values * area).astype(BF16), area + values * density
+
+
+def token_sum(values):
+    return jnp.sum(values.astype(F32), axis=(0, 1))
+
+
+def by_images(
+    inputs,
+    pad_mask,
+    norm1_gain,
+    norm1_shift,
+    qkv_weight,
+    qv_bias,
+    out_weight,
+    out_bias,
+    norm2_gain,
+    norm2_shift,
+    up_weight,
+    up_bias,
+    down_weight,
+    down_bias,
+    cotangent,
+):
+    width = inputs.shape[2]
+    slots = pad_mask.shape[1]
+    tensors = lax.axis_size("tensor")
+    shards = lax.axis_size("dp") * tensors
+    me = lax.axis_index("tensor")
+    images = inputs.shape[1] // tensors
+    head_width = qkv_weight.shape[2]
+    hidden = up_weight.shape[1]
+    piece = norm1_gain.shape[1]
+    hidden_piece = up_bias.shape[1]
+
+    flat = jnp.concatenate(
+        [
+            v.reshape(-1)
+            for v in (norm1_gain, norm1_shift, out_bias, norm2_gain, norm2_shift, down_bias, qv_bias, up_bias)
+        ]
+    ).reshape(1, -1)
+    flat = lax.all_gather(flat, BOTH, axis=0, tiled=True).astype(F32)
+    gain_one, shift_one, out_shift, gain_two, shift_two, down_shift = [
+        flat[:, n * piece : (n + 1) * piece].reshape(width) for n in range(6)
+    ]
+    query_bias = flat[:, 6 * piece : 7 * piece].reshape(tensors, head_width)
+    value_bias = flat[:, 7 * piece : 8 * piece].reshape(tensors, head_width)
+    up_row = flat[:, 8 * piece :].reshape(tensors, hidden)
+
+    def gather(shard):
+        whole = lax.all_gather(shard, BOTH, axis=0, tiled=True)
+        return whole.reshape(tensors, -1, shard.shape[1])
+
+    qkv_full = gather(qkv_weight.reshape(qkv_weight.shape[0], -1))
+    out_full = gather(jnp.transpose(out_weight))
+    up_full = gather(up_weight)
+    down_full = gather(jnp.transpose(down_weight))
+
+    mask = lax.dynamic_slice_in_dim(pad_mask, me * images, images, 0)
+    lengths = jnp.sum(mask, axis=1).astype(jnp.int32)
+    kept = (mask > 0).astype(F32)[:, :, None]
+    x = to_images(jnp.swapaxes(inputs, 0, 1)).astype(F32)
+    cot = to_images(jnp.swapaxes(cotangent, 0, 1))
+
+    unit_one, inverse_one = normalize(x)
+    normed_one = (unit_one * gain_one + shift_one).astype(BF16)
+    parts = range(tensors)
+    product = functools.partial(jnp.einsum, preferred_element_type=F32)
+    qkvs, attendeds, lses = [], [], []
+    for t in parts:
+        bias = jnp.concatenate([query_bias[t], jnp.zeros((head_width,), F32), value_bias[t]])
+        qkvs.append((product("bsd,dc->bsc", normed_one, qkv_full[t]) + bias).astype(BF16))
+        attended, lse = attention_forward(lengths, qkvs[t])
+        attendeds.append(attended)
+        lses.append(lse)
+    projected = sum(product("bsc,dc->bsd", attendeds[t], out_full[t]) for t in parts)
+    after_attn = x + projected + out_shift
+    unit_two, inverse_two = normalize(after_attn)
+    normed_two = (unit_two * gain_two + shift_two).astype(BF16)
+    acts, slopes = [], []
+    for t in parts:
+        up_values = product("bsd,df->bsf", normed_two, up_full[t]) + up_row[t]
+        act, slope = gelu_pair(up_values)
+        acts.append(act)
+        slopes.append(slope)
+    out_grad = cot * kept
+    out_low = out_grad.astype(BF16)
+    down_shift_grad = token_sum(out_grad)
+
+    def scatter(grads):
+        stacked = jnp.concatenate(grads, axis=0).astype(BF16)
+        return lax.psum_scatter(stacked, BOTH, scatter_dimension=0, tiled=True).astype(F32)
+
+    down_owned = scatter([product("bsd,bsf->df", out_low, acts[t]) for t in parts])
+    up_grads = []
+    for t in parts:
+        act_grad = product("bsd,df->bsf", out_low, down_full[t])
+        up_grads.append((act_grad * slopes[t]).astype(BF16))
+    up_owned = scatter([product("bsd,bsf->df", normed_two, up_grads[t]) for t in parts])
+    normed_two_grad = sum(product("bsf,df->bsd", up_grads[t], up_full[t]) for t in parts)
+    mlp_out = sum(product("bsf,df->bsd", acts[t], down_full[t]) for t in parts)
+    block_output = to_slots((after_attn + mlp_out + down_shift) * kept)
+    up_shift_grad = jnp.stack([token_sum(up_grads[t]) for t in parts])
+    gain_two_grad = token_sum(normed_two_grad * unit_two)
+    shift_two_grad = token_sum(normed_two_grad)
+    after_attn_grad = out_grad + normalize_back(normed_two_grad, unit_two, inverse_two, gain_two)
+    out_shift_grad = token_sum(after_attn_grad)
+    proj_low = after_attn_grad.astype(BF16)
+    out_owned = scatter([product("bsd,bsc->dc", proj_low, attendeds[t]) for t in parts])
+    pieces, query_sums, value_sums = [], [], []
+    for t in parts:
+        attended_grad = product("bsd,dc->bsc", proj_low, out_full[t]).astype(BF16)
+        pieces.append(attention_backward(lengths, qkvs[t], lses[t], attended_grad))
+        query_sums.append(token_sum(pieces[t][0]))
+        value_sums.append(token_sum(pieces[t][2]))
+    qkv_owned = scatter(
+        [
+            jnp.concatenate([product("bsd,bsc->dc", normed_one, p) for p in pieces[t]], axis=1)
+            for t in parts
+        ]
+    )
+    normed_one_grad = sum(
+        product(
+            "bsc,dc->bsd",
+            pieces[t][n],
+            qkv_full[t][:, n * head_width : (n + 1) * head_width],
+        )
+        for t in parts
+        for n in range(3)
+    )
+    gain_one_grad = token_sum(normed_one_grad * unit_one)
+    shift_one_grad = token_sum(normed_one_grad)
+    input_grad = after_attn_grad + normalize_back(normed_one_grad, unit_one, inverse_one, gain_one)
+    input_grad = to_slots(input_grad)
+
+    vectors = [gain_one_grad, shift_one_grad, out_shift_grad, gain_two_grad, shift_two_grad, down_shift_grad]
+    vectors += [jnp.stack(query_sums), jnp.stack(value_sums), up_shift_grad]
+    small = jnp.concatenate([v.reshape(shards, -1) for v in vectors], axis=1)
+    small = lax.psum_scatter(small, BOTH, scatter_dimension=0, tiled=True)
+    row = lambda n: small[:, n * piece : (n + 1) * piece]
+    return (
+        block_output,
+        input_grad,
+        row(0),
+        row(1),
+        qkv_owned.reshape(qkv_weight.shape),
+        jnp.stack([row(6), row(7)], axis=0),
+        jnp.transpose(out_owned),
+        row(2),
+        row(3),
+        row(4),
+        up_owned,
+        small[:, 8 * piece : 8 * piece + hidden_piece],
+        jnp.transpose(down_owned),
+        row(5),
+    )
+
+
 def solution(mesh):
     in_specs = (
         P("tensor", "dp", None),
@@ -302,6 +652,12 @@
         P("tensor", "dp"),
         P("tensor", "dp"),
     )
+    dims = dict(zip(mesh.axis_names, mesh.devices.shape))
+
+    def choose(inputs, *rest):
+        whole_images = inputs.shape[1] % dims["tensor"] == 0
+        return (by_images if whole_images else on_device)(inputs, *rest)
+
     return jax.shard_map(
-        on_device, mesh=mesh, in_specs=in_specs, out_specs=out_specs, check_vma=False
-    )
+        choose, mesh=mesh, in_specs=in_specs, out_specs=out_specs, check_vma=False
+    )

time: 1870 us -> 945 us (0.51)
  waiting for transfers between devices: 1210 us -> 270 us
  blocking collectives: 74.8 us -> 198 us
  matrix products: 306 us -> 212 us
  Pallas kernels: 0 us -> 82 us
  other arithmetic: 160 us -> 91.4 us
    reduce_scatter x7 -> x3, waiting for transfers between devices: 693 us -> 116 us  [scatter(): lax.psum_scatter(stacked, BOTH, scatter_dimension=0, tiled=True).astype(F32)]
    unnamed x23 -> x9, waiting for transfers between devices: 265 us -> 1.98 us
    unnamed x1, blocking collectives: 7.26 us -> 154 us
    all_gather x8 -> x4, waiting for transfers between devices: 253 us -> 108 us  [gather(): whole = lax.all_gather(shard, BOTH, axis=0, tiled=True)]
    dot_general x40 -> x32, matrix products: 306 us -> 212 us  [the longest x6 39.7 us: by_images(): product('bsc,dc->bsd', pieces[t][n], qkv_full[t][:, n * head_width:(n + 1...]
    convert_element_type x12 -> x5, other arithmetic: 90.9 us -> 6.16 us  [the longest x1 2.07 us: by_images(): normed_two = (unit_two * gain_two + shift_two).astype(BF16)]
    pallas_call x0 -> x4, Pallas kernels: none -> 82 us  [the longest x2 50.3 us: attention_backward(): pl.pallas_call(functools.partial(attention_backward_kernel, key_rows=key_...]
    concatenate x1 -> x5, other arithmetic: 0.01 us -> 59.9 us  [the longest x4 59.8 us: scatter(): stacked = jnp.concatenate(grads, axis=0).astype(BF16)]
  transfers between devices with their start and end apart: 19 -> 12, of which waited for: 15 -> 4; matrix products, arithmetic and copies ran while one was open for 18% -> 31% of each run, Pallas kernels for 0% -> 9%
where the time goes in v1:
time: 945 us; the launch traced here: 938 us
  waiting for transfers between devices  270 us (29%)
  matrix products  212 us (22%)
  blocking collectives  198 us (21%)
  other arithmetic  91.4 us (10%)
  Pallas kernels  82 us (9%)
  local copies, waits for them, and re-layouts  63.8 us (7%)
  between operations  15.3 us (2%)
    unnamed x1, blocking collectives  154 us
    reduce_scatter x3, waiting for transfers between devices, scatter(): lax.psum_scatter(stacked, BOTH, scatter_dimension=0, tiled=True).astype(F32)  116 us
    all_gather x4, waiting for transfers between devices, gather(): whole = lax.all_gather(shard, BOTH, axis=0, tiled=True)  108 us
    concatenate x4, other arithmetic, scatter(): stacked = jnp.concatenate(grads, axis=0).astype(BF16)  59.8 us
    pallas_call x2, Pallas kernels, attention_backward(): pl.pallas_call(functools.partial(attention_backward_kernel, key_rows=key_...  50.3 us
    ppermute x2, waiting for transfers between devices, to_images(): came = lax.ppermute(sent, 'tensor', [(0, 1), (1, 0)])  43.9 us
    all_gather x1, blocking collectives, by_images(): flat = lax.all_gather(flat, BOTH, axis=0, tiled=True).astype(F32)  43.8 us
    unnamed x138, local copies, waits for them, and re-layouts  39.7 us
  transfers between devices with their start and end apart: 12, of which 4 were waited for; matrix products, arithmetic and copies ran while one was open for 31% of the time, Pallas kernels for 9%

profile of v1, /device:TPU:0, one launch (start us, length us, event | category | flops | bytes accessed | tf_op | source)
XLA Modules:
  0.0 938.0 jit_solution(9489898820729288587)
XLA Ops:
  11.0 5.4 constant_dynamic-slice_fusion.4
  17.8 3.0 collective-permute-start
  20.8 4.2 constant_dynamic-slice_fusion.1
  27.6 43.8 %all-gather.1 = bf16[32,1,384]{2,1,0:T(2,128)(2,1)S(1)} all-gather(bf16[1,1,384]{2,1,0:T(2,128)(2,1)S(1)} %reshape.202), channel_id=2, replica_groups=mesh['dp'=16,'tensor'=2] {'tensor','dp'}, dimensions={0}, use_global_device_ids=true | all-gather | bytes 25344 | tf_op jit(solution)/shard_map/all_gather | solution.py:504
  78.3 43.9 %collective-permute-done.2 = f32[2,320,1024]{2,1,0:T(8,128)} collective-permute-done((f32[2,320,1024]{2,1,0:T(8,128)}, f32[2,320,1024]{2,1,0:T(8,128)}, u32[]{:S(2)}, u32[]{:S(2)}) %collective-permute-start.2) | collective-permute-done | bytes 2621472 | tf_op jit(solution)/shard_map/ppermute | solution.py:423
  124.3 2.4 copy-done.16
  128.5 7.2 add_convert_fusion.q_ref.k_ref.v_ref
  135.7 15.9 %attention_forward.3 = (bf16[2,640,512]{2,1,0:T(8,128)(2,1)S(1)}, f32[2,4,2,640]{3,2,1,0:T(2,128)S(1)}) custom-call(s32[2]{0:T(128)S(1)} %dynamic-slice_reduce_fusion.lengths, bf16[2,640,1536]{2,1,0:T(8,128)(2,1)S(1)} %add_convert_fusion.q_ref.k_ref.v_ref, bf16[2,640,1536]{2,1,0:T(8,128)(2,1)S(1)} %add_convert_fusion.q_ref.k_ref.v_ref, ...), custom_call_target="tpu_custom_call" | custom-call | flops 3355443200 | bytes 5242880 | tf_op jit(solution)/shard_map/attention_forward/pallas_call | solution.py:357
  151.7 4.7 add_convert_fusion.1.q_ref.k_ref.v_ref
  156.4 15.8 %attention_forward.2 = (bf16[2,640,512]{2,1,0:T(8,128)(2,1)S(1)}, f32[2,4,2,640]{3,2,1,0:T(2,128)S(1)}) custom-call(s32[2]{0:T(128)S(1)} %dynamic-slice_reduce_fusion.lengths, bf16[2,640,1536]{2,1,0:T(8,128)(2,1)S(1)} %add_convert_fusion.1.q_ref.k_ref.v_ref, bf16[2,640,1536]{2,1,0:T(8,128)(2,1)S(1)} %add_convert_fusion.1.q_ref.k_ref.v_ref, ...), custom_call_target="tpu_custom_call" | custom-call | flops 3355443200 | bytes 5242880 | tf_op jit(solution)/shard_map/attention_forward/pallas_call | solution.py:357
  174.1 2.9 fusion.41
  183.3 51.3 %all-gather.11.cloned.1.call-done = bf16[2048,2048]{1,0:T(8,128)(2,1)} async-done(((bf16[64,2048]{1,0:T(8,128)(2,1)}), bf16[2048,2048]{1,0:T(8,128)(2,1)}) %all-gather.11.cloned.1.call-update) | async-done | bytes 8388624 | tf_op jit(solution)/shard_map/all_gather | solution.py:513
  234.7 12.6 %multiply_convert_fusion = (bf16[2,640,2048]{2,1,0:T(8,128)(2,1)}, f32[2,640,2048]{2,1,0:T(8,128)}) fusion(f32[2048]{0:T(1024)S(1)} %get-tuple-element.103, bf16[2,640,1024]{2,1,0:T(8,128)(2,1)} %add_convert_fusion.2, bf16[2048,2048]{1,0:T(8,128)(2,1)} %all-gather.11.cloned.1.call-done), kind=kOutput, calls=%fused_computation.16 | convolution fusion | flops 5384437760 | bytes 22552576 | tf_op jit(solution)/shard_map/bsd,df->bsf/dot_general | solution.py:544
  247.3 9.6 %multiply_convert_fusion.1 = (bf16[2,640,2048]{2,1,0:T(8,128)(2,1)}, f32[2,640,2048]{2,1,0:T(8,128)}) fusion(f32[2048]{0:T(1024)S(1)} %get-tuple-element.104, bf16[2,640,1024]{2,1,0:T(8,128)(2,1)S(1)} %copy-done.22, bf16[2048,2048]{1,0:T(8,128)(2,1)S(1)} %copy-done.48), kind=kOutput, calls=%fused_computation.18 | convolution fusion | flops 5384437760 | bytes 22552576 | tf_op jit(solution)/shard_map/bsd,df->bsf/dot_general | solution.py:544
  256.9 56.6 %all-gather.13.cloned.1.call-done = bf16[2048,2048]{1,0:T(8,128)(2,1)} async-done(((bf16[64,2048]{1,0:T(8,128)(2,1)}), bf16[2048,2048]{1,0:T(8,128)(2,1)}) %all-gather.13.cloned.1.call-update) | async-done | bytes 8388624 | tf_op jit(solution)/shard_map/all_gather | solution.py:513
  313.5 13.5 %convert_reduce_fusion = (f32[2048]{0:T(1024)}, bf16[2,640,2048]{2,1,0:T(8,128)(2,1)S(1)}) fusion(f32[2,640,2048]{2,1,0:T(8,128)} %get-tuple-element.122, f32[2048]{0:T(1024)S(1)} %get-tuple-element.103, bf16[2,640,1024]{2,1,0:T(8,128)(2,1)} %multiply_convert_fusion.2, bf16[2048,2048]{1,0:T(8,128)(2,1)} %all-gather.13.cloned.1.call-done), kind=kOutput, calls=%fused_computation.14 | convolution fusion | flops 5402785792 | bytes 22560768 | tf_op jit(solution)/shard_map/bsd,df->bsf/dot_general | solution.py:559
  327.0 16.4 %convert_reduce_fusion.1 = (f32[2048]{0:T(1024)}, bf16[2,640,2048]{2,1,0:T(8,128)(2,1)}) fusion(f32[2,640,2048]{2,1,0:T(8,128)} %get-tuple-element.120, f32[2048]{0:T(1024)S(1)} %get-tuple-element.104, bf16[2,640,1024]{2,1,0:T(8,128)(2,1)S(1)} %copy-done.24, bf16[2048,2048]{1,0:T(8,128)(2,1)} %all-gather.13.cloned.1.call-done), kind=kOutput, calls=%fused_computation.15 | convolution fusion | flops 5402785792 | bytes 22560768 | tf_op jit(solution)/shard_map/bsd,df->bsf/dot_general | solution.py:559
  343.3 10.6 %fusion.27 = f32[2,640,1024]{2,1,0:T(8,128)} fusion(bf16[2,640,2048]{2,1,0:T(8,128)(2,1)} %get-tuple-element.128, bf16[2048,2048]{1,0:T(8,128)(2,1)} %all-gather.11.cloned.1.call-done), kind=kOutput, calls=%fused_computation.65 | convolution fusion | flops 5368709120 | bytes 14680064 | tf_op jit(solution)/shard_map/bsf,df->bsd/dot_general | solution.py:562
  354.0 12.6 %multiply_reduce_fusion = (f32[1024]{0:T(1024)}, f32[2,640]{1,0:T(2,128)S(1)}, f32[2,640]{1,0:T(2,128)S(1)}, f32[1024]{0:T(1024)}, f32[2,640,1024]{2,1,0:T(8,128)}) fusion(f32[2,640,1024]{2,1,0:T(8,128)S(1)} %bitcast.183, f32[2,640]{1,0:T(2,128)S(1)} %add_rsqrt_fusion, f32[2,640]{1,0:T(2,128)S(1)} %broadcast_multiply_fusion.4, f32[1024]{0:T(1024)S(1)} %mul.190, ...), kind=kOutput, calls=%fused_computation.49 | convolution fusion | flops 5381812224 | bytes 25198592 | tf_op jit(solution)/shard_map/bsf,df->bsd/dot_general | solution.py:562
  366.6 5.2 fusion.52
  377.4 3.5 convolution_convert_fusion.1.g_ref
  380.9 25.3 %attention_backward.2 = (bf16[2,640,512]{2,1,0:T(8,128)(2,1)S(1)}, bf16[2,640,512]{2,1,0:T(8,128)(2,1)S(1)}, bf16[2,640,512]{2,1,0:T(8,128)(2,1)S(1)}) custom-call(s32[2]{0:T(128)S(1)} %dynamic-slice_reduce_fusion.lengths, bf16[2,640,1536]{2,1,0:T(8,128)(2,1)} %copy-done.8, bf16[2,640,1536]{2,1,0:T(8,128)(2,1)} %copy-done.8, ...), custom_call_target="tpu_custom_call" | custom-call | flops 8388608000 | bytes 9175040 | tf_op jit(solution)/shard_map/attention_backward/pallas_call | solution.py:388
  408.1 2.8 bitcast_convert_fusion.11
  414.2 25.0 %attention_backward.3 = (bf16[2,640,512]{2,1,0:T(8,128)(2,1)S(1)}, bf16[2,640,512]{2,1,0:T(8,128)(2,1)S(1)}, bf16[2,640,512]{2,1,0:T(8,128)(2,1)S(1)}) custom-call(s32[2]{0:T(128)S(1)} %dynamic-slice_reduce_fusion.lengths, bf16[2,640,1536]{2,1,0:T(8,128)(2,1)} %copy-done.7, bf16[2,640,1536]{2,1,0:T(8,128)(2,1)} %copy-done.7, ...), custom_call_target="tpu_custom_call" | custom-call | flops 8388608000 | bytes 9175040 | tf_op jit(solution)/shard_map/attention_backward/pallas_call | solution.py:388
  444.8 41.3 %maximum_maximum_fusion = bf16[2048,1536]{0,1:T(8,128)(2,1)} fusion(bf16[1024,512]{0,1:T(8,128)(2,1)S(1)} %bitcast_convert_fusion.6, bf16[1024,512]{0,1:T(8,128)(2,1)S(1)} %bitcast_convert_fusion.7, bf16[1024,512]{0,1:T(8,128)(2,1)S(1)} %bitcast_convert_fusion.8, bf16[1024,512]{0,1:T(8,128)(2,1)S(1)} %bitcast_convert_fusion.9, ...), kind=kLoop, calls=%fused_computation.31 | loop fusion | flops 37748736 | bytes 12582912 | tf_op jit(solution)/shard_map/concatenate | solution.py:553
  486.1 8.7 copy.101
  494.8 10.3 %bitcast_convert_fusion.2 = bf16[1024,2048]{1,0:T(8,128)(2,1)} fusion(bf16[2,640,1024]{2,1,0:T(8,128)(2,1)} %add_convert_fusion.2, bf16[2,640,2048]{2,1,0:T(8,128)(2,1)} %copy-done.51), kind=kOutput, calls=%fused_computation.24 | convolution fusion | flops 5370806272 | bytes 12058624 | tf_op jit(solution)/shard_map/bsd,bsf->df/dot_general | solution.py:561
  505.2 9.7 %bitcast_convert_fusion.3 = bf16[1024,2048]{1,0:T(8,128)(2,1)} fusion(bf16[2,640,1024]{2,1,0:T(8,128)(2,1)S(1)} %copy-done.23, bf16[2,640,2048]{2,1,0:T(8,128)(2,1)} %get-tuple-element.128), kind=kOutput, calls=%fused_computation.25 | convolution fusion | flops 5370806272 | bytes 12058624 | tf_op jit(solution)/shard_map/bsd,bsf->df/dot_general | solution.py:561
  514.9 8.4 pad_maximum_fusion
  523.4 10.4 %bitcast_convert_fusion = bf16[1024,2048]{1,0:T(8,128)(2,1)} fusion(bf16[2,640,1024]{2,1,0:T(8,128)(2,1)} %multiply_convert_fusion.2, bf16[2,640,2048]{2,1,0:T(8,128)(2,1)} %get-tuple-element.121), kind=kOutput, calls=%fused_computation.22 | convolution fusion | flops 5370806272 | bytes 12058624 | tf_op jit(solution)/shard_map/bsd,bsf->df/dot_general | solution.py:556
  533.9 10.3 %bitcast_convert_fusion.1 = bf16[1024,2048]{1,0:T(8,128)(2,1)} fusion(bf16[2,640,1024]{2,1,0:T(8,128)(2,1)S(1)} %copy-done.25, bf16[2,640,2048]{2,1,0:T(8,128)(2,1)} %get-tuple-element.119), kind=kOutput, calls=%fused_computation.23 | convolution fusion | flops 5370806272 | bytes 12058624 | tf_op jit(solution)/shard_map/bsd,bsf->df/dot_general | solution.py:556
  544.2 8.7 pad_maximum_fusion.1
  553.7 5.5 fusion.39
  559.2 5.2 fusion.40
  564.4 5.5 fusion.38
  569.9 5.3 fusion.37
  575.2 5.4 fusion.36
  580.6 12.8 %fusion.24 = (f32[1024]{0:T(1024)S(1)}, f32[2,640]{1,0:T(2,128)S(1)}, f32[2,640]{1,0:T(2,128)S(1)}, f32[1024]{0:T(1024)S(1)}, f32[2,640,1024]{2,1,0:T(8,128)}) fusion(bf16[2,640,1024]{2,1,0:T(8,128)(2,1)S(1)} %copy-done.13, f32[2,640]{1,0:T(2,128)S(1)} %add_rsqrt_fusion.1, f32[2,640]{1,0:T(2,128)S(1)} %broadcast_multiply_fusion.5, f32[1024]{0:T(1024)S(1)} %mul.184, ...), kind=kOutput, calls=%fused_computation.44 | convolution fusion | flops 1361833472 | bytes 36470784 | tf_op jit(solution)/shard_map/bsc,dc->bsd/dot_general | solution.py:585
  593.4 3.8 fusion.23
  602.2 11.3 %fusion.29 = f32[2,640,1024]{2,1,0:T(8,128)} fusion(bf16[2,640,2048]{2,1,0:T(8,128)(2,1)} %get-tuple-element.119, bf16[2048,2048]{1,0:T(8,128)(2,1)} %all-gather.13.cloned.1.call-done), kind=kOutput, calls=%fused_computation.67 | convolution fusion | flops 5368709120 | bytes 14680064 | tf_op jit(solution)/shard_map/bsf,df->bsd/dot_general | solution.py:563
  613.6 8.6 add_multiply_fusion.2
  622.2 2.3 copy-done.21
  632.3 154.3 %all-reduce = f32[32,384]{1,0:T(8,128)S(1)} all-reduce(f32[32,384]{1,0:T(8,128)S(1)} %concatenate.47), channel_id=3, replica_groups=mesh['dp'=16,'tensor'=2] {'tensor','dp'}, use_global_device_ids=true, to_apply=%region_21.22.clone | all-reduce | flops 12288 | bytes 98304
  789.7 3.2 dynamic-slice_select_fusion.1
  793.5 5.7 copy.87
  799.3 2.3 dynamic-slice_select_fusion.3
  802.3 5.7 copy.86
  813.3 115.9 %reduce-scatter.11.cloned.1.call-done = bf16[64,2048]{1,0:T(8,128)(2,1)} async-done(((bf16[2048,2048]{1,0:T(8,128)(2,1)}), bf16[64,2048]{1,0:T(8,128)(2,1)}) %reduce-scatter.11.cloned.1.call-update) | async-done | bytes 262160 | tf_op jit(solution)/shard_map/reduce_scatter | solution.py:554
  (242 shorter events, 67.9 us)
Async XLA Ops:
  7.2 121.4 %all-gather.7.cloned.1.call-start = ((), (), s32[]{:S(2)}) async-start(), calls=%async_computation.4 | async-start | bytes 6488064 | tf_op jit(solution)/shard_map/all_gather | solution.py:513
  8.9 165.2 %all-gather.9.cloned.1.call-start = ((), (), s32[]{:S(2)}) async-start(), calls=%async_computation.5 | async-start | bytes 2162688 | tf_op jit(solution)/shard_map/all_gather | solution.py:513
  9.6 225.1 %all-gather.11.cloned.1.call-start = ((), (), s32[]{:S(2)}) async-start(), calls=%async_computation.6 | async-start | bytes 8650752 | tf_op jit(solution)/shard_map/all_gather | solution.py:513
  10.4 303.1 %all-gather.13.cloned.1.call-start = ((), (), s32[]{:S(2)}) async-start(), calls=%async_computation.7 | async-start | bytes 8650752 | tf_op jit(solution)/shard_map/all_gather | solution.py:513
  10.9 797.1 %reduce-scatter.7.cloned.1.call-start = ((), (), s32[]{:S(2)}) async-start(), calls=%async_computation.8 | async-start | bytes 2162688 | tf_op jit(solution)/shard_map/reduce_scatter | solution.py:554
  11.0 9.8 %copy-start.20 = (f32[320,4,1024]{2,1,0:T(4,128)S(1)}, f32[320,4,1024]{2,1,0:T(4,128)}, u32[]{:S(2)}) copy-start(f32[320,4,1024]{2,1,0:T(4,128)} %param.29) | copy-start | bytes 15728644
  17.8 58.1 %collective-permute-start = (bf16[2,320,1024]{2,1,0:T(8,128)(2,1)}, bf16[2,320,1024]{2,1,0:T(8,128)(2,1)S(1)}, u32[]{:S(2)}, u32[]{:S(2)}) collective-permute-start(bf16[2,320,1024]{2,1,0:T(8,128)(2,1)} %bitcast.180), channel_id=1, source_target_pairs={{0,1},{1,0},{2,3},{3,2},{4,5},{5,4},{6,7},{7,6},{8,9},{9,8},{10,11... | collective-permute-start | bytes 3932168 | tf_op jit(solution)/shard_map/ppermute | solution.py:423
  25.0 47.8 %copy-start.36 = (s32[4,640]{1,0:T(4,128)S(1)}, s32[4,640]{1,0:T(4,128)}, u32[]{:S(2)}) copy-start(s32[4,640]{1,0:T(4,128)} %param.16) | copy-start | bytes 30724
  27.3 94.9 %collective-permute-start.2 = (f32[2,320,1024]{2,1,0:T(8,128)}, f32[2,320,1024]{2,1,0:T(8,128)}, u32[]{:S(2)}, u32[]{:S(2)}) collective-permute-start(f32[2,320,1024]{2,1,0:T(8,128)} %bitcast.179), channel_id=1, source_target_pairs={{0,1},{1,0},{2,3},{3,2},{4,5},{5,4},{6,7},{7,6},{8,9},{9,8},{10,11... | collective-permute-start | bytes 7864328 | tf_op jit(solution)/shard_map/ppermute | solution.py:423
  73.0 293.6 %copy-start.32 = (f32[2,640]{1,0:T(2,128)}, f32[2,640]{1,0:T(2,128)S(1)}, u32[]{:S(2)}) copy-start(f32[2,640]{1,0:T(2,128)S(1)} %compare_convert_fusion) | copy-start | bytes 15364
  135.7 16.0 %copy-start.7 = (bf16[2,640,1536]{2,1,0:T(8,128)(2,1)}, bf16[2,640,1536]{2,1,0:T(8,128)(2,1)S(1)}, u32[]{:S(2)}) copy-start(bf16[2,640,1536]{2,1,0:T(8,128)(2,1)S(1)} %add_convert_fusion.q_ref.k_ref.v_ref) | copy-start | bytes 11796484
  135.7 16.0 %copy-start.10 = (bf16[2,640,1024]{2,1,0:T(8,128)(2,1)S(1)}, bf16[2,640,1024]{2,1,0:T(8,128)(2,1)}, u32[]{:S(2)}) copy-start(bf16[2,640,1024]{2,1,0:T(8,128)(2,1)} %copy-done.9) | copy-start | bytes 7864324
  135.7 16.0 %copy-start.19 = (bf16[2048,1536]{1,0:T(8,128)(2,1)S(1)}, bf16[2048,1536]{1,0:T(8,128)(2,1)}, u32[]{:S(2)}) copy-start(bf16[2048,1536]{1,0:T(8,128)(2,1)} %all-gather.7.cloned.1.call-done) | copy-start | bytes 18874372
  234.7 12.6 %copy-start.22 = (bf16[2,640,1024]{2,1,0:T(8,128)(2,1)S(1)}, bf16[2,640,1024]{2,1,0:T(8,128)(2,1)}, u32[]{:S(2)}) copy-start(bf16[2,640,1024]{2,1,0:T(8,128)(2,1)} %add_convert_fusion.2) | copy-start | bytes 7864324
  234.7 12.6 %copy-start.48 = (bf16[2048,2048]{1,0:T(8,128)(2,1)S(1)}, bf16[2048,2048]{1,0:T(8,128)(2,1)}, u32[]{:S(2)}) copy-start(bf16[2048,2048]{1,0:T(8,128)(2,1)} %all-gather.11.cloned.1.call-done) | copy-start | bytes 25165828
  313.5 13.5 %copy-start.24 = (bf16[2,640,1024]{2,1,0:T(8,128)(2,1)S(1)}, bf16[2,640,1024]{2,1,0:T(8,128)(2,1)}, u32[]{:S(2)}) copy-start(bf16[2,640,1024]{2,1,0:T(8,128)(2,1)} %multiply_convert_fusion.2) | copy-start | bytes 7864324
  313.5 40.5 %slice-start = ((s8[5242880]{0:T(1024)(128)(4,1)}), s8[4194304]{0:T(1024)(128)(4,1)S(1)}, s32[]{:S(2)}) async-start(s8[5242880]{0:T(1024)(128)(4,1)} %bitcast.182), calls=%async_computation.12 | async-start | bytes 8388608
  327.0 27.0 %copy-start.51 = (bf16[2,640,2048]{2,1,0:T(8,128)(2,1)}, bf16[2,640,2048]{2,1,0:T(8,128)(2,1)S(1)}, u32[]{:S(2)}) copy-start(bf16[2,640,2048]{2,1,0:T(8,128)(2,1)S(1)} %get-tuple-element.126) | copy-start | bytes 15728644
  327.0 27.0 %slice-start.1 = ((s8[5242880]{0:T(1024)(128)(4,1)}), s8[1048576]{0:T(1024)(128)(4,1)S(1)}, s32[]{:S(2)}) async-start(s8[5242880]{0:T(1024)(128)(4,1)} %bitcast.182), calls=%async_computation.13 | async-start | bytes 2097152
  327.0 39.6 %slice-start.6 = ((s8[5242880]{0:T(1024)(128)(4,1)}), s8[4194304]{0:T(1024)(128)(4,1)S(1)}, s32[]{:S(2)}) async-start(s8[5242880]{0:T(1024)(128)(4,1)} %bitcast.188), calls=%async_computation.18 | async-start | bytes 8388608
  343.3 23.3 %slice-start.7 = ((s8[5242880]{0:T(1024)(128)(4,1)}), s8[1048576]{0:T(1024)(128)(4,1)S(1)}, s32[]{:S(2)}) async-start(s8[5242880]{0:T(1024)(128)(4,1)} %bitcast.188), calls=%async_computation.19 | async-start | bytes 2097152
  377.3 432.2 %reduce-scatter.13.cloned.1.call-start = ((), (), s32[]{:S(2)}) async-start(), calls=%async_computation.11 | async-start | bytes 6488064
  380.9 25.3 %copy-start.12 = (bf16[2,640,1024]{2,1,0:T(8,128)(2,1)S(1)}, bf16[2,640,1024]{2,1,0:T(8,128)(2,1)}, u32[]{:S(2)}) copy-start(bf16[2,640,1024]{2,1,0:T(8,128)(2,1)} %copy-done.9) | copy-start | bytes 7864324
  406.2 6.2 copy-start
  494.8 316.8 %reduce-scatter.9.cloned.1.call-start = ((), (), s32[]{:S(2)}) async-start(), calls=%async_computation.9 | async-start | bytes 8650752 | tf_op jit(solution)/shard_map/reduce_scatter | solution.py:554
  494.8 10.3 %copy-start.23 = (bf16[2,640,1024]{2,1,0:T(8,128)(2,1)S(1)}, bf16[2,640,1024]{2,1,0:T(8,128)(2,1)}, u32[]{:S(2)}) copy-start(bf16[2,640,1024]{2,1,0:T(8,128)(2,1)} %add_convert_fusion.2) | copy-start | bytes 7864324
  523.4 405.9 %reduce-scatter.11.cloned.1.call-start = ((), (), s32[]{:S(2)}) async-start(), calls=%async_computation.10 | async-start | bytes 8650752 | tf_op jit(solution)/shard_map/reduce_scatter | solution.py:554
  523.4 10.5 %copy-start.25 = (bf16[2,640,1024]{2,1,0:T(8,128)(2,1)S(1)}, bf16[2,640,1024]{2,1,0:T(8,128)(2,1)}, u32[]{:S(2)}) copy-start(bf16[2,640,1024]{2,1,0:T(8,128)(2,1)} %multiply_convert_fusion.2) | copy-start | bytes 7864324
  564.4 5.5 copy-start.3
  569.9 5.3 copy-start.6
  575.2 5.4 copy-start.13
  575.2 18.2 %slice-start.4 = ((s8[5242880]{0:T(1024)(128)(4,1)}), s8[4194304]{0:T(1024)(128)(4,1)S(1)}, s32[]{:S(2)}) async-start(s8[5242880]{0:T(1024)(128)(4,1)} %bitcast.186), calls=%async_computation.16 | async-start | bytes 8388608
  580.6 12.8 %slice-start.5 = ((s8[5242880]{0:T(1024)(128)(4,1)}), s8[1048576]{0:T(1024)(128)(4,1)S(1)}, s32[]{:S(2)}) async-start(s8[5242880]{0:T(1024)(128)(4,1)} %bitcast.186), calls=%async_computation.17 | async-start | bytes 2097152
  599.5 14.1 %slice-start.2 = ((s8[5242880]{0:T(1024)(128)(4,1)}), s8[4194304]{0:T(1024)(128)(4,1)S(1)}, s32[]{:S(2)}) async-start(s8[5242880]{0:T(1024)(128)(4,1)} %bitcast.184), calls=%async_computation.14 | async-start | bytes 8388608
  599.5 14.1 %slice-start.10 = ((s8[8388608]{0:T(1024)(128)(4,1)}), s8[4194304]{0:T(1024)(128)(4,1)S(1)}, s32[]{:S(2)}) async-start(s8[8388608]{0:T(1024)(128)(4,1)} %bitcast.213), calls=%async_computation.22 | async-start | bytes 8388608
  601.2 12.4 %slice-start.3 = ((s8[5242880]{0:T(1024)(128)(4,1)}), s8[1048576]{0:T(1024)(128)(4,1)S(1)}, s32[]{:S(2)}) async-start(s8[5242880]{0:T(1024)(128)(4,1)} %bitcast.184), calls=%async_computation.15 | async-start | bytes 2097152
  601.2 12.4 %copy-start.33 = (f32[2,640]{1,0:T(2,128)S(1)}, f32[2,640]{1,0:T(2,128)}, u32[]{:S(2)}) copy-start(f32[2,640]{1,0:T(2,128)} %copy-done.32) | copy-start | bytes 15364
  601.2 12.4 %slice-start.11 = ((s8[8388608]{0:T(1024)(128)(4,1)}), s8[4194304]{0:T(1024)(128)(4,1)S(1)}, s32[]{:S(2)}) async-start(s8[8388608]{0:T(1024)(128)(4,1)} %bitcast.213), calls=%async_computation.23 | async-start | bytes 8388608
  601.2 188.5 %collective-permute-start.3 = (f32[2,320,1024]{2,1,0:T(8,128)}, f32[2,320,1024]{2,1,0:T(8,128)}, u32[]{:S(2)}, u32[]{:S(2)}) collective-permute-start(f32[2,320,1024]{2,1,0:T(8,128)} %constant_dynamic-slice_fusion), channel_id=1, source_target_pairs={{0,1},{1,0},{2,3},{3,2},{4,5},{5,4},{6,7},{7,6},{8,9},{9,8},{10,11... | collective-permute-start | bytes 7864328 | tf_op jit(solution)/shard_map/ppermute | solution.py:439
  624.5 7.3 copy-start.37
  624.5 7.3 copy-start.38
  624.5 7.4 copy-start.35
  624.5 7.4 copy-start.34
  624.6 7.5 copy-start.40
  624.6 7.6 copy-start.39
  626.3 173.0 %collective-permute-start.1 = (f32[2,320,1024]{2,1,0:T(8,128)}, f32[2,320,1024]{2,1,0:T(8,128)}, u32[]{:S(2)}, u32[]{:S(2)}) collective-permute-start(f32[2,320,1024]{2,1,0:T(8,128)} %constant_dynamic-slice_fusion.3), channel_id=1, source_target_pairs={{0,1},{1,0},{2,3},{3,2},{4,5},{5,4},{6,7},{7,6},{8,9},{9,8},{10,11... | collective-permute-start | bytes 7864328 | tf_op jit(solution)/shard_map/ppermute | solution.py:439
  792.9 6.4 slice-start.8
  793.5 5.8 slice-start.9
  (28 other events, 69.3 us)
Sparse Core Ops, SparseCore 0:
  11.5 85.9 all-gather.6
  100.3 55.1 all-gather.8
  158.3 76.3 all-gather.10
  237.4 76.0 all-gather.12
  377.4 135.0 reduce-scatter.6
  519.0 111.7 reduce-scatter.12
  633.0 148.9 reduce-scatter.8
  784.4 144.8 reduce-scatter.10

commit v2 on v1

--- a/solution.py
+++ b/solution.py
@@ -275,7 +275,6 @@
     )
 
 
-BOTH = ("tensor", "dp")
 NT = (((1,), (1,)), ((), ()))
 NN = (((1,), (0,)), ((), ()))
 
@@ -310,7 +309,7 @@
 
 
 def attention_backward_kernel(
-    lengths, q_ref, k_ref, v_ref, lse_ref, g_ref, dq_ref, dk_ref, dv_ref, *, key_rows
+    lengths, q_ref, k_ref, v_ref, lse_ref, g_ref, d_ref, *, key_rows
 ):
     length = lengths[pl.program_id(0)]
     slots = q_ref.shape[1]
@@ -336,24 +335,25 @@
         dks.append(dot_nn(score_grad, plain))
         dqs.append(dot_nn(keys_t[head * HD : (head + 1) * HD], score_grad))
     first = lane < HD
-    dq_ref[0] = (jnp.transpose(jnp.concatenate(dqs, axis=0)) * scale).astype(BF16)
-    dk_ref[0, :key_rows] = (jnp.where(first, dks[0], dks[1]) * scale).astype(BF16)
-    dv_ref[0, :key_rows] = jnp.where(first, dvs[0], dvs[1]).astype(BF16)
+    d_ref[0, :, :PAIR] = (jnp.transpose(jnp.concatenate(dqs, axis=0)) * scale).astype(BF16)
+    d_ref[0, :key_rows, PAIR : 2 * PAIR] = (jnp.where(first, dks[0], dks[1]) * scale).astype(BF16)
+    d_ref[0, :key_rows, 2 * PAIR :] = jnp.where(first, dvs[0], dvs[1]).astype(BF16)
     if key_rows < slots:
-        rest = jnp.zeros((slots - key_rows, PAIR), BF16)
-        dk_ref[0, key_rows:] = rest
-        dv_ref[0, key_rows:] = rest
+        d_ref[0, key_rows:, PAIR:] = jnp.zeros((slots - key_rows, 2 * PAIR), BF16)
 
 
 def key_count(slots):
     return min(slots, -(-VALID // 16) * 16)
+
+
+def pair_block(slots, each, offset):
+    return pl.BlockSpec((1, slots, PAIR), lambda b, p, ln: (b, 0, each * p + offset))
 
 
 def attention_forward(lengths, qkv):
     images, slots, columns = qkv.shape
     width = columns // 3
     pairs = width // PAIR
-    part = lambda offset: pl.BlockSpec((1, slots, PAIR), lambda b, p, ln: (b, 0, offset + p))
     return pl.pallas_call(
         functools.partial(attention_forward_kernel, key_rows=key_count(slots)),
         out_shape=(
@@ -363,13 +363,13 @@
         grid_spec=pltpu.PrefetchScalarGridSpec(
             num_scalar_prefetch=1,
             grid=(images, pairs),
-            in_specs=[part(0), part(pairs), part(2 * pairs)],
+            in_specs=[pair_block(slots, 3, n) for n in range(3)],
             out_specs=(
-                part(0),
+                pair_block(slots, 1, 0),
                 pl.BlockSpec((1, 1, 2, slots), lambda b, p, ln: (b, p, 0, 0)),
             ),
         ),
-        compiler_params=pltpu.CompilerParams(vmem_limit_bytes=48 << 20),
+        compiler_params=pltpu.CompilerParams(vmem_limit_bytes=40 << 20),
         cost_estimate=pl.CostEstimate(
             flops=images * pairs * 2 * 4 * slots * slots * PAIR,
             bytes_accessed=images * slots * width * 8,
@@ -383,24 +383,20 @@
     images, slots, columns = qkv.shape
     width = columns // 3
     pairs = width // PAIR
-    part = lambda offset: pl.BlockSpec((1, slots, PAIR), lambda b, p, ln: (b, 0, offset + p))
-    piece = jax.ShapeDtypeStruct((images, slots, width), BF16)
     return pl.pallas_call(
         functools.partial(attention_backward_kernel, key_rows=key_count(slots)),
-        out_shape=(piece, piece, piece),
+        out_shape=jax.ShapeDtypeStruct(qkv.shape, BF16),
         grid_spec=pltpu.PrefetchScalarGridSpec(
             num_scalar_prefetch=1,
             grid=(images, pairs),
-            in_specs=[
-                part(0),
-                part(pairs),
-                part(2 * pairs),
+            in_specs=[pair_block(slots, 3, n) for n in range(3)]
+            + [
                 pl.BlockSpec((1, 1, 2, slots), lambda b, p, ln: (b, p, 0, 0)),
-                part(0),
+                pair_block(slots, 1, 0),
             ],
-            out_specs=(part(0), part(0), part(0)),
+            out_specs=pl.BlockSpec((1, slots, 3 * PAIR), lambda b, p, ln: (b, 0, p)),
         ),
-        compiler_params=pltpu.CompilerParams(vmem_limit_bytes=48 << 20),
+        compiler_params=pltpu.CompilerParams(vmem_limit_bytes=40 << 20),
         cost_estimate=pl.CostEstimate(
             flops=images * pairs * 2 * 10 * slots * slots * PAIR,
             bytes_accessed=images * slots * width * 14,
@@ -410,12 +406,186 @@
     )(lengths, qkv, qkv, qkv, lse, grads)
 
 
+def swap(array, axis, step):
+    return lax.ppermute(array, axis, [(n, n ^ step) for n in range(lax.axis_size(axis))])
+
+
+def shift(array, groups, by):
+    count = 4 * groups
+    return lax.ppermute(array, "dp", [(n, (n + 4 * by) % count) for n in range(count)])
+
+
+def place():
+    index = lax.axis_index("dp")
+    return jnp.stack(
+        [lax.axis_index("tensor"), index // 4, (index // 2) % 2, index % 2]
+    ).astype(jnp.int32)
+
+
+def assemble_kernel(where, *refs, groups, columns):
+    *sources, out_ref, extra_ref, sems = refs
+    t, z, x, c = [where[n] for n in range(4)]
+    half = sources[0].shape[2]
+    tail = extra_ref.shape[4]
+    copies = []
+
+    def move(source, target):
+        copies.append(pltpu.make_async_copy(source, target, sems.at[len(copies)]))
+        copies[-1].start()
+
+    for turn in range(2):
+        for kind in range(4):
+            source = sources[4 * turn + kind]
+            for near in range(2):
+                for ahead in range(groups):
+                    far = kind % 2
+                    along_t, along_x = (far, near) if kind < 2 else (near, far)
+                    rows = pl.ds((kind // 2) * half, half)
+                    origin = lax.rem(z + groups - ahead, groups), x ^ along_x, c ^ turn
+                    side = t ^ along_t
+                    start = pl.multiple_of(side * columns, 128)
+                    move(
+                        source.at[near, ahead, :, pl.ds(0, columns)],
+                        out_ref.at[(*origin, rows, pl.ds(start, columns))],
+                    )
+                    if kind < 2:
+                        move(
+                            source.at[near, ahead, pl.ds(0, tail), pl.ds(columns, 128)],
+                            extra_ref.at[(side, *origin)],
+                        )
+    for copy in copies:
+        copy.wait()
+
+
+def gather_staged(shard, vector, coords):
+    rows, columns = shard.shape
+    groups = lax.axis_size("dp") // 4
+    entries = vector.shape[0]
+    tail = 16
+    beside = jnp.zeros((rows * 128,), BF16).at[:entries].set(vector).reshape(rows, 128)
+    shard = jnp.concatenate([shard, beside], axis=1)
+    line = jnp.stack([shard] + [shift(shard, groups, by) for by in range(1, groups)])
+    upper, lower = line[:, : rows // 2], line[:, rows // 2 :]
+    upper = jnp.stack([upper, swap(upper, "dp", 2)])
+    lower = jnp.stack([lower, swap(lower, "tensor", 1)])
+    mine = [upper, swap(upper, "tensor", 1), lower, swap(lower, "dp", 2)]
+    theirs = [swap(piece, "dp", 1) for piece in mine]
+    anywhere = pl.BlockSpec(memory_space=pl.ANY)
+    inside = pl.BlockSpec(memory_space=pltpu.VMEM)
+    whole, extra = pl.pallas_call(
+        functools.partial(assemble_kernel, groups=groups, columns=columns),
+        out_shape=(
+            jax.ShapeDtypeStruct((groups, 2, 2, rows, 2 * columns), BF16),
+            jax.ShapeDtypeStruct((2, groups, 2, 2, tail, 128), BF16),
+        ),
+        grid_spec=pltpu.PrefetchScalarGridSpec(
+            num_scalar_prefetch=1,
+            in_specs=[anywhere] * 8,
+            out_specs=(inside, inside),
+            scratch_shapes=[pltpu.SemaphoreType.DMA((24 * groups,))],
+        ),
+        compiler_params=pltpu.CompilerParams(vmem_limit_bytes=(4 << 20) + 16 * groups * rows * columns),
+        cost_estimate=pl.CostEstimate(
+            flops=0, transcendentals=0, bytes_accessed=32 * groups * rows * columns
+        ),
+        name="assemble",
+    )(coords, *mine, *theirs)
+    extra = extra.reshape(2, 4 * groups, tail * 128)[:, :, :entries]
+    return whole.reshape(4 * groups * rows, 2 * columns), extra
+
+
+def beside_kernel(source, out_ref, sems, *, offset, columns):
+    copies = [
+        pltpu.make_async_copy(
+            source.at[t, :, pl.ds(offset, columns)],
+            out_ref.at[:, pl.ds(t * columns, columns)],
+            sems.at[t],
+        )
+        for t in range(2)
+    ]
+    for copy in copies:
+        copy.start()
+    for copy in copies:
+        copy.wait()
+
+
+def beside(gathered, offset, columns):
+    rows = gathered.shape[1]
+    return pl.pallas_call(
+        functools.partial(beside_kernel, offset=offset, columns=columns),
+        out_shape=jax.ShapeDtypeStruct((rows, 2 * columns), BF16),
+        in_specs=[pl.BlockSpec(memory_space=pl.ANY)],
+        out_specs=pl.BlockSpec(memory_space=pltpu.VMEM),
+        scratch_shapes=[pltpu.SemaphoreType.DMA((2,))],
+        compiler_params=pltpu.CompilerParams(vmem_limit_bytes=(4 << 20) + 4 * rows * columns),
+        cost_estimate=pl.CostEstimate(flops=0, transcendentals=0, bytes_accessed=8 * rows * columns),
+        name="beside",
+    )(gathered)
+
+
+def take(array, index, axis):
+    return lax.dynamic_index_in_dim(array, index, axis, keepdims=False)
+
+
+def side(array, index):
+    half = array.shape[-1] // 2
+    return lax.dynamic_slice_in_dim(array, index * half, half, array.ndim - 1)
+
+
+class Sum:
+    def __init__(self, whole, coords, sent=BF16):
+        self.t, self.z, self.x, self.c = [coords[n] for n in range(4)]
+        self.groups = lax.axis_size("dp") // 4
+        self.rows = whole.shape[0] // (4 * self.groups)
+        self.sent = sent
+        self.state = [whole.reshape(self.groups, 2, 2, self.rows, whole.shape[1])]
+        self.stage = 0
+
+    def over_tensor(self, array):
+        return side(array, self.t) + swap(side(array, 1 - self.t).astype(self.sent), "tensor", 1).astype(F32)
+
+    def over_pair(self, array, mine, dim, step):
+        return take(array, mine, dim) + swap(take(array, 1 - mine, dim).astype(self.sent), "dp", step).astype(F32)
+
+    def step(self):
+        half = self.rows // 2
+        if self.stage == 0:
+            self.state = [self.over_pair(self.state[0], self.c, 2, 1)]
+        elif self.stage == 1:
+            whole = self.state[0]
+            self.state = [
+                self.over_tensor(whole[:, :, :half]),
+                self.over_pair(whole[:, :, half:], self.x, 1, 2),
+            ]
+        elif self.stage == 2:
+            upper, lower = self.state
+            self.state = [self.over_pair(upper, self.x, 1, 2), self.over_tensor(lower)]
+        elif self.stage == 3:
+            line = jnp.concatenate(self.state, axis=1)
+            total = take(line, self.z, 0)
+            for by in range(1, self.groups):
+                sent = take(line, lax.rem(self.z + by, self.groups), 0).astype(self.sent)
+                total = total + shift(sent, self.groups, by).astype(F32)
+            self.state = [total]
+        self.stage += 1
+
+    def result(self):
+        while self.stage < 4:
+            self.step()
+        return self.state[0]
+
+
+def advance(sums, *values):
+    for one in sums:
+        one.step()
+    states = [one.state for one in sums]
+    values, states = lax.optimization_barrier((values, states))
+    for one, state in zip(sums, states):
+        one.state = state
+    return values if len(values) > 1 else values[0]
+
+
 def to_images(rows):
-    count = lax.axis_size("tensor")
-    if count == 1:
-        return rows
-    if count > 2:
-        return lax.all_to_all(rows, "tensor", 0, 1, tiled=True)
     me = lax.axis_index("tensor")
     own, part = rows.shape[0] // 2, rows.shape[1]
     kept = lax.dynamic_slice_in_dim(rows, me * own, own, 0)
@@ -427,16 +597,11 @@
 
 
 def to_slots(rows):
-    count = lax.axis_size("tensor")
-    if count == 1:
-        return jnp.swapaxes(rows, 0, 1)
-    if count > 2:
-        return jnp.swapaxes(lax.all_to_all(rows, "tensor", 1, 0, tiled=True), 0, 1)
     me = lax.axis_index("tensor")
     own, part = rows.shape[0], rows.shape[1] // 2
     kept = lax.dynamic_slice_in_dim(rows, me * part, part, 1)
-    sent = lax.dynamic_slice_in_dim(rows, (1 - me) * part, part, 1)
-    came = lax.ppermute(sent, "tensor", [(0, 1), (1, 0)])
+    sent = lax.dynamic_slice_in_dim(rows, (1 - me) * part, part, 1).astype(BF16)
+    came = lax.ppermute(sent, "tensor", [(0, 1), (1, 0)]).astype(rows.dtype)
     first = jnp.where(me == 0, kept, came)
     second = jnp.where(me == 0, came, kept)
     return jnp.swapaxes(jnp.concatenate([first, second], axis=0), 0, 1)
@@ -485,121 +650,111 @@
     cotangent,
 ):
     width = inputs.shape[2]
-    slots = pad_mask.shape[1]
-    tensors = lax.axis_size("tensor")
-    shards = lax.axis_size("dp") * tensors
     me = lax.axis_index("tensor")
-    images = inputs.shape[1] // tensors
+    images = inputs.shape[1] // 2
     head_width = qkv_weight.shape[2]
+    pairs = head_width // PAIR
     hidden = up_weight.shape[1]
     piece = norm1_gain.shape[1]
-    hidden_piece = up_bias.shape[1]
-
-    flat = jnp.concatenate(
+    depth = qkv_weight.shape[0]
+    coords = place()
+    product = functools.partial(jnp.einsum, preferred_element_type=F32)
+
+    x = to_images(jnp.swapaxes(inputs, 0, 1)).astype(F32)
+    vector = jnp.concatenate(
         [
             v.reshape(-1)
             for v in (norm1_gain, norm1_shift, out_bias, norm2_gain, norm2_shift, down_bias, qv_bias, up_bias)
         ]
-    ).reshape(1, -1)
-    flat = lax.all_gather(flat, BOTH, axis=0, tiled=True).astype(F32)
+    )
+    paired = jnp.swapaxes(qkv_weight.reshape(depth, 3, pairs, PAIR), 1, 2).reshape(depth, -1)
+    qkv_full, flat = gather_staged(paired, vector, coords)
+    flat = flat.astype(F32)
     gain_one, shift_one, out_shift, gain_two, shift_two, down_shift = [
-        flat[:, n * piece : (n + 1) * piece].reshape(width) for n in range(6)
+        flat[:, :, n * piece : (n + 1) * piece].reshape(width) for n in range(6)
     ]
-    query_bias = flat[:, 6 * piece : 7 * piece].reshape(tensors, head_width)
-    value_bias = flat[:, 7 * piece : 8 * piece].reshape(tensors, head_width)
-    up_row = flat[:, 8 * piece :].reshape(tensors, hidden)
-
-    def gather(shard):
-        whole = lax.all_gather(shard, BOTH, axis=0, tiled=True)
-        return whole.reshape(tensors, -1, shard.shape[1])
-
-    qkv_full = gather(qkv_weight.reshape(qkv_weight.shape[0], -1))
-    out_full = gather(jnp.transpose(out_weight))
-    up_full = gather(up_weight)
-    down_full = gather(jnp.transpose(down_weight))
-
+    query_bias = flat[:, :, 6 * piece : 7 * piece].reshape(2 * pairs, PAIR)
+    value_bias = flat[:, :, 7 * piece : 8 * piece].reshape(2 * pairs, PAIR)
+    qkv_bias = jnp.stack([query_bias, jnp.zeros_like(query_bias), value_bias], axis=1).reshape(-1)
+    up_row = flat[:, :, 8 * piece :].reshape(2 * hidden)
+
+    others = jnp.concatenate([jnp.transpose(out_weight), up_weight, jnp.transpose(down_weight)], axis=1)
+    others = lax.all_gather(others, ("tensor", "dp"), axis=0, tiled=True).reshape(2, width, -1)
+    out_full = beside(others, 0, head_width)
+    up_full = beside(others, head_width, hidden)
+    down_full = beside(others, head_width + hidden, hidden)
+
+    here = lax.dynamic_slice_in_dim(pad_mask, me * inputs.shape[0], inputs.shape[0], 1) > 0
+    down_shift_grad = token_sum(cotangent * jnp.transpose(here).astype(F32)[:, :, None])
     mask = lax.dynamic_slice_in_dim(pad_mask, me * images, images, 0)
     lengths = jnp.sum(mask, axis=1).astype(jnp.int32)
     kept = (mask > 0).astype(F32)[:, :, None]
-    x = to_images(jnp.swapaxes(inputs, 0, 1)).astype(F32)
-    cot = to_images(jnp.swapaxes(cotangent, 0, 1))
 
     unit_one, inverse_one = normalize(x)
     normed_one = (unit_one * gain_one + shift_one).astype(BF16)
-    parts = range(tensors)
-    product = functools.partial(jnp.einsum, preferred_element_type=F32)
-    qkvs, attendeds, lses = [], [], []
-    for t in parts:
-        bias = jnp.concatenate([query_bias[t], jnp.zeros((head_width,), F32), value_bias[t]])
-        qkvs.append((product("bsd,dc->bsc", normed_one, qkv_full[t]) + bias).astype(BF16))
-        attended, lse = attention_forward(lengths, qkvs[t])
-        attendeds.append(attended)
-        lses.append(lse)
-    projected = sum(product("bsc,dc->bsd", attendeds[t], out_full[t]) for t in parts)
+    qkv = (product("bsd,dc->bsc", normed_one, qkv_full) + qkv_bias).astype(BF16)
+    cotangent, qkv = lax.optimization_barrier((cotangent, qkv))
+    cot = to_images(jnp.swapaxes(cotangent.astype(BF16), 0, 1)).astype(F32)
+    attended, lse = attention_forward(lengths, qkv)
+    projected = product("bsc,dc->bsd", attended, out_full)
     after_attn = x + projected + out_shift
     unit_two, inverse_two = normalize(after_attn)
     normed_two = (unit_two * gain_two + shift_two).astype(BF16)
-    acts, slopes = [], []
-    for t in parts:
-        up_values = product("bsd,df->bsf", normed_two, up_full[t]) + up_row[t]
-        act, slope = gelu_pair(up_values)
-        acts.append(act)
-        slopes.append(slope)
-    out_grad = cot * kept
-    out_low = out_grad.astype(BF16)
-    down_shift_grad = token_sum(out_grad)
-
-    def scatter(grads):
-        stacked = jnp.concatenate(grads, axis=0).astype(BF16)
-        return lax.psum_scatter(stacked, BOTH, scatter_dimension=0, tiled=True).astype(F32)
-
-    down_owned = scatter([product("bsd,bsf->df", out_low, acts[t]) for t in parts])
-    up_grads = []
-    for t in parts:
-        act_grad = product("bsd,df->bsf", out_low, down_full[t])
-        up_grads.append((act_grad * slopes[t]).astype(BF16))
-    up_owned = scatter([product("bsd,bsf->df", normed_two, up_grads[t]) for t in parts])
-    normed_two_grad = sum(product("bsf,df->bsd", up_grads[t], up_full[t]) for t in parts)
-    mlp_out = sum(product("bsf,df->bsd", acts[t], down_full[t]) for t in parts)
-    block_output = to_slots((after_attn + mlp_out + down_shift) * kept)
-    up_shift_grad = jnp.stack([token_sum(up_grads[t]) for t in parts])
+    up_values = product("bsd,df->bsf", normed_two, up_full) + up_row
+    act, slope = gelu_pair(up_values)
+    out_low = (cot * kept).astype(BF16)
+    out_grad = out_low.astype(F32)
+
+    down = Sum(product("bsd,bsf->df", out_low, act), coords)
+    (out_low,), (down.state,) = lax.optimization_barrier(((out_low,), (down.state,)))
+    act_grad = product("bsd,df->bsf", out_low, down_full)
+    up_grad = (act_grad * slope).astype(BF16)
+    up_grad, normed_two = advance([down], up_grad, normed_two)
+    up = Sum(product("bsd,bsf->df", normed_two, up_grad), coords)
+    up_shift_grad = token_sum(up_grad)
+    down.step()
+    (up_grad,), (down.state, up.state) = lax.optimization_barrier(((up_grad,), (down.state, up.state)))
+    normed_two_grad = product("bsf,df->bsd", up_grad, up_full)
+    normed_two_grad = advance([down, up], normed_two_grad)
     gain_two_grad = token_sum(normed_two_grad * unit_two)
     shift_two_grad = token_sum(normed_two_grad)
     after_attn_grad = out_grad + normalize_back(normed_two_grad, unit_two, inverse_two, gain_two)
     out_shift_grad = token_sum(after_attn_grad)
     proj_low = after_attn_grad.astype(BF16)
-    out_owned = scatter([product("bsd,bsc->dc", proj_low, attendeds[t]) for t in parts])
-    pieces, query_sums, value_sums = [], [], []
-    for t in parts:
-        attended_grad = product("bsd,dc->bsc", proj_low, out_full[t]).astype(BF16)
-        pieces.append(attention_backward(lengths, qkvs[t], lses[t], attended_grad))
-        query_sums.append(token_sum(pieces[t][0]))
-        value_sums.append(token_sum(pieces[t][2]))
-    qkv_owned = scatter(
-        [
-            jnp.concatenate([product("bsd,bsc->dc", normed_one, p) for p in pieces[t]], axis=1)
-            for t in parts
-        ]
-    )
-    normed_one_grad = sum(
-        product(
-            "bsc,dc->bsd",
-            pieces[t][n],
-            qkv_full[t][:, n * head_width : (n + 1) * head_width],
-        )
-        for t in parts
-        for n in range(3)
-    )
+    out = Sum(product("bsd,bsc->dc", proj_low, attended), coords)
+    attended_grad = product("bsd,dc->bsc", proj_low, out_full).astype(BF16)
+    down.step()
+    up.step()
+    (attended_grad, qkv), (down.state, up.state, out.state) = lax.optimization_barrier(
+        ((attended_grad, qkv), (down.state, up.state, out.state))
+    )
+    qkv_grad = attention_backward(lengths, qkv, lse, attended_grad)
+    qkv_grad, normed_one = advance([up, out], qkv_grad, normed_one)
+    qkv_sum = Sum(product("bsd,bsc->dc", normed_one, qkv_grad), coords)
+    up.step()
+    out.step()
+    (qkv_grad, act), (up.state, out.state, qkv_sum.state) = lax.optimization_barrier(
+        ((qkv_grad, act), (up.state, out.state, qkv_sum.state))
+    )
+    mlp_out = product("bsf,df->bsd", act, down_full)
+    mlp_out, qkv_grad = advance([out, qkv_sum], mlp_out, qkv_grad)
+    block_output = to_slots((after_attn + mlp_out + down_shift) * kept)
+    normed_one_grad = product("bsc,dc->bsd", qkv_grad, qkv_full)
+    bias_sums = token_sum(qkv_grad).reshape(2 * pairs, 3, PAIR)
+    normed_one_grad = advance([out, qkv_sum], normed_one_grad)
     gain_one_grad = token_sum(normed_one_grad * unit_one)
     shift_one_grad = token_sum(normed_one_grad)
     input_grad = after_attn_grad + normalize_back(normed_one_grad, unit_one, inverse_one, gain_one)
     input_grad = to_slots(input_grad)
 
     vectors = [gain_one_grad, shift_one_grad, out_shift_grad, gain_two_grad, shift_two_grad, down_shift_grad]
-    vectors += [jnp.stack(query_sums), jnp.stack(value_sums), up_shift_grad]
-    small = jnp.concatenate([v.reshape(shards, -1) for v in vectors], axis=1)
-    small = lax.psum_scatter(small, BOTH, scatter_dimension=0, tiled=True)
+    vectors += [bias_sums[:, 0], bias_sums[:, 2], up_shift_grad]
+    small = jnp.concatenate([v.reshape(2, lax.axis_size("dp"), -1) for v in vectors], axis=2)
+    entries = small.shape[2]
+    small = jnp.swapaxes(small.reshape(2, -1, entries // 2), 0, 1).reshape(-1, entries)
+    small = Sum(small, coords, F32).result().reshape(1, entries)
     row = lambda n: small[:, n * piece : (n + 1) * piece]
+    qkv_owned = jnp.swapaxes(qkv_sum.result().reshape(depth, pairs, 3, PAIR), 1, 2)
     return (
         block_output,
         input_grad,
@@ -607,13 +762,13 @@
         row(1),
         qkv_owned.reshape(qkv_weight.shape),
         jnp.stack([row(6), row(7)], axis=0),
-        jnp.transpose(out_owned),
+        jnp.transpose(out.result()),
         row(2),
         row(3),
         row(4),
-        up_owned,
-        small[:, 8 * piece : 8 * piece + hidden_piece],
-        jnp.transpose(down_owned),
+        up.result(),
+        small[:, 8 * piece :],
+        jnp.transpose(down.result()),
         row(5),
     )
 
@@ -655,7 +810,7 @@
     dims = dict(zip(mesh.axis_names, mesh.devices.shape))
 
     def choose(inputs, *rest):
-        whole_images = inputs.shape[1] % dims["tensor"] == 0
+        whole_images = dims["tensor"] == 2 and dims["dp"] % 4 == 0 and inputs.shape[1] % 2 == 0
         return (by_images if whole_images else on_device)(inputs, *rest)
 
     return jax.shard_map(

time: 945 us -> 727 us (0.77)
  blocking collectives: 198 us -> 0 us
  waiting for transfers between devices: 270 us -> 157 us
  starting transfers between devices: 5.34 us -> 75 us
  local copies, waits for them, and re-layouts: 63.8 us -> 133 us
  matrix products: 212 us -> 149 us
  other arithmetic: 91.4 us -> 102 us
    unnamed x1 -> x0, blocking collectives: 154 us -> none
    ppermute x2 -> x53, waiting for transfers between devices: 0.01 us -> 128 us  [the longest x33 66.9 us: swap(): lax.ppermute(array, axis, [(n, n ^ step) for n in range(lax.axis_size(axi...]
    reduce_scatter x3 -> x0, waiting for transfers between devices: 116 us -> none  [scatter(): lax.psum_scatter(stacked, BOTH, scatter_dimension=0, tiled=True).astype(F32)]
    all_gather x4 -> x1, waiting for transfers between devices: 108 us -> 0.01 us  [by_images(): lax.all_gather(others, ('tensor', 'dp'), axis=0, tiled=True)]
    ppermute x2 -> x53, starting transfers between devices: 2.05 us -> 71.9 us  [the longest x18 44.5 us: shift(): lax.ppermute(array, 'dp', [(n, (n + 4 * by) % count) for n in range(count)])]
    dot_general x32 -> x12, matrix products: 212 us -> 149 us  [the longest x1 23.8 us: by_images(): act_grad = product('bsd,df->bsf', out_low, down_full)]
    concatenate x5 -> x1, other arithmetic: 59.9 us -> 2.04 us  [by_images(): jnp.concatenate([jnp.transpose(out_weight), up_weight, jnp.transpose(down...]
    add x0 -> x30, other arithmetic: none -> 52.9 us  [the longest x15 34.6 us: over_pair(): take(array, mine, dim)]
  transfers between devices with their start and end apart: 12 -> 56, of which waited for: 4 -> 21; matrix products, arithmetic and copies ran while one was open for 31% -> 31% of each run, Pallas kernels for 9% -> 12%
where the time goes in v2:
time: 727 us; the launch traced here: 720 us
  waiting for transfers between devices  157 us (22%)
  matrix products  149 us (20%)
  local copies, waits for them, and re-layouts  133 us (18%)
  other arithmetic  102 us (14%)
  Pallas kernels  87.7 us (12%)
  starting transfers between devices  75 us (10%)
  between operations  16.2 us (2%)
    ppermute x33, waiting for transfers between devices, swap(): lax.ppermute(array, axis, [(n, n ^ step) for n in range(lax.axis_size(axi...  66.9 us
    unnamed x180, local copies, waits for them, and re-layouts  59.9 us
    pallas_call x1, Pallas kernels, attention_backward(): pl.pallas_call(functools.partial(attention_backward_kernel, key_rows=key_...  48.2 us
    ppermute x18, starting transfers between devices, shift(): lax.ppermute(array, 'dp', [(n, (n + 4 * by) % count) for n in range(count)])  44.5 us
    add x15, other arithmetic, over_pair(): take(array, mine, dim)  34.6 us
    ppermute x18, waiting for transfers between devices, shift(): lax.ppermute(array, 'dp', [(n, (n + 4 * by) % count) for n in range(count)])  33.6 us
    pallas_call x1, Pallas kernels, attention_forward(): pl.pallas_call(functools.partial(attention_forward_kernel, key_rows=key_c...  31.8 us
    ppermute x2, waiting for transfers between devices, to_images(): came = lax.ppermute(sent, 'tensor', [(0, 1), (1, 0)])  29.3 us
  transfers between devices with their start and end apart: 56, of which 21 were waited for; matrix products, arithmetic and copies ran while one was open for 31% of the time, Pallas kernels for 12%

profile of v2, /device:TPU:0, one launch (start us, length us, event | category | flops | bytes accessed | tf_op | source)
XLA Modules:
  0.0 720.1 jit_solution(9029864253853822149)
XLA Ops:
  11.4 4.8 concatenate.35
  16.2 4.1 collective-permute-start.2
  24.1 20.4 %collective-permute-done.2 = bf16[64,1664]{1,0:T(8,128)(2,1)S(1)} collective-permute-done((bf16[64,1664]{1,0:T(8,128)(2,1)S(1)}, bf16[64,1664]{1,0:T(8,128)(2,1)S(1)}, u32[]{:S(2)}, u32[]{:S(2)}) %collective-permute-start.2) | collective-permute-done | bytes 213024 | tf_op jit(solution)/shard_map/ppermute | solution.py:415
  49.7 3.8 constant_dynamic-slice_fusion.22
  58.1 5.7 collective-permute-done.6
  67.4 29.3 %collective-permute-done = bf16[2,320,1024]{2,1,0:T(8,128)(2,1)} collective-permute-done((bf16[2,320,1024]{2,1,0:T(8,128)(2,1)}, bf16[2,320,1024]{2,1,0:T(8,128)(2,1)}, u32[]{:S(2)}, u32[]{:S(2)}) %collective-permute-start) | collective-permute-done | bytes 1310752 | tf_op jit(solution)/shard_map/ppermute | solution.py:593
  98.1 21.9 %collective-permute-done.5.refs_1_ = bf16[2,4,32,1664]{3,2,1,0:T(8,128)(2,1)S(1)} collective-permute-done((bf16[2,4,32,1664]{3,2,1,0:T(8,128)(2,1)S(1)}, bf16[2,4,32,1664]{3,2,1,0:T(8,128)(2,1)S(1)}, u32[]{:S(2)}, u32[]{:S(2)}) %collective-permute-start.5) | collective-permute-done | bytes 852000 | tf_op jit(solution)/shard_map/ppermute | solution.py:410
  123.6 4.4 assemble.1
  134.6 14.2 %add_convert_fusion.q_ref.k_ref.v_ref = bf16[2,640,3072]{2,1,0:T(8,128)(2,1)} fusion(f32[3072]{0:T(1024)S(1)} %add.403, bf16[2,640,1024]{2,1,0:T(8,128)(2,1)S(1)} %fusion.20, bf16[1024,3072,1]{1,0,2:T(8,128)(2,1)} %bitcast.251), kind=kOutput, calls=%fused_computation.11 | convolution fusion | flops 8060928000 | bytes 16789504 | tf_op jit(solution)/shard_map/bsd,dc->bsc/dot_general | solution.py:695
  159.4 31.8 %attention_forward.1 = (bf16[2,640,1024]{2,1,0:T(8,128)(2,1)S(1)}, f32[2,8,2,640]{3,2,1,0:T(2,128)S(1)}) custom-call(s32[2]{0:T(128)S(1)} %fusion.88.lengths, bf16[2,640,3072]{2,1,0:T(8,128)(2,1)S(1)} %copy-done.11, bf16[2,640,3072]{2,1,0:T(8,128)(2,1)S(1)} %copy-done.11, bf16[2,640,3072]{2,1,0:T(8,128)(2,1)S(1)} %copy-done.11), custom_call_target="tpu_custom_call" | custom-call | flops 6710886400 | bytes 10485760 | tf_op jit(solution)/shard_map/attention_forward/pallas_call | solution.py:357
  197.1 6.4 copy-done
  203.8 6.0 copy-done.1
  223.5 17.0 %multiply_convert_fusion = (bf16[2,640,4096]{2,1,0:T(8,128)(2,1)}, f32[2,640,4096]{2,1,0:T(8,128)}) fusion(f32[4096]{0:T(1024)S(1)} %bitcast.287, bf16[2,640,1024]{2,1,0:T(8,128)(2,1)S(1)} %add_convert_fusion.1, bf16[1024,4096]{1,0:T(8,128)(2,1)S(1)} %copy-done.5), kind=kOutput, calls=%fused_computation.8 | convolution fusion | flops 10768875520 | bytes 42483712 | tf_op jit(solution)/shard_map/bsd,df->bsf/dot_general | solution.py:703
  240.5 15.3 %fusion.108 = f32[1024,4096,1]{1,0,2:T(8,128)S(1)} fusion(bf16[2,640,1024]{2,1,0:T(8,128)(2,1)} %multiply_convert_fusion.1, bf16[2,640,4096]{2,1,0:T(8,128)(2,1)} %get-tuple-element.100), kind=kOutput, calls=%fused_computation.261 | convolution fusion | flops 10737418240 | bytes 29884416 | tf_op jit(solution)/shard_map/bsd,bsf->df/dot_general | solution.py:708
  255.9 5.7 copy-done.31
  264.4 3.6 multiply_reduce_fusion
  269.3 6.4 copy-done.2
  277.4 23.8 %fusion.5 = bf16[2,640,4096]{2,1,0:T(8,128)(2,1)} fusion(f32[2,640,4096]{2,1,0:T(8,128)} %get-tuple-element.226, bf16[2,640,1024]{2,1,0:T(8,128)(2,1)S(1)} %copy-done.40, f32[4096]{0:T(1024)S(1)} %bitcast.288, bf16[1024,4096]{1,0:T(8,128)(2,1)S(1)} %beside.5), kind=kOutput, calls=%fused_computation.6 | convolution fusion | flops 10795089920 | bytes 42483712 | tf_op jit(solution)/shard_map/bsd,df->bsf/dot_general | solution.py:710
  301.3 5.8 bitcast_add_fusion.1
  313.6 17.3 %fusion.109 = f32[1024,4096,1]{1,0,2:T(8,128)} fusion(bf16[2,640,1024]{2,1,0:T(8,128)(2,1)S(1)} %add_convert_fusion.1, bf16[2,640,4096]{2,1,0:T(8,128)(2,1)} %fusion.5), kind=kOutput, calls=%fused_computation.262 | convolution fusion | flops 10737418240 | bytes 29884416 | tf_op jit(solution)/shard_map/bsd,bsf->df/dot_general | solution.py:713
  330.9 6.3 convert_reduce_fusion
  340.8 6.8 fusion.29
  350.9 13.8 %fusion.9 = f32[2,640,1024]{2,1,0:T(8,128)S(1)} fusion(bf16[2,640,4096]{2,1,0:T(8,128)(2,1)} %fusion.5, bf16[1024,4096]{1,0:T(8,128)(2,1)S(1)} %bitcast.250), kind=kOutput, calls=%fused_computation.17 | convolution fusion | flops 10737418240 | bytes 24117248 | tf_op jit(solution)/shard_map/bsf,df->bsd/dot_general | solution.py:717
  368.0 10.2 %bitcast_add_fusion = f32[4,2,64,4096]{3,2,0,1:T(8,128)} fusion(bf16[4,2,64,4096]{3,2,0,1:T(8,128)(2,1)} %collective-permute-done.18, f32[4,2,2,64,4096]{4,3,2,1,0:T(8,128)} %bitcast.268, s32[]{:T(128)S(6)} %select_n.187), kind=kLoop, calls=%fused_computation.12 | loop fusion | flops 4194304 | bytes 20971524 | tf_op jit(solution)/shard_map/add | solution.py:548
  381.6 15.5 %collective-permute-start.19 = (bf16[64,2048]{1,0:T(8,128)(2,1)}, bf16[64,2048]{1,0:T(8,128)(2,1)}, u32[]{:S(2)}, u32[]{:S(2)}) collective-permute-start(bf16[64,2048]{1,0:T(8,128)(2,1)} %get-tuple-element.187), channel_id=1, source_target_pairs={{0,8},{2,10},{4,12},{6,14},{8,16},{10,18},{12,20},{14,22},{16,24},... | collective-permute-start | bytes 786440 | tf_op jit(solution)/shard_map/ppermute | solution.py:415
  397.1 4.2 collective-permute-start.20
  401.3 4.9 fusion.99
  408.9 4.5 fusion.38
  413.5 4.7 fusion.100
  423.1 4.1 fusion.34.g_ref
  431.6 14.7 %collective-permute-done.22 = bf16[4,2,32,2048]{3,2,0,1:T(8,128)(2,1)} collective-permute-done((bf16[4,2,32,2048]{3,2,0,1:T(8,128)(2,1)S(1)}, bf16[4,2,32,2048]{3,2,0,1:T(8,128)(2,1)}, u32[]{:S(2)}, u32[]{:S(2)}) %collective-permute-start.22) | collective-permute-done | bytes 1048608 | tf_op jit(solution)/shard_map/ppermute | solution.py:410
  451.9 48.2 %attention_backward.1 = bf16[2,640,3072]{2,1,0:T(8,128)(2,1)S(1)} custom-call(s32[2]{0:T(128)S(1)} %copy-done.9, bf16[2,640,3072]{2,1,0:T(8,128)(2,1)} %add_convert_fusion.q_ref.k_ref.v_ref, bf16[2,640,3072]{2,1,0:T(8,128)(2,1)} %add_convert_fusion.q_ref.k_ref.v_ref, bf16[2,640,3072]{2,1,0:T(8,128)(2,1)} %add_convert_fusion.q_ref.k_ref.v_ref, ...), custom_call_target="tpu_custom_call" | custom-call | flops 16777216000 | bytes 18350080 | tf_op jit(solution)/shard_map/attention_backward/pallas_call | solution.py:386
  503.4 3.7 collective-permute-start.29
  511.7 10.3 %fusion.110 = f32[1024,3072,1]{1,0,2:T(8,128)S(1)} fusion(bf16[2,640,1024]{2,1,0:T(8,128)(2,1)} %copy-done.39, bf16[2,640,3072]{2,1,0:T(8,128)(2,1)S(1)} %attention_backward.1), kind=kOutput, calls=%fused_computation.263 | convolution fusion | flops 8053063680 | bytes 23068672 | tf_op jit(solution)/shard_map/bsd,bsc->dc/dot_general | solution.py:733
  524.7 4.5 collective-permute-done.28
  534.0 15.1 %fusion.6 = f32[2,640,1024]{2,1,0:T(8,128)} fusion(bf16[2,640,4096]{2,1,0:T(8,128)(2,1)} %get-tuple-element.100, bf16[1024,4096]{1,0:T(8,128)(2,1)S(1)} %bitcast.248), kind=kOutput, calls=%fused_computation.14 | convolution fusion | flops 10737418240 | bytes 24117248 | tf_op jit(solution)/shard_map/bsf,df->bsd/dot_general | solution.py:739
  557.8 7.8 %bitcast_add_fusion.2 = f32[4,2,64,3072]{3,2,0,1:T(8,128)} fusion(bf16[4,2,64,3072]{3,2,0,1:T(8,128)(2,1)} %collective-permute-done.34, f32[4,2,2,64,3072]{4,3,2,1,0:T(8,128)} %bitcast.270, s32[]{:T(128)S(6)} %select_n.187), kind=kLoop, calls=%fused_computation.26 | loop fusion | flops 3145728 | bytes 15728644 | tf_op jit(solution)/shard_map/add | solution.py:548
  565.6 10.4 %fusion.111 = f32[2,640,1024]{2,1,0:T(8,128)} fusion(bf16[2,640,3072]{2,1,0:T(8,128)(2,1)S(1)} %attention_backward.1, bf16[1024,3072,1]{1,0,2:T(8,128)(2,1)S(1)} %bitcast.254), kind=kOutput, calls=%fused_computation.264 | convolution fusion | flops 8053063680 | bytes 19398656 | tf_op jit(solution)/shard_map/bsc,dc->bsd/dot_general | solution.py:742
  578.1 3.8 collective-permute-start.38
  596.8 10.2 %collective-permute-done.40 = bf16[4,32,3072]{2,1,0:T(8,128)(2,1)} collective-permute-done((bf16[4,32,3072]{2,1,0:T(8,128)(2,1)}, bf16[4,32,3072]{2,1,0:T(8,128)(2,1)}, u32[]{:S(2)}, u32[]{:S(2)}) %collective-permute-start.40) | collective-permute-done | bytes 786464 | tf_op jit(solution)/shard_map/ppermute | solution.py:410
  614.8 4.2 fusion.25
  624.8 5.0 fusion.24
  644.3 3.7 dynamic-slice_convert_fusion.3
  662.2 4.4 collective-permute-done.53
  668.0 12.1 %collective-permute-done.41 = bf16[2,320,1024]{2,1,0:T(8,128)(2,1)} collective-permute-done((bf16[2,320,1024]{2,1,0:T(8,128)(2,1)}, bf16[2,320,1024]{2,1,0:T(8,128)(2,1)}, u32[]{:S(2)}, u32[]{:S(2)}) %collective-permute-start.41) | collective-permute-done | bytes 1310752 | tf_op jit(solution)/shard_map/ppermute | solution.py:604
  683.4 5.7 copy.87
  689.1 15.3 %collective-permute-done.35 = bf16[2,320,1024]{2,1,0:T(8,128)(2,1)} collective-permute-done((bf16[2,320,1024]{2,1,0:T(8,128)(2,1)}, bf16[2,320,1024]{2,1,0:T(8,128)(2,1)}, u32[]{:S(2)}, u32[]{:S(2)}) %collective-permute-start.35) | collective-permute-done | bytes 1310752 | tf_op jit(solution)/shard_map/ppermute | solution.py:604
  707.0 5.7 copy.86
  (429 shorter events, 196.3 us)
Async XLA Ops:
  7.2 189.9 %all-gather.2.cloned.1.call-start = ((), (), s32[]{:S(2)}) async-start(), calls=%async_computation | async-start | bytes 19464192 | tf_op jit(solution)/shard_map/all_gather | solution.py:682
  16.2 28.3 %collective-permute-start.2 = (bf16[64,1664]{1,0:T(8,128)(2,1)S(1)}, bf16[64,1664]{1,0:T(8,128)(2,1)S(1)}, u32[]{:S(2)}, u32[]{:S(2)}) collective-permute-start(bf16[64,1664]{1,0:T(8,128)(2,1)S(1)} %get-tuple-element.201), channel_id=1, source_target_pairs={{0,16},{2,18},{4,20},{6,22},{8,24},{10,26},{12,28},{14,30},{16,0},... | collective-permute-start | bytes 638984 | tf_op jit(solution)/shard_map/ppermute | solution.py:415
  20.3 24.2 %collective-permute-start.1 = (bf16[64,1664]{1,0:T(8,128)(2,1)S(1)}, bf16[64,1664]{1,0:T(8,128)(2,1)S(1)}, u32[]{:S(2)}, u32[]{:S(2)}) collective-permute-start(bf16[64,1664]{1,0:T(8,128)(2,1)S(1)} %get-tuple-element.201), channel_id=1, source_target_pairs={{0,8},{2,10},{4,12},{6,14},{8,16},{10,18},{12,20},{14,22},{16,24},... | collective-permute-start | bytes 638984 | tf_op jit(solution)/shard_map/ppermute | solution.py:415
  21.9 23.6 %collective-permute-start.3 = (bf16[64,1664]{1,0:T(8,128)(2,1)S(1)}, bf16[64,1664]{1,0:T(8,128)(2,1)S(1)}, u32[]{:S(2)}, u32[]{:S(2)}) collective-permute-start(bf16[64,1664]{1,0:T(8,128)(2,1)S(1)} %get-tuple-element.201), channel_id=1, source_target_pairs={{0,24},{2,26},{4,28},{6,30},{8,0},{10,2},{12,4},{14,6},{16,8},{18,... | collective-permute-start | bytes 638984 | tf_op jit(solution)/shard_map/ppermute | solution.py:415
  46.7 8.7 %collective-permute-start.4 = (bf16[4,32,1664]{2,1,0:T(8,128)(2,1)}, bf16[4,32,1664]{2,1,0:T(8,128)(2,1)}, u32[]{:S(2)}, u32[]{:S(2)}) collective-permute-start(bf16[4,32,1664]{2,1,0:T(8,128)(2,1)} %get-tuple-element.196), channel_id=1, source_target_pairs={{0,4},{2,6},{4,0},{6,2},{8,12},{10,14},{12,8},{14,10},{16,20},{18,... | collective-permute-start | bytes 1277960 | tf_op jit(solution)/shard_map/ppermute | solution.py:410
  48.2 15.7 %collective-permute-start.6 = (bf16[4,32,1664]{2,1,0:T(8,128)(2,1)}, bf16[4,32,1664]{2,1,0:T(8,128)(2,1)S(1)}, u32[]{:S(2)}, u32[]{:S(2)}) collective-permute-start(bf16[4,32,1664]{2,1,0:T(8,128)(2,1)} %get-tuple-element.195), channel_id=1, source_target_pairs={{0,1},{1,0},{2,3},{3,2},{4,5},{5,4},{6,7},{7,6},{8,9},{9,8},{10,11... | collective-permute-start | bytes 1277960 | tf_op jit(solution)/shard_map/ppermute | solution.py:410
  54.9 41.7 %collective-permute-start = (bf16[2,320,1024]{2,1,0:T(8,128)(2,1)}, bf16[2,320,1024]{2,1,0:T(8,128)(2,1)}, u32[]{:S(2)}, u32[]{:S(2)}) collective-permute-start(bf16[2,320,1024]{2,1,0:T(8,128)(2,1)} %bitcast.242), channel_id=1, source_target_pairs={{0,1},{1,0},{2,3},{3,2},{4,5},{5,4},{6,7},{7,6},{8,9},{9,8},{10,11... | collective-permute-start | bytes 3932168 | tf_op jit(solution)/shard_map/ppermute | solution.py:593
  56.5 63.4 %collective-permute-start.5 = (bf16[2,4,32,1664]{3,2,1,0:T(8,128)(2,1)S(1)}, bf16[2,4,32,1664]{3,2,1,0:T(8,128)(2,1)S(1)}, u32[]{:S(2)}, u32[]{:S(2)}) collective-permute-start(bf16[2,4,32,1664]{3,2,1,0:T(8,128)(2,1)S(1)} %pad_maximum_fusion.1.refs_0_), channel_id=1, source_target_pairs={{0,1},{1,0},{2,3},{3,2},{4,5},{5,4},{6,7},{7,6},{8,9},{9,8},{10,11... | collective-permute-start | bytes 2555912 | tf_op jit(solution)/shard_map/ppermute | solution.py:410
  64.0 56.0 %collective-permute-start.7 = (bf16[2,4,32,1664]{3,2,1,0:T(8,128)(2,1)S(1)}, bf16[2,4,32,1664]{3,2,1,0:T(8,128)(2,1)S(1)}, u32[]{:S(2)}, u32[]{:S(2)}) collective-permute-start(bf16[2,4,32,1664]{3,2,1,0:T(8,128)(2,1)S(1)} %pad_maximum_fusion.2.refs_2_), channel_id=1, source_target_pairs={{0,4},{2,6},{4,0},{6,2},{8,12},{10,14},{12,8},{14,10},{16,20},{18,... | collective-permute-start | bytes 2555912 | tf_op jit(solution)/shard_map/ppermute | solution.py:410
  66.8 55.0 %collective-permute-start.8 = (bf16[2,4,32,1664]{3,2,1,0:T(8,128)(2,1)S(1)}, bf16[2,4,32,1664]{3,2,1,0:T(8,128)(2,1)S(1)}, u32[]{:S(2)}, u32[]{:S(2)}) collective-permute-start(bf16[2,4,32,1664]{3,2,1,0:T(8,128)(2,1)S(1)} %pad_maximum_fusion.1.refs_0_), channel_id=1, source_target_pairs={{0,2},{2,0},{4,6},{6,4},{8,10},{10,8},{12,14},{14,12},{16,18},{18,... | collective-permute-start | bytes 2555912 | tf_op jit(solution)/shard_map/ppermute | solution.py:410
  66.9 55.0 %collective-permute-start.10 = (bf16[2,4,32,1664]{3,2,1,0:T(8,128)(2,1)S(1)}, bf16[2,4,32,1664]{3,2,1,0:T(8,128)(2,1)S(1)}, u32[]{:S(2)}, u32[]{:S(2)}) collective-permute-start(bf16[2,4,32,1664]{3,2,1,0:T(8,128)(2,1)S(1)} %pad_maximum_fusion.2.refs_2_), channel_id=1, source_target_pairs={{0,2},{2,0},{4,6},{6,4},{8,10},{10,8},{12,14},{14,12},{16,18},{18,... | collective-permute-start | bytes 2555912 | tf_op jit(solution)/shard_map/ppermute | solution.py:410
  152.8 38.4 %collective-permute-start.12 = (bf16[2,320,1024]{2,1,0:T(8,128)(2,1)}, bf16[2,320,1024]{2,1,0:T(8,128)(2,1)}, u32[]{:S(2)}, u32[]{:S(2)}) collective-permute-start(bf16[2,320,1024]{2,1,0:T(8,128)(2,1)} %dynamic-slice_bitcast_fusion), channel_id=1, source_target_pairs={{0,1},{1,0},{2,3},{3,2},{4,5},{5,4},{6,7},{7,6},{8,9},{9,8},{10,11... | collective-permute-start | bytes 3932168 | tf_op jit(solution)/shard_map/ppermute | solution.py:593
  264.2 37.1 %collective-permute-start.13 = (bf16[4,2,64,4096]{3,2,0,1:T(8,128)(2,1)}, bf16[4,2,64,4096]{3,2,0,1:T(8,128)(2,1)}, u32[]{:S(2)}, u32[]{:S(2)}) collective-permute-start(bf16[4,2,64,4096]{3,2,0,1:T(8,128)(2,1)} %fusion.28), channel_id=1, source_target_pairs={{0,2},{2,0},{4,6},{6,4},{8,10},{10,8},{12,14},{14,12},{16,18},{18,... | collective-permute-start | bytes 12582920 | tf_op jit(solution)/shard_map/ppermute | solution.py:410
  313.1 25.7 %collective-permute-start.14 = (bf16[4,2,32,2048]{3,2,0,1:T(8,128)(2,1)S(1)}, bf16[4,2,32,2048]{3,2,0,1:T(8,128)(2,1)}, u32[]{:S(2)}, u32[]{:S(2)}) collective-permute-start(bf16[4,2,32,2048]{3,2,0,1:T(8,128)(2,1)S(1)} %dynamic-slice_convert_fusion.9), channel_id=1, source_target_pairs={{0,1},{1,0},{2,3},{3,2},{4,5},{5,4},{6,7},{7,6},{8,9},{9,8},{10,11... | collective-permute-start | bytes 3145736 | tf_op jit(solution)/shard_map/ppermute | solution.py:410
  313.5 27.0 %collective-permute-start.15 = (bf16[4,32,4096]{2,1,0:T(8,128)(2,1)S(1)}, bf16[4,32,4096]{2,1,0:T(8,128)(2,1)S(1)}, u32[]{:S(2)}, u32[]{:S(2)}) collective-permute-start(bf16[4,32,4096]{2,1,0:T(8,128)(2,1)S(1)} %fusion.41), channel_id=1, source_target_pairs={{0,4},{2,6},{4,0},{6,2},{8,12},{10,14},{12,8},{14,10},{16,20},{18,... | collective-permute-start | bytes 3145736 | tf_op jit(solution)/shard_map/ppermute | solution.py:410
  347.6 20.4 %collective-permute-start.18 = (bf16[4,2,64,4096]{3,2,0,1:T(8,128)(2,1)}, bf16[4,2,64,4096]{3,2,0,1:T(8,128)(2,1)}, u32[]{:S(2)}, u32[]{:S(2)}) collective-permute-start(bf16[4,2,64,4096]{3,2,0,1:T(8,128)(2,1)} %fusion.29), channel_id=1, source_target_pairs={{0,2},{2,0},{4,6},{6,4},{8,10},{10,8},{12,14},{14,12},{16,18},{18,... | collective-permute-start | bytes 12582920 | tf_op jit(solution)/shard_map/ppermute | solution.py:410
  347.7 17.1 %collective-permute-start.17 = (bf16[4,32,2048]{2,1,0:T(8,128)(2,1)S(1)}, bf16[4,32,2048]{2,1,0:T(8,128)(2,1)S(1)}, u32[]{:S(2)}, u32[]{:S(2)}) collective-permute-start(bf16[4,32,2048]{2,1,0:T(8,128)(2,1)S(1)} %dynamic-slice_convert_fusion.14), channel_id=1, source_target_pairs={{0,1},{1,0},{2,3},{3,2},{4,5},{5,4},{6,7},{7,6},{8,9},{9,8},{10,11... | collective-permute-start | bytes 1572872 | tf_op jit(solution)/shard_map/ppermute | solution.py:410
  349.1 17.8 %collective-permute-start.16 = (bf16[4,32,2048]{2,1,0:T(8,128)(2,1)S(1)}, bf16[4,32,2048]{2,1,0:T(8,128)(2,1)S(1)}, u32[]{:S(2)}, u32[]{:S(2)}) collective-permute-start(bf16[4,32,2048]{2,1,0:T(8,128)(2,1)S(1)} %fusion.45), channel_id=1, source_target_pairs={{0,4},{2,6},{4,0},{6,2},{8,12},{10,14},{12,8},{14,10},{16,20},{18,... | collective-permute-start | bytes 1572872 | tf_op jit(solution)/shard_map/ppermute | solution.py:410
  381.6 47.7 %collective-permute-start.19 = (bf16[64,2048]{1,0:T(8,128)(2,1)}, bf16[64,2048]{1,0:T(8,128)(2,1)}, u32[]{:S(2)}, u32[]{:S(2)}) collective-permute-start(bf16[64,2048]{1,0:T(8,128)(2,1)} %get-tuple-element.187), channel_id=1, source_target_pairs={{0,8},{2,10},{4,12},{6,14},{8,16},{10,18},{12,20},{14,22},{16,24},... | collective-permute-start | bytes 786440 | tf_op jit(solution)/shard_map/ppermute | solution.py:415
  397.1 32.1 %collective-permute-start.21 = (bf16[64,2048]{1,0:T(8,128)(2,1)}, bf16[64,2048]{1,0:T(8,128)(2,1)}, u32[]{:S(2)}, u32[]{:S(2)}) collective-permute-start(bf16[64,2048]{1,0:T(8,128)(2,1)} %get-tuple-element.188), channel_id=1, source_target_pairs={{0,24},{2,26},{4,28},{6,30},{8,0},{10,2},{12,4},{14,6},{16,8},{18,... | collective-permute-start | bytes 786440 | tf_op jit(solution)/shard_map/ppermute | solution.py:415
  397.1 32.1 %collective-permute-start.20 = (bf16[64,2048]{1,0:T(8,128)(2,1)S(1)}, bf16[64,2048]{1,0:T(8,128)(2,1)}, u32[]{:S(2)}, u32[]{:S(2)}) collective-permute-start(bf16[64,2048]{1,0:T(8,128)(2,1)S(1)} %get-tuple-element.189), channel_id=1, source_target_pairs={{0,16},{2,18},{4,20},{6,22},{8,24},{10,26},{12,28},{14,30},{16,0},... | collective-permute-start | bytes 786440 | tf_op jit(solution)/shard_map/ppermute | solution.py:415
  421.9 24.3 %collective-permute-start.22 = (bf16[4,2,32,2048]{3,2,0,1:T(8,128)(2,1)S(1)}, bf16[4,2,32,2048]{3,2,0,1:T(8,128)(2,1)}, u32[]{:S(2)}, u32[]{:S(2)}) collective-permute-start(bf16[4,2,32,2048]{3,2,0,1:T(8,128)(2,1)S(1)} %dynamic-slice_convert_fusion.7), channel_id=1, source_target_pairs={{0,1},{1,0},{2,3},{3,2},{4,5},{5,4},{6,7},{7,6},{8,9},{9,8},{10,11... | collective-permute-start | bytes 3145736 | tf_op jit(solution)/shard_map/ppermute | solution.py:410
  422.3 26.2 %collective-permute-start.23 = (bf16[4,32,4096]{2,1,0:T(8,128)(2,1)S(1)}, bf16[4,32,4096]{2,1,0:T(8,128)(2,1)S(1)}, u32[]{:S(2)}, u32[]{:S(2)}) collective-permute-start(bf16[4,32,4096]{2,1,0:T(8,128)(2,1)S(1)} %fusion.42), channel_id=1, source_target_pairs={{0,4},{2,6},{4,0},{6,2},{8,12},{10,14},{12,8},{14,10},{16,20},{18,... | collective-permute-start | bytes 3145736 | tf_op jit(solution)/shard_map/ppermute | solution.py:410
  449.0 51.2 %collective-permute-start.24 = (bf16[4,32,2048]{2,1,0:T(8,128)(2,1)S(1)}, bf16[4,32,2048]{2,1,0:T(8,128)(2,1)S(1)}, u32[]{:S(2)}, u32[]{:S(2)}) collective-permute-start(bf16[4,32,2048]{2,1,0:T(8,128)(2,1)S(1)} %fusion.46), channel_id=1, source_target_pairs={{0,4},{2,6},{4,0},{6,2},{8,12},{10,14},{12,8},{14,10},{16,20},{18,... | collective-permute-start | bytes 1572872 | tf_op jit(solution)/shard_map/ppermute | solution.py:410
  449.4 50.9 %collective-permute-start.25 = (bf16[4,32,2048]{2,1,0:T(8,128)(2,1)S(1)}, bf16[4,32,2048]{2,1,0:T(8,128)(2,1)S(1)}, u32[]{:S(2)}, u32[]{:S(2)}) collective-permute-start(bf16[4,32,2048]{2,1,0:T(8,128)(2,1)S(1)} %dynamic-slice_convert_fusion.12), channel_id=1, source_target_pairs={{0,1},{1,0},{2,3},{3,2},{4,5},{5,4},{6,7},{7,6},{8,9},{9,8},{10,11... | collective-permute-start | bytes 1572872 | tf_op jit(solution)/shard_map/ppermute | solution.py:410
  451.8 48.6 %collective-permute-start.26 = (bf16[4,2,64,1024]{3,2,0,1:T(8,128)(2,1)S(1)}, bf16[4,2,64,1024]{3,2,0,1:T(8,128)(2,1)S(1)}, u32[]{:S(2)}, u32[]{:S(2)}) collective-permute-start(bf16[4,2,64,1024]{3,2,0,1:T(8,128)(2,1)S(1)} %fusion.43), channel_id=1, source_target_pairs={{0,2},{2,0},{4,6},{6,4},{8,10},{10,8},{12,14},{14,12},{16,18},{18,... | collective-permute-start | bytes 3145736 | tf_op jit(solution)/shard_map/ppermute | solution.py:410
  503.1 21.6 %collective-permute-start.27 = (bf16[64,2048]{1,0:T(8,128)(2,1)S(1)}, bf16[64,2048]{1,0:T(8,128)(2,1)}, u32[]{:S(2)}, u32[]{:S(2)}) collective-permute-start(bf16[64,2048]{1,0:T(8,128)(2,1)S(1)} %get-tuple-element.184), channel_id=1, source_target_pairs={{0,8},{2,10},{4,12},{6,14},{8,16},{10,18},{12,20},{14,22},{16,24},... | collective-permute-start | bytes 786440 | tf_op jit(solution)/shard_map/ppermute | solution.py:415
  503.4 21.3 %collective-permute-start.29 = (bf16[64,2048]{1,0:T(8,128)(2,1)S(1)}, bf16[64,2048]{1,0:T(8,128)(2,1)}, u32[]{:S(2)}, u32[]{:S(2)}) collective-permute-start(bf16[64,2048]{1,0:T(8,128)(2,1)S(1)} %get-tuple-element.185), channel_id=1, source_target_pairs={{0,24},{2,26},{4,28},{6,30},{8,0},{10,2},{12,4},{14,6},{16,8},{18,... | collective-permute-start | bytes 786440 | tf_op jit(solution)/shard_map/ppermute | solution.py:415
  507.1 22.1 %collective-permute-start.28 = (bf16[64,2048]{1,0:T(8,128)(2,1)S(1)}, bf16[64,2048]{1,0:T(8,128)(2,1)}, u32[]{:S(2)}, u32[]{:S(2)}) collective-permute-start(bf16[64,2048]{1,0:T(8,128)(2,1)S(1)} %get-tuple-element.186), channel_id=1, source_target_pairs={{0,16},{2,18},{4,20},{6,22},{8,24},{10,26},{12,28},{14,30},{16,0},... | collective-permute-start | bytes 786440 | tf_op jit(solution)/shard_map/ppermute | solution.py:415
  508.7 15.9 %collective-permute-start.30 = (bf16[4,2,32,512]{3,2,0,1:T(8,128)(2,1)}, bf16[4,2,32,512]{3,2,0,1:T(8,128)(2,1)S(1)}, u32[]{:S(2)}, u32[]{:S(2)}) collective-permute-start(bf16[4,2,32,512]{3,2,0,1:T(8,128)(2,1)} %dynamic-slice_convert_fusion.19), channel_id=1, source_target_pairs={{0,1},{1,0},{2,3},{3,2},{4,5},{5,4},{6,7},{7,6},{8,9},{9,8},{10,11... | collective-permute-start | bytes 786440 | tf_op jit(solution)/shard_map/ppermute | solution.py:410
  510.0 12.0 %collective-permute-start.31 = (bf16[4,32,1024]{2,1,0:T(8,128)(2,1)}, bf16[4,32,1024]{2,1,0:T(8,128)(2,1)}, u32[]{:S(2)}, u32[]{:S(2)}) collective-permute-start(bf16[4,32,1024]{2,1,0:T(8,128)(2,1)} %fusion.69), channel_id=1, source_target_pairs={{0,4},{2,6},{4,0},{6,2},{8,12},{10,14},{12,8},{14,10},{16,20},{18,... | collective-permute-start | bytes 786440 | tf_op jit(solution)/shard_map/ppermute | solution.py:410
  532.1 19.7 %collective-permute-start.32 = (bf16[4,32,512]{2,1,0:T(8,128)(2,1)}, bf16[4,32,512]{2,1,0:T(8,128)(2,1)}, u32[]{:S(2)}, u32[]{:S(2)}) collective-permute-start(bf16[4,32,512]{2,1,0:T(8,128)(2,1)} %fusion.73), channel_id=1, source_target_pairs={{0,4},{2,6},{4,0},{6,2},{8,12},{10,14},{12,8},{14,10},{16,20},{18,... | collective-permute-start | bytes 393224 | tf_op jit(solution)/shard_map/ppermute | solution.py:410
  533.9 24.0 %collective-permute-start.34 = (bf16[4,2,64,3072]{3,2,0,1:T(8,128)(2,1)S(1)}, bf16[4,2,64,3072]{3,2,0,1:T(8,128)(2,1)}, u32[]{:S(2)}, u32[]{:S(2)}) collective-permute-start(bf16[4,2,64,3072]{3,2,0,1:T(8,128)(2,1)S(1)} %fusion.30), channel_id=1, source_target_pairs={{0,2},{2,0},{4,6},{6,4},{8,10},{10,8},{12,14},{14,12},{16,18},{18,... | collective-permute-start | bytes 9437192 | tf_op jit(solution)/shard_map/ppermute | solution.py:410
  578.1 17.0 %collective-permute-start.36 = (bf16[64,512]{1,0:T(8,128)(2,1)}, bf16[64,512]{1,0:T(8,128)(2,1)S(1)}, u32[]{:S(2)}, u32[]{:S(2)}) collective-permute-start(bf16[64,512]{1,0:T(8,128)(2,1)} %get-tuple-element.197), channel_id=1, source_target_pairs={{0,8},{2,10},{4,12},{6,14},{8,16},{10,18},{12,20},{14,22},{16,24},... | collective-permute-start | bytes 196616 | tf_op jit(solution)/shard_map/ppermute | solution.py:415
  578.1 17.0 %collective-permute-start.38 = (bf16[64,512]{1,0:T(8,128)(2,1)}, bf16[64,512]{1,0:T(8,128)(2,1)}, u32[]{:S(2)}, u32[]{:S(2)}) collective-permute-start(bf16[64,512]{1,0:T(8,128)(2,1)} %get-tuple-element.198), channel_id=1, source_target_pairs={{0,24},{2,26},{4,28},{6,30},{8,0},{10,2},{12,4},{14,6},{16,8},{18,... | collective-permute-start | bytes 196616 | tf_op jit(solution)/shard_map/ppermute | solution.py:415
  581.9 13.2 %collective-permute-start.37 = (bf16[64,512]{1,0:T(8,128)(2,1)}, bf16[64,512]{1,0:T(8,128)(2,1)}, u32[]{:S(2)}, u32[]{:S(2)}) collective-permute-start(bf16[64,512]{1,0:T(8,128)(2,1)} %get-tuple-element.199), channel_id=1, source_target_pairs={{0,16},{2,18},{4,20},{6,22},{8,24},{10,26},{12,28},{14,30},{16,0},... | collective-permute-start | bytes 196616 | tf_op jit(solution)/shard_map/ppermute | solution.py:415
  588.1 18.9 %collective-permute-start.40 = (bf16[4,32,3072]{2,1,0:T(8,128)(2,1)}, bf16[4,32,3072]{2,1,0:T(8,128)(2,1)}, u32[]{:S(2)}, u32[]{:S(2)}) collective-permute-start(bf16[4,32,3072]{2,1,0:T(8,128)(2,1)} %fusion.44), channel_id=1, source_target_pairs={{0,4},{2,6},{4,0},{6,2},{8,12},{10,14},{12,8},{14,10},{16,20},{18,... | collective-permute-start | bytes 2359304 | tf_op jit(solution)/shard_map/ppermute | solution.py:410
  593.4 18.6 %collective-permute-start.39 = (bf16[4,2,32,1536]{3,2,0,1:T(8,128)(2,1)S(1)}, bf16[4,2,32,1536]{3,2,0,1:T(8,128)(2,1)S(1)}, u32[]{:S(2)}, u32[]{:S(2)}) collective-permute-start(bf16[4,2,32,1536]{3,2,0,1:T(8,128)(2,1)S(1)} %dynamic-slice_convert_fusion.11), channel_id=1, source_target_pairs={{0,1},{1,0},{2,3},{3,2},{4,5},{5,4},{6,7},{7,6},{8,9},{9,8},{10,11... | collective-permute-start | bytes 2359304 | tf_op jit(solution)/shard_map/ppermute | solution.py:410
  619.6 10.3 %collective-permute-start.42 = (f32[4,2,2,384]{3,2,1,0:T(2,128)S(1)}, f32[4,2,2,384]{3,2,1,0:T(2,128)S(1)}, u32[]{:S(2)}, u32[]{:S(2)}) collective-permute-start(f32[4,2,2,384]{3,2,1,0:T(2,128)S(1)} %dynamic-slice_bitcast_fusion.1), channel_id=1, source_target_pairs={{0,2},{2,0},{4,6},{6,4},{8,10},{10,8},{12,14},{14,12},{16,18},{18,... | collective-permute-start | bytes 73736 | tf_op jit(solution)/shard_map/ppermute | solution.py:410
  622.8 27.4 %collective-permute-start.51 = (bf16[4,32,1536]{2,1,0:T(8,128)(2,1)}, bf16[4,32,1536]{2,1,0:T(8,128)(2,1)}, u32[]{:S(2)}, u32[]{:S(2)}) collective-permute-start(bf16[4,32,1536]{2,1,0:T(8,128)(2,1)} %dynamic-slice_convert_fusion.16), channel_id=1, source_target_pairs={{0,1},{1,0},{2,3},{3,2},{4,5},{5,4},{6,7},{7,6},{8,9},{9,8},{10,11... | collective-permute-start | bytes 1179656 | tf_op jit(solution)/shard_map/ppermute | solution.py:410
  624.5 26.8 %collective-permute-start.50 = (bf16[4,32,1536]{2,1,0:T(8,128)(2,1)S(1)}, bf16[4,32,1536]{2,1,0:T(8,128)(2,1)}, u32[]{:S(2)}, u32[]{:S(2)}) collective-permute-start(bf16[4,32,1536]{2,1,0:T(8,128)(2,1)S(1)} %fusion.51), channel_id=1, source_target_pairs={{0,4},{2,6},{4,0},{6,2},{8,12},{10,14},{12,8},{14,10},{16,20},{18,... | collective-permute-start | bytes 1179656 | tf_op jit(solution)/shard_map/ppermute | solution.py:410
  640.3 9.1 %collective-permute-start.48 = (f32[2,192]{1,0:T(2,128)S(1)}, f32[2,192]{1,0:T(2,128)S(1)}, u32[]{:S(2)}, u32[]{:S(2)}) collective-permute-start(f32[2,192]{1,0:T(2,128)S(1)} %get-tuple-element.213), channel_id=1, source_target_pairs={{0,16},{2,18},{4,20},{6,22},{8,24},{10,26},{12,28},{14,30},{16,0},... | collective-permute-start | bytes 4616 | tf_op jit(solution)/shard_map/ppermute | solution.py:415
  641.5 8.6 %collective-permute-start.49 = (f32[2,192]{1,0:T(2,128)S(1)}, f32[2,192]{1,0:T(2,128)S(1)}, u32[]{:S(2)}, u32[]{:S(2)}) collective-permute-start(f32[2,192]{1,0:T(2,128)S(1)} %get-tuple-element.214), channel_id=1, source_target_pairs={{0,24},{2,26},{4,28},{6,30},{8,0},{10,2},{12,4},{14,6},{16,8},{18,... | collective-permute-start | bytes 4616 | tf_op jit(solution)/shard_map/ppermute | solution.py:415
  648.0 32.0 %collective-permute-start.41 = (bf16[2,320,1024]{2,1,0:T(8,128)(2,1)}, bf16[2,320,1024]{2,1,0:T(8,128)(2,1)}, u32[]{:S(2)}, u32[]{:S(2)}) collective-permute-start(bf16[2,320,1024]{2,1,0:T(8,128)(2,1)} %get-tuple-element.227), channel_id=1, source_target_pairs={{0,1},{1,0},{2,3},{3,2},{4,5},{5,4},{6,7},{7,6},{8,9},{9,8},{10,11... | collective-permute-start | bytes 3932168 | tf_op jit(solution)/shard_map/ppermute | solution.py:604
  649.4 55.0 %collective-permute-start.35 = (bf16[2,320,1024]{2,1,0:T(8,128)(2,1)}, bf16[2,320,1024]{2,1,0:T(8,128)(2,1)}, u32[]{:S(2)}, u32[]{:S(2)}) collective-permute-start(bf16[2,320,1024]{2,1,0:T(8,128)(2,1)} %get-tuple-element.228), channel_id=1, source_target_pairs={{0,1},{1,0},{2,3},{3,2},{4,5},{5,4},{6,7},{7,6},{8,9},{9,8},{10,11... | collective-permute-start | bytes 3932168 | tf_op jit(solution)/shard_map/ppermute | solution.py:604
  652.4 9.7 %collective-permute-start.52 = (bf16[64,1536]{1,0:T(8,128)(2,1)S(1)}, bf16[64,1536]{1,0:T(8,128)(2,1)S(1)}, u32[]{:S(2)}, u32[]{:S(2)}) collective-permute-start(bf16[64,1536]{1,0:T(8,128)(2,1)S(1)} %get-tuple-element.190), channel_id=1, source_target_pairs={{0,8},{2,10},{4,12},{6,14},{8,16},{10,18},{12,20},{14,22},{16,24},... | collective-permute-start | bytes 589832 | tf_op jit(solution)/shard_map/ppermute | solution.py:415
  652.9 13.8 %collective-permute-start.53 = (bf16[64,1536]{1,0:T(8,128)(2,1)S(1)}, bf16[64,1536]{1,0:T(8,128)(2,1)S(1)}, u32[]{:S(2)}, u32[]{:S(2)}) collective-permute-start(bf16[64,1536]{1,0:T(8,128)(2,1)S(1)} %get-tuple-element.191), channel_id=1, source_target_pairs={{0,16},{2,18},{4,20},{6,22},{8,24},{10,26},{12,28},{14,30},{16,0},... | collective-permute-start | bytes 589832 | tf_op jit(solution)/shard_map/ppermute | solution.py:415
  654.4 12.2 %collective-permute-start.54 = (bf16[64,1536]{1,0:T(8,128)(2,1)S(1)}, bf16[64,1536]{1,0:T(8,128)(2,1)S(1)}, u32[]{:S(2)}, u32[]{:S(2)}) collective-permute-start(bf16[64,1536]{1,0:T(8,128)(2,1)S(1)} %get-tuple-element.192), channel_id=1, source_target_pairs={{0,24},{2,26},{4,28},{6,30},{8,0},{10,2},{12,4},{14,6},{16,8},{18,... | collective-permute-start | bytes 589832 | tf_op jit(solution)/shard_map/ppermute | solution.py:415
  (95 other events, 1082.3 us)
Sparse Core Ops, SparseCore 0:
  10.9 165.6 all-gather.1

commit v3 on v2

--- a/solution.py
+++ b/solution.py
@@ -457,7 +457,7 @@
         copy.wait()
 
 
-def gather_staged(shard, vector, coords):
+def gather_staged(shard, vector, coords, beside_first, after):
     rows, columns = shard.shape
     groups = lax.axis_size("dp") // 4
     entries = vector.shape[0]
@@ -465,6 +465,7 @@
     beside = jnp.zeros((rows * 128,), BF16).at[:entries].set(vector).reshape(rows, 128)
     shard = jnp.concatenate([shard, beside], axis=1)
     line = jnp.stack([shard] + [shift(shard, groups, by) for by in range(1, groups)])
+    line, beside_first, after = lax.optimization_barrier((line, beside_first, after))
     upper, lower = line[:, : rows // 2], line[:, rows // 2 :]
     upper = jnp.stack([upper, swap(upper, "dp", 2)])
     lower = jnp.stack([lower, swap(lower, "tensor", 1)])
@@ -491,33 +492,23 @@
         name="assemble",
     )(coords, *mine, *theirs)
     extra = extra.reshape(2, 4 * groups, tail * 128)[:, :, :entries]
-    return whole.reshape(4 * groups * rows, 2 * columns), extra
-
-
-def beside_kernel(source, out_ref, sems, *, offset, columns):
-    copies = [
-        pltpu.make_async_copy(
-            source.at[t, :, pl.ds(offset, columns)],
-            out_ref.at[:, pl.ds(t * columns, columns)],
-            sems.at[t],
-        )
-        for t in range(2)
-    ]
-    for copy in copies:
-        copy.start()
-    for copy in copies:
-        copy.wait()
+    return whole.reshape(4 * groups * rows, 2 * columns), extra, beside_first, after
+
+
+def beside_kernel(source, out_ref):
+    out_ref[...] = source[0]
 
 
 def beside(gathered, offset, columns):
     rows = gathered.shape[1]
+    wide = min(columns, 512)
     return pl.pallas_call(
-        functools.partial(beside_kernel, offset=offset, columns=columns),
+        beside_kernel,
         out_shape=jax.ShapeDtypeStruct((rows, 2 * columns), BF16),
-        in_specs=[pl.BlockSpec(memory_space=pl.ANY)],
-        out_specs=pl.BlockSpec(memory_space=pltpu.VMEM),
-        scratch_shapes=[pltpu.SemaphoreType.DMA((2,))],
-        compiler_params=pltpu.CompilerParams(vmem_limit_bytes=(4 << 20) + 4 * rows * columns),
+        grid=(2, columns // wide),
+        in_specs=[pl.BlockSpec((1, rows, wide), lambda t, n: (t, 0, offset // wide + n))],
+        out_specs=pl.BlockSpec((rows, wide), lambda t, n: (0, t * (columns // wide) + n)),
+        compiler_params=pltpu.CompilerParams(vmem_limit_bytes=(4 << 20) + 8 * rows * wide),
         cost_estimate=pl.CostEstimate(flops=0, transcendentals=0, bytes_accessed=8 * rows * columns),
         name="beside",
     )(gathered)
@@ -542,10 +533,12 @@
         self.stage = 0
 
     def over_tensor(self, array):
-        return side(array, self.t) + swap(side(array, 1 - self.t).astype(self.sent), "tensor", 1).astype(F32)
+        came = swap(side(array, 1 - self.t).astype(self.sent), "tensor", 1).astype(F32)
+        return (side(array, self.t).astype(F32) + came).astype(self.sent)
 
     def over_pair(self, array, mine, dim, step):
-        return take(array, mine, dim) + swap(take(array, 1 - mine, dim).astype(self.sent), "dp", step).astype(F32)
+        came = swap(take(array, 1 - mine, dim).astype(self.sent), "dp", step).astype(F32)
+        return (take(array, mine, dim).astype(F32) + came).astype(self.sent)
 
     def step(self):
         half = self.rows // 2
@@ -562,7 +555,7 @@
             self.state = [self.over_pair(upper, self.x, 1, 2), self.over_tensor(lower)]
         elif self.stage == 3:
             line = jnp.concatenate(self.state, axis=1)
-            total = take(line, self.z, 0)
+            total = take(line, self.z, 0).astype(F32)
             for by in range(1, self.groups):
                 sent = take(line, lax.rem(self.z + by, self.groups), 0).astype(self.sent)
                 total = total + shift(sent, self.groups, by).astype(F32)
@@ -585,23 +578,30 @@
     return values if len(values) > 1 else values[0]
 
 
-def to_images(rows):
+def to_images(rows, after=()):
     me = lax.axis_index("tensor")
     own, part = rows.shape[0] // 2, rows.shape[1]
     kept = lax.dynamic_slice_in_dim(rows, me * own, own, 0)
     sent = lax.dynamic_slice_in_dim(rows, (1 - me) * own, own, 0)
+    sent, after = lax.optimization_barrier((sent, after))
     came = lax.ppermute(sent, "tensor", [(0, 1), (1, 0)])
     whole = jnp.zeros((own, 2 * part) + rows.shape[2:], rows.dtype)
     whole = lax.dynamic_update_slice_in_dim(whole, kept, me * part, 1)
-    return lax.dynamic_update_slice_in_dim(whole, came, (1 - me) * part, 1)
-
-
-def to_slots(rows):
+    return lax.dynamic_update_slice_in_dim(whole, came, (1 - me) * part, 1), after
+
+
+def split_slots(rows, slots):
     me = lax.axis_index("tensor")
-    own, part = rows.shape[0], rows.shape[1] // 2
+    part = slots // 2
+    rows = jnp.pad(rows, ((0, 0), (0, slots - rows.shape[1]), (0, 0)))
     kept = lax.dynamic_slice_in_dim(rows, me * part, part, 1)
     sent = lax.dynamic_slice_in_dim(rows, (1 - me) * part, part, 1).astype(BF16)
-    came = lax.ppermute(sent, "tensor", [(0, 1), (1, 0)]).astype(rows.dtype)
+    return kept, sent[:, : part // 2], sent[:, part // 2 :]
+
+
+def join_slots(kept, *came):
+    me = lax.axis_index("tensor")
+    came = jnp.concatenate(came, axis=1).astype(kept.dtype)
     first = jnp.where(me == 0, kept, came)
     second = jnp.where(me == 0, came, kept)
     return jnp.swapaxes(jnp.concatenate([first, second], axis=0), 0, 1)
@@ -650,6 +650,8 @@
     cotangent,
 ):
     width = inputs.shape[2]
+    slots = pad_mask.shape[1]
+    used = key_count(slots)
     me = lax.axis_index("tensor")
     images = inputs.shape[1] // 2
     head_width = qkv_weight.shape[2]
@@ -660,7 +662,7 @@
     coords = place()
     product = functools.partial(jnp.einsum, preferred_element_type=F32)
 
-    x = to_images(jnp.swapaxes(inputs, 0, 1)).astype(F32)
+    x, (qkv_weight,) = to_images(jnp.swapaxes(inputs, 0, 1), (qkv_weight,))
     vector = jnp.concatenate(
         [
             v.reshape(-1)
@@ -668,7 +670,10 @@
         ]
     )
     paired = jnp.swapaxes(qkv_weight.reshape(depth, 3, pairs, PAIR), 1, 2).reshape(depth, -1)
-    qkv_full, flat = gather_staged(paired, vector, coords)
+    qkv_full, flat, x, (out_weight, up_weight, down_weight) = gather_staged(
+        paired, vector, coords, x, (out_weight, up_weight, down_weight)
+    )
+    x = x[:, :used].astype(F32)
     flat = flat.astype(F32)
     gain_one, shift_one, out_shift, gain_two, shift_two, down_shift = [
         flat[:, :, n * piece : (n + 1) * piece].reshape(width) for n in range(6)
@@ -678,23 +683,23 @@
     qkv_bias = jnp.stack([query_bias, jnp.zeros_like(query_bias), value_bias], axis=1).reshape(-1)
     up_row = flat[:, :, 8 * piece :].reshape(2 * hidden)
 
-    others = jnp.concatenate([jnp.transpose(out_weight), up_weight, jnp.transpose(down_weight)], axis=1)
+    others = jnp.concatenate([jnp.transpose(out_weight), up_weight], axis=1)
     others = lax.all_gather(others, ("tensor", "dp"), axis=0, tiled=True).reshape(2, width, -1)
     out_full = beside(others, 0, head_width)
     up_full = beside(others, head_width, hidden)
-    down_full = beside(others, head_width + hidden, hidden)
+    last = lax.all_gather(jnp.transpose(down_weight), ("tensor", "dp"), axis=0, tiled=True)
 
     here = lax.dynamic_slice_in_dim(pad_mask, me * inputs.shape[0], inputs.shape[0], 1) > 0
     down_shift_grad = token_sum(cotangent * jnp.transpose(here).astype(F32)[:, :, None])
     mask = lax.dynamic_slice_in_dim(pad_mask, me * images, images, 0)
     lengths = jnp.sum(mask, axis=1).astype(jnp.int32)
-    kept = (mask > 0).astype(F32)[:, :, None]
+    kept = (mask[:, :used] > 0).astype(F32)[:, :, None]
 
     unit_one, inverse_one = normalize(x)
     normed_one = (unit_one * gain_one + shift_one).astype(BF16)
     qkv = (product("bsd,dc->bsc", normed_one, qkv_full) + qkv_bias).astype(BF16)
     cotangent, qkv = lax.optimization_barrier((cotangent, qkv))
-    cot = to_images(jnp.swapaxes(cotangent.astype(BF16), 0, 1)).astype(F32)
+    cot = to_images(jnp.swapaxes(cotangent.astype(BF16), 0, 1))[0][:, :used].astype(F32)
     attended, lse = attention_forward(lengths, qkv)
     projected = product("bsc,dc->bsd", attended, out_full)
     after_attn = x + projected + out_shift
@@ -706,7 +711,8 @@
     out_grad = out_low.astype(F32)
 
     down = Sum(product("bsd,bsf->df", out_low, act), coords)
-    (out_low,), (down.state,) = lax.optimization_barrier(((out_low,), (down.state,)))
+    out_low, last, down.state = lax.optimization_barrier((out_low, last, down.state))
+    down_full = beside(last.reshape(2, width, -1), 0, hidden)
     act_grad = product("bsd,df->bsf", out_low, down_full)
     up_grad = (act_grad * slope).astype(BF16)
     up_grad, normed_two = advance([down], up_grad, normed_two)
@@ -723,38 +729,44 @@
     proj_low = after_attn_grad.astype(BF16)
     out = Sum(product("bsd,bsc->dc", proj_low, attended), coords)
     attended_grad = product("bsd,dc->bsc", proj_low, out_full).astype(BF16)
-    down.step()
-    up.step()
-    (attended_grad, qkv), (down.state, up.state, out.state) = lax.optimization_barrier(
-        ((attended_grad, qkv), (down.state, up.state, out.state))
+    attended_grad, act = advance([down, up], attended_grad, act)
+    mlp_out = product("bsf,df->bsd", act, down_full)
+    finished = (after_attn + mlp_out + down_shift) * kept
+    (attended_grad, qkv), (finished, out.state) = lax.optimization_barrier(
+        ((attended_grad, qkv), (finished, out.state))
     )
     qkv_grad = attention_backward(lengths, qkv, lse, attended_grad)
-    qkv_grad, normed_one = advance([up, out], qkv_grad, normed_one)
+    held, near, far = split_slots(finished, slots)
+    block_output = join_slots(held, swap(near, "tensor", 1), swap(far, "tensor", 1))
+    qkv_grad, normed_one, block_output = advance([up, out], qkv_grad, normed_one, block_output)
     qkv_sum = Sum(product("bsd,bsc->dc", normed_one, qkv_grad), coords)
-    up.step()
-    out.step()
-    (qkv_grad, act), (up.state, out.state, qkv_sum.state) = lax.optimization_barrier(
-        ((qkv_grad, act), (up.state, out.state, qkv_sum.state))
-    )
-    mlp_out = product("bsf,df->bsd", act, down_full)
-    mlp_out, qkv_grad = advance([out, qkv_sum], mlp_out, qkv_grad)
-    block_output = to_slots((after_attn + mlp_out + down_shift) * kept)
+    qkv_grad = advance([up, out], qkv_grad)
     normed_one_grad = product("bsc,dc->bsd", qkv_grad, qkv_full)
     bias_sums = token_sum(qkv_grad).reshape(2 * pairs, 3, PAIR)
     normed_one_grad = advance([out, qkv_sum], normed_one_grad)
     gain_one_grad = token_sum(normed_one_grad * unit_one)
     shift_one_grad = token_sum(normed_one_grad)
     input_grad = after_attn_grad + normalize_back(normed_one_grad, unit_one, inverse_one, gain_one)
-    input_grad = to_slots(input_grad)
+    input_grad, gain_one_grad, shift_one_grad = advance(
+        [out, qkv_sum], input_grad, gain_one_grad, shift_one_grad
+    )
 
     vectors = [gain_one_grad, shift_one_grad, out_shift_grad, gain_two_grad, shift_two_grad, down_shift_grad]
     vectors += [bias_sums[:, 0], bias_sums[:, 2], up_shift_grad]
     small = jnp.concatenate([v.reshape(2, lax.axis_size("dp"), -1) for v in vectors], axis=2)
     entries = small.shape[2]
     small = jnp.swapaxes(small.reshape(2, -1, entries // 2), 0, 1).reshape(-1, entries)
-    small = Sum(small, coords, F32).result().reshape(1, entries)
+    small = Sum(small, coords, F32)
+    held, near, far = split_slots(input_grad, slots)
+    near_came = swap(near, "tensor", 1)
+    near_came, far = advance([small, qkv_sum], near_came, far)
+    far_came = swap(far, "tensor", 1)
+    far_came, near_came = advance([small, qkv_sum], far_came, near_came)
+    input_grad = join_slots(held, near_came, far_came)
+    total = qkv_sum.result()
+    small = small.result().reshape(1, entries)
     row = lambda n: small[:, n * piece : (n + 1) * piece]
-    qkv_owned = jnp.swapaxes(qkv_sum.result().reshape(depth, pairs, 3, PAIR), 1, 2)
+    qkv_owned = jnp.swapaxes(total.reshape(depth, pairs, 3, PAIR), 1, 2)
     return (
         block_output,
         input_grad,

time: 727 us -> 625 us (0.86)
  local copies, waits for them, and re-layouts: 133 us -> 94.6 us
  waiting for transfers between devices: 157 us -> 127 us
  other arithmetic: 102 us -> 75.1 us
    add x25 -> x5, other arithmetic: 46.6 us -> 0.2 us  [the longest x2 0.16 us: over_tensor(): return (side(array, self.t).astype(F32) + came).astype(self.sent)]
    ppermute x2 -> x0, waiting for transfers between devices: 27.4 us -> none  [to_slots(): came = lax.ppermute(sent, 'tensor', [(0, 1), (1, 0)]).astype(rows.dtype)]
    convert_element_type x2 -> x21, other arithmetic: 0.08 us -> 26.8 us  [the longest x12 22.1 us: over_pair(): return (take(array, mine, dim).astype(F32) + came).astype(self.sent)]
    unnamed x180 -> x161, local copies, waits for them, and re-layouts: 59.9 us -> 35.5 us
    ppermute x2, waiting for transfers between devices: 29.3 us -> 9.04 us  [to_images(): came = lax.ppermute(sent, 'tensor', [(0, 1), (1, 0)])]
    convert_element_type x12 -> x2, local copies, waits for them, and re-layouts: 14.3 us -> 2.18 us  [split_slots(): sent = lax.dynamic_slice_in_dim(rows, (1 - me) * part, part, 1).astype(BF16)]
    all_gather x0 -> x1, waiting for transfers between devices: none -> 10.5 us  [by_images(): lax.all_gather(jnp.transpose(down_weight), ('tensor', 'dp'), axis=0, tile...]
    slice x4 -> x5, local copies, waits for them, and re-layouts: 11 us -> 1.36 us  [step(): whole[:, :, half:]]
  transfers between devices with their start and end apart: 56 -> 59, of which waited for: 21 -> 23; matrix products, arithmetic and copies ran while one was open for 31% -> 32% of each run, Pallas kernels for 12% -> 14%
where the time goes in v3:
time: 625 us; the launch traced here: 618 us
  matrix products  145 us (23%)
  waiting for transfers between devices  127 us (20%)
  local copies, waits for them, and re-layouts  94.6 us (15%)
  Pallas kernels  89 us (14%)
  other arithmetic  75.1 us (12%)
  starting transfers between devices  70.6 us (11%)
  between operations  16.1 us (3%)
    ppermute x37, waiting for transfers between devices, swap(): lax.ppermute(array, axis, [(n, n ^ step) for n in range(lax.axis_size(axi...  73.9 us
    pallas_call x1, Pallas kernels, attention_backward(): pl.pallas_call(functools.partial(attention_backward_kernel, key_rows=key_...  47.7 us
    ppermute x18, starting transfers between devices, shift(): lax.ppermute(array, 'dp', [(n, (n + 4 * by) % count) for n in range(count)])  35.5 us
    unnamed x161, local copies, waits for them, and re-layouts  35.5 us
    ppermute x18, waiting for transfers between devices, shift(): lax.ppermute(array, 'dp', [(n, (n + 4 * by) % count) for n in range(count)])  33.1 us
    pallas_call x1, Pallas kernels, attention_forward(): pl.pallas_call(functools.partial(attention_forward_kernel, key_rows=key_c...  32 us
    ppermute x37, starting transfers between devices, swap(): lax.ppermute(array, axis, [(n, n ^ step) for n in range(lax.axis_size(axi...  31.9 us
    reduce_sum x6, other arithmetic, token_sum(): return jnp.sum(values.astype(F32), axis=(0, 1))  22.9 us
  transfers between devices with their start and end apart: 59, of which 23 were waited for; matrix products, arithmetic and copies ran while one was open for 32% of the time, Pallas kernels for 14%

profile of v3, /device:TPU:0, one launch (start us, length us, event | category | flops | bytes accessed | tf_op | source)
XLA Modules:
  0.0 618.1 jit_solution(3391406701708804923)
XLA Ops:
  7.3 5.3 constant_dynamic-slice_fusion.31
  26.9 7.8 %collective-permute-done.1 = bf16[64,1664]{1,0:T(8,128)(2,1)} collective-permute-done((bf16[64,1664]{1,0:T(8,128)(2,1)S(1)}, bf16[64,1664]{1,0:T(8,128)(2,1)}, u32[]{:S(2)}, u32[]{:S(2)}) %collective-permute-start.1) | collective-permute-done | bytes 213024 | tf_op jit(solution)/shard_map/ppermute | solution.py:415
  35.9 9.0 %collective-permute-done.3 = bf16[2,320,1024]{2,1,0:T(8,128)(2,1)} collective-permute-done((bf16[2,320,1024]{2,1,0:T(8,128)(2,1)S(1)}, bf16[2,320,1024]{2,1,0:T(8,128)(2,1)}, u32[]{:S(2)}, u32[]{:S(2)}) %collective-permute-start.3) | collective-permute-done | bytes 1310752 | tf_op jit(solution)/shard_map/ppermute | solution.py:587
  52.4 7.9 %collective-permute-done.6 = bf16[4,32,1664]{2,1,0:T(8,128)(2,1)S(1)} collective-permute-done((bf16[4,32,1664]{2,1,0:T(8,128)(2,1)S(1)}, bf16[4,32,1664]{2,1,0:T(8,128)(2,1)S(1)}, u32[]{:S(2)}, u32[]{:S(2)}) %collective-permute-start.6) | collective-permute-done | bytes 426016 | tf_op jit(solution)/shard_map/ppermute | solution.py:410
  65.2 19.9 %collective-permute-done.7.refs_3_ = bf16[2,4,32,1664]{3,2,1,0:T(8,128)(2,1)S(1)} collective-permute-done((bf16[2,4,32,1664]{3,2,1,0:T(8,128)(2,1)S(1)}, bf16[2,4,32,1664]{3,2,1,0:T(8,128)(2,1)S(1)}, u32[]{:S(2)}, u32[]{:S(2)}) %collective-permute-start.7) | collective-permute-done | bytes 852000 | tf_op jit(solution)/shard_map/ppermute | solution.py:410
  90.2 4.7 assemble.1
  101.4 14.1 %add_convert_fusion.q_ref.k_ref.v_ref = bf16[2,592,3072]{2,1,0:T(8,128)(2,1)} fusion(f32[3072]{0:T(1024)S(1)} %add.407, bf16[2,592,1024]{2,1,0:T(8,128)(2,1)S(1)} %fusion.23, bf16[1024,3072,1]{1,0,2:T(8,128)(2,1)} %bitcast.256), kind=kOutput, calls=%fused_computation.11 | convolution fusion | flops 7456358400 | bytes 16003072 | tf_op jit(solution)/shard_map/bsd,dc->bsc/dot_general | solution.py:700
  120.3 3.1 copy-done
  123.4 32.0 %attention_forward.1 = (bf16[2,592,1024]{2,1,0:T(8,128)(2,1)S(1)}, f32[2,8,2,592]{3,2,1,0:T(2,128)S(1)}) custom-call(s32[2]{0:T(128)S(1)} %fusion.74.lengths, bf16[2,592,3072]{2,1,0:T(8,128)(2,1)S(1)} %copy-done, bf16[2,592,3072]{2,1,0:T(8,128)(2,1)S(1)} %copy-done, bf16[2,592,3072]{2,1,0:T(8,128)(2,1)S(1)} %copy-done), custom_call_target="tpu_custom_call" | custom-call | flops 5742002176 | bytes 9699328 | tf_op jit(solution)/shard_map/attention_forward/pallas_call | solution.py:357
  161.2 4.0 copy-done.1
  167.8 6.7 %fusion.99 = (f32[2,592]{1,0:T(2,128)S(1)}, f32[2,592,1024]{2,1,0:T(8,128)S(1)}) fusion(f32[1024]{0:T(1024)S(1)} %add.411, bf16[2,592,1024]{2,1,0:T(8,128)(2,1)S(1)} %get-tuple-element.100, bf16[1024,1024]{1,0:T(8,128)(2,1)S(1)} %beside.3, bf16[2,640,1024]{2,1,0:T(8,128)(2,1)} %constant_dynamic-update-slice_fusion.1), kind=kOutput, calls=%fused_computation.252 | convolution fusion | flops 2487876352 | bytes 11805312 | tf_op jit(solution)/shard_map/bsc,dc->bsd/dot_general | solution.py:704
  176.8 15.2 %multiply_convert_fusion = (bf16[2,592,4096]{2,1,0:T(8,128)(2,1)S(1)}, f32[2,592,4096]{2,1,0:T(8,128)}) fusion(f32[4096]{0:T(1024)S(1)} %bitcast.290, bf16[2,592,1024]{2,1,0:T(8,128)(2,1)S(1)} %add_convert_fusion.1, bf16[1024,4096]{1,0:T(8,128)(2,1)S(1)} %beside.4), kind=kOutput, calls=%fused_computation.8 | convolution fusion | flops 9961209856 | bytes 39927808 | tf_op jit(solution)/shard_map/bsd,df->bsf/dot_general | solution.py:708
  192.0 3.7 copy-done.62
  195.7 14.1 %fusion.100 = f32[1024,4096,1]{1,0,2:T(8,128)} fusion(bf16[2,592,1024]{2,1,0:T(8,128)(2,1)S(1)} %copy-done.24, bf16[2,592,4096]{2,1,0:T(8,128)(2,1)S(1)} %get-tuple-element.119), kind=kOutput, calls=%fused_computation.253 | convolution fusion | flops 9932111872 | bytes 28901376 | tf_op jit(solution)/shard_map/bsd,bsf->df/dot_general | solution.py:713
  209.8 10.5 %all-gather.5.cloned.1.call-done = bf16[2048,2048]{1,0:T(8,128)(2,1)} async-done(((bf16[64,2048]{1,0:T(8,128)(2,1)}), bf16[2048,2048]{1,0:T(8,128)(2,1)}) %all-gather.5.cloned.1.call-update) | async-done | bytes 8388624 | tf_op jit(solution)/shard_map/all_gather | solution.py:690
  220.2 6.0 fusion.31
  226.7 3.6 multiply_reduce_fusion
  231.1 3.4 copy-done.2
  236.5 22.4 %fusion.5 = bf16[2,592,4096]{2,1,0:T(8,128)(2,1)} fusion(f32[2,592,4096]{2,1,0:T(8,128)} %get-tuple-element.272, bf16[2,592,1024]{2,1,0:T(8,128)(2,1)S(1)} %copy-done.24, f32[4096]{0:T(1024)S(1)} %bitcast.291, bf16[1024,4096]{1,0:T(8,128)(2,1)S(1)} %beside.5), kind=kOutput, calls=%fused_computation.6 | convolution fusion | flops 9985458176 | bytes 39927808 | tf_op jit(solution)/shard_map/bsd,df->bsf/dot_general | solution.py:716
  258.8 6.0 fusion.7
  269.3 13.7 %fusion.101 = f32[1024,4096,1]{1,0,2:T(8,128)} fusion(bf16[2,592,1024]{2,1,0:T(8,128)(2,1)S(1)} %copy-done.26, bf16[2,592,4096]{2,1,0:T(8,128)(2,1)S(1)} %copy-done.15), kind=kOutput, calls=%fused_computation.254 | convolution fusion | flops 9932111872 | bytes 28901376 | tf_op jit(solution)/shard_map/bsd,bsf->df/dot_general | solution.py:719
  283.0 7.9 %collective-permute-done.15 = bf16[4,32,4096]{2,1,0:T(8,128)(2,1)S(1)} collective-permute-done((bf16[4,32,4096]{2,1,0:T(8,128)(2,1)S(1)}, bf16[4,32,4096]{2,1,0:T(8,128)(2,1)S(1)}, u32[]{:S(2)}, u32[]{:S(2)}) %collective-permute-start.15) | collective-permute-done | bytes 1048608 | tf_op jit(solution)/shard_map/ppermute | solution.py:410
  292.6 6.2 %fusion.32 = bf16[4,2,64,4096]{3,2,0,1:T(8,128)(2,1)} fusion(s32[]{:T(128)S(6)} %select_n.187, f32[4,2,2,64,4096]{4,3,2,1,0:T(8,128)} %bitcast.272), kind=kLoop, calls=%fused_computation.65 | loop fusion | bytes 8388612 | tf_op jit(solution)/shard_map/convert_element_type | solution.py:540
  298.8 5.9 convert_reduce_fusion
  307.7 14.6 %fusion.11 = f32[2,592,1024]{2,1,0:T(8,128)} fusion(bf16[2,592,4096]{2,1,0:T(8,128)(2,1)} %fusion.5, bf16[1024,4096]{1,0:T(8,128)(2,1)S(1)} %bitcast.255), kind=kOutput, calls=%fused_computation.19 | convolution fusion | flops 9932111872 | bytes 22937600 | tf_op jit(solution)/shard_map/bsf,df->bsd/dot_general | solution.py:723
  323.7 7.0 %fusion.6 = bf16[4,2,64,4096]{3,2,0,1:T(8,128)(2,1)} fusion(bf16[4,2,64,4096]{3,2,0,1:T(8,128)(2,1)S(1)} %collective-permute-done.18, f32[4,2,2,64,4096]{4,3,2,1,0:T(8,128)} %bitcast.273, s32[]{:T(128)S(6)} %select_n.186), kind=kLoop, calls=%fused_computation.13 | loop fusion | flops 6291456 | bytes 16777220 | tf_op jit(solution)/shard_map/convert_element_type | solution.py:541
  330.7 3.8 multiply_reduce_fusion.1
  334.6 4.5 fusion.89
  339.1 4.5 fusion.52
  358.7 9.1 %collective-permute-done.20 = bf16[64,2048]{1,0:T(8,128)(2,1)} collective-permute-done((bf16[64,2048]{1,0:T(8,128)(2,1)S(1)}, bf16[64,2048]{1,0:T(8,128)(2,1)}, u32[]{:S(2)}, u32[]{:S(2)}) %collective-permute-start.20) | collective-permute-done | bytes 262176 | tf_op jit(solution)/shard_map/ppermute | solution.py:415
  372.9 6.9 %collective-permute-done.22 = bf16[4,2,32,2048]{3,2,0,1:T(8,128)(2,1)} collective-permute-done((bf16[4,2,32,2048]{3,2,0,1:T(8,128)(2,1)}, bf16[4,2,32,2048]{3,2,0,1:T(8,128)(2,1)}, u32[]{:S(2)}, u32[]{:S(2)}) %collective-permute-start.22) | collective-permute-done | bytes 1048608 | tf_op jit(solution)/shard_map/ppermute | solution.py:410
  382.5 16.0 %add_multiply_fusion.1 = f32[2,592,1024]{2,1,0:T(8,128)S(1)} fusion(f32[2,592,1024]{2,1,0:T(8,128)} %copy-done.10, f32[1024]{0:T(1024)S(1)} %add.450, f32[2,592]{1,0:T(2,128)S(1)} %copy-done.52, bf16[2,592,4096]{2,1,0:T(8,128)(2,1)} %copy-done.62, bf16[1024,4096]{1,0:T(8,128)(2,1)} %copy-done.4), kind=kOutput, calls=%fused_computation.55 | convolution fusion | flops 9935749120 | bytes 27796096 | tf_op jit(solution)/shard_map/bsf,df->bsd/dot_general | solution.py:733
  406.9 47.7 %attention_backward.1 = bf16[2,592,3072]{2,1,0:T(8,128)(2,1)S(1)} custom-call(s32[2]{0:T(128)S(1)} %fusion.74.lengths, bf16[2,592,3072]{2,1,0:T(8,128)(2,1)} %add_convert_fusion.q_ref.k_ref.v_ref, bf16[2,592,3072]{2,1,0:T(8,128)(2,1)} %add_convert_fusion.q_ref.k_ref.v_ref, bf16[2,592,3072]{2,1,0:T(8,128)(2,1)} %add_convert_fusion.q_ref.k_ref.v_ref, ...), custom_call_target="tpu_custom_call" | custom-call | flops 14355005440 | bytes 16973824 | tf_op jit(solution)/shard_map/attention_backward/pallas_call | solution.py:386
  458.6 11.2 %fusion.103 = f32[1024,3072,1]{1,0,2:T(8,128)} fusion(bf16[2,592,1024]{2,1,0:T(8,128)(2,1)S(1)} %copy-done.23, bf16[2,592,3072]{2,1,0:T(8,128)(2,1)S(1)} %attention_backward.1), kind=kOutput, calls=%fused_computation.256 | convolution fusion | flops 7449083904 | bytes 22282240 | tf_op jit(solution)/shard_map/bsd,bsc->dc/dot_general | solution.py:742
  469.8 3.2 fusion.33
  479.0 5.7 copy.74
  485.9 8.9 %collective-permute-done.30 = bf16[64,2048]{1,0:T(8,128)(2,1)S(1)} collective-permute-done((bf16[64,2048]{1,0:T(8,128)(2,1)S(1)}, bf16[64,2048]{1,0:T(8,128)(2,1)S(1)}, u32[]{:S(2)}, u32[]{:S(2)}) %collective-permute-start.30) | collective-permute-done | bytes 262176 | tf_op jit(solution)/shard_map/ppermute | solution.py:415
  499.7 9.9 %fusion.102 = f32[2,592,1024]{2,1,0:T(8,128)} fusion(bf16[2,592,3072]{2,1,0:T(8,128)(2,1)S(1)} %attention_backward.1, bf16[1024,3072,1]{1,0,2:T(8,128)(2,1)S(1)} %bitcast.259), kind=kOutput, calls=%fused_computation.255 | convolution fusion | flops 7449083904 | bytes 18415616 | tf_op jit(solution)/shard_map/bsc,dc->bsd/dot_general | solution.py:744
  517.5 5.0 fusion.15
  525.2 5.8 collective-permute-start.37
  533.6 3.4 fusion.28
  537.1 4.4 fusion.27
  549.3 3.2 collective-permute-done.45
  553.1 12.7 %collective-permute-done.42 = bf16[2,160,1024]{2,1,0:T(8,128)(2,1)S(1)} collective-permute-done((bf16[2,160,1024]{2,1,0:T(8,128)(2,1)S(1)}, bf16[2,160,1024]{2,1,0:T(8,128)(2,1)S(1)}, u32[]{:S(2)}, u32[]{:S(2)}) %collective-permute-start.42) | collective-permute-done | bytes 655392 | tf_op jit(solution)/shard_map/ppermute | solution.py:410
  565.9 6.3 %collective-permute-start.49 = (bf16[64,1536]{1,0:T(8,128)(2,1)S(1)}, bf16[64,1536]{1,0:T(8,128)(2,1)S(1)}, u32[]{:S(2)}, u32[]{:S(2)}) collective-permute-start(bf16[64,1536]{1,0:T(8,128)(2,1)S(1)} %get-tuple-element.240), channel_id=1, source_target_pairs={{0,8},{2,10},{4,12},{6,14},{8,16},{10,18},{12,20},{14,22},{16,24},... | collective-permute-start | bytes 589832 | tf_op jit(solution)/shard_map/ppermute | solution.py:415
  579.3 6.1 collective-permute-done.50
  585.5 7.5 %collective-permute-done.46 = bf16[2,160,1024]{2,1,0:T(8,128)(2,1)S(1)} collective-permute-done((bf16[2,160,1024]{2,1,0:T(8,128)(2,1)S(1)}, bf16[2,160,1024]{2,1,0:T(8,128)(2,1)S(1)}, u32[]{:S(2)}, u32[]{:S(2)}) %collective-permute-start.46) | collective-permute-done | bytes 655392 | tf_op jit(solution)/shard_map/ppermute | solution.py:410
  602.2 5.7 copy.75
  (417 shorter events, 155.9 us)
Async XLA Ops:
  7.3 153.9 %all-gather.3.cloned.1.call-start = ((), (), s32[]{:S(2)}) async-start(), calls=%async_computation | async-start | bytes 10813440 | tf_op jit(solution)/shard_map/all_gather | solution.py:687
  13.0 31.9 %collective-permute-start.3 = (bf16[2,320,1024]{2,1,0:T(8,128)(2,1)S(1)}, bf16[2,320,1024]{2,1,0:T(8,128)(2,1)}, u32[]{:S(2)}, u32[]{:S(2)}) collective-permute-start(bf16[2,320,1024]{2,1,0:T(8,128)(2,1)S(1)} %bitcast.279), channel_id=1, source_target_pairs={{0,1},{1,0},{2,3},{3,2},{4,5},{5,4},{6,7},{7,6},{8,9},{9,8},{10,11... | collective-permute-start | bytes 3932168 | tf_op jit(solution)/shard_map/ppermute | solution.py:587
  16.7 10.1 %collective-permute-start = (bf16[64,1664]{1,0:T(8,128)(2,1)S(1)}, bf16[64,1664]{1,0:T(8,128)(2,1)S(1)}, u32[]{:S(2)}, u32[]{:S(2)}) collective-permute-start(bf16[64,1664]{1,0:T(8,128)(2,1)S(1)} %get-tuple-element.247), channel_id=1, source_target_pairs={{0,8},{2,10},{4,12},{6,14},{8,16},{10,18},{12,20},{14,22},{16,24},... | collective-permute-start | bytes 638984 | tf_op jit(solution)/shard_map/ppermute | solution.py:415
  18.4 16.3 %collective-permute-start.1 = (bf16[64,1664]{1,0:T(8,128)(2,1)S(1)}, bf16[64,1664]{1,0:T(8,128)(2,1)}, u32[]{:S(2)}, u32[]{:S(2)}) collective-permute-start(bf16[64,1664]{1,0:T(8,128)(2,1)S(1)} %get-tuple-element.247), channel_id=1, source_target_pairs={{0,16},{2,18},{4,20},{6,22},{8,24},{10,26},{12,28},{14,30},{16,0},... | collective-permute-start | bytes 638984 | tf_op jit(solution)/shard_map/ppermute | solution.py:415
  20.9 13.7 %collective-permute-start.2 = (bf16[64,1664]{1,0:T(8,128)(2,1)S(1)}, bf16[64,1664]{1,0:T(8,128)(2,1)}, u32[]{:S(2)}, u32[]{:S(2)}) collective-permute-start(bf16[64,1664]{1,0:T(8,128)(2,1)S(1)} %get-tuple-element.247), channel_id=1, source_target_pairs={{0,24},{2,26},{4,28},{6,30},{8,0},{10,2},{12,4},{14,6},{16,8},{18,... | collective-permute-start | bytes 638984 | tf_op jit(solution)/shard_map/ppermute | solution.py:415
  48.2 172.0 %all-gather.5.cloned.1.call-start = ((), (), s32[]{:S(2)}) async-start(), calls=%async_computation.1 | async-start | bytes 8650752 | tf_op jit(solution)/shard_map/all_gather | solution.py:690
  49.1 11.1 %collective-permute-start.6 = (bf16[4,32,1664]{2,1,0:T(8,128)(2,1)S(1)}, bf16[4,32,1664]{2,1,0:T(8,128)(2,1)S(1)}, u32[]{:S(2)}, u32[]{:S(2)}) collective-permute-start(bf16[4,32,1664]{2,1,0:T(8,128)(2,1)S(1)} %get-tuple-element.238), channel_id=1, source_target_pairs={{0,1},{1,0},{2,3},{3,2},{4,5},{5,4},{6,7},{7,6},{8,9},{9,8},{10,11... | collective-permute-start | bytes 1277960 | tf_op jit(solution)/shard_map/ppermute | solution.py:410
  50.9 12.9 %collective-permute-start.4 = (bf16[4,32,1664]{2,1,0:T(8,128)(2,1)S(1)}, bf16[4,32,1664]{2,1,0:T(8,128)(2,1)S(1)}, u32[]{:S(2)}, u32[]{:S(2)}) collective-permute-start(bf16[4,32,1664]{2,1,0:T(8,128)(2,1)S(1)} %get-tuple-element.239), channel_id=1, source_target_pairs={{0,4},{2,6},{4,0},{6,2},{8,12},{10,14},{12,8},{14,10},{16,20},{18,... | collective-permute-start | bytes 1277960 | tf_op jit(solution)/shard_map/ppermute | solution.py:410
  60.3 24.7 %collective-permute-start.7 = (bf16[2,4,32,1664]{3,2,1,0:T(8,128)(2,1)S(1)}, bf16[2,4,32,1664]{3,2,1,0:T(8,128)(2,1)S(1)}, u32[]{:S(2)}, u32[]{:S(2)}) collective-permute-start(bf16[2,4,32,1664]{3,2,1,0:T(8,128)(2,1)S(1)} %pad_maximum_fusion.4.refs_2_), channel_id=1, source_target_pairs={{0,4},{2,6},{4,0},{6,2},{8,12},{10,14},{12,8},{14,10},{16,20},{18,... | collective-permute-start | bytes 2555912 | tf_op jit(solution)/shard_map/ppermute | solution.py:410
  63.9 21.3 %collective-permute-start.5 = (bf16[2,4,32,1664]{3,2,1,0:T(8,128)(2,1)S(1)}, bf16[2,4,32,1664]{3,2,1,0:T(8,128)(2,1)S(1)}, u32[]{:S(2)}, u32[]{:S(2)}) collective-permute-start(bf16[2,4,32,1664]{3,2,1,0:T(8,128)(2,1)S(1)} %pad_maximum_fusion.3.refs_0_), channel_id=1, source_target_pairs={{0,1},{1,0},{2,3},{3,2},{4,5},{5,4},{6,7},{7,6},{8,9},{9,8},{10,11... | collective-permute-start | bytes 2555912 | tf_op jit(solution)/shard_map/ppermute | solution.py:410
  64.7 25.5 %collective-permute-start.10 = (bf16[2,4,32,1664]{3,2,1,0:T(8,128)(2,1)S(1)}, bf16[2,4,32,1664]{3,2,1,0:T(8,128)(2,1)S(1)}, u32[]{:S(2)}, u32[]{:S(2)}) collective-permute-start(bf16[2,4,32,1664]{3,2,1,0:T(8,128)(2,1)S(1)} %pad_maximum_fusion.4.refs_2_), channel_id=1, source_target_pairs={{0,2},{2,0},{4,6},{6,4},{8,10},{10,8},{12,14},{14,12},{16,18},{18,... | collective-permute-start | bytes 2555912 | tf_op jit(solution)/shard_map/ppermute | solution.py:410
  64.7 25.5 %collective-permute-start.8 = (bf16[2,4,32,1664]{3,2,1,0:T(8,128)(2,1)S(1)}, bf16[2,4,32,1664]{3,2,1,0:T(8,128)(2,1)S(1)}, u32[]{:S(2)}, u32[]{:S(2)}) collective-permute-start(bf16[2,4,32,1664]{3,2,1,0:T(8,128)(2,1)S(1)} %pad_maximum_fusion.3.refs_0_), channel_id=1, source_target_pairs={{0,2},{2,0},{4,6},{6,4},{8,10},{10,8},{12,14},{14,12},{16,18},{18,... | collective-permute-start | bytes 2555912 | tf_op jit(solution)/shard_map/ppermute | solution.py:410
  119.4 36.0 %collective-permute-start.12 = (bf16[2,320,1024]{2,1,0:T(8,128)(2,1)}, bf16[2,320,1024]{2,1,0:T(8,128)(2,1)}, u32[]{:S(2)}, u32[]{:S(2)}) collective-permute-start(bf16[2,320,1024]{2,1,0:T(8,128)(2,1)} %dynamic-slice_bitcast_fusion), channel_id=1, source_target_pairs={{0,1},{1,0},{2,3},{3,2},{4,5},{5,4},{6,7},{7,6},{8,9},{9,8},{10,11... | collective-permute-start | bytes 3932168 | tf_op jit(solution)/shard_map/ppermute | solution.py:587
  226.2 32.6 %collective-permute-start.13 = (bf16[4,2,64,4096]{3,2,0,1:T(8,128)(2,1)}, bf16[4,2,64,4096]{3,2,0,1:T(8,128)(2,1)}, u32[]{:S(2)}, u32[]{:S(2)}) collective-permute-start(bf16[4,2,64,4096]{3,2,0,1:T(8,128)(2,1)} %fusion.31), channel_id=1, source_target_pairs={{0,2},{2,0},{4,6},{6,4},{8,10},{10,8},{12,14},{14,12},{16,18},{18,... | collective-permute-start | bytes 12582920 | tf_op jit(solution)/shard_map/ppermute | solution.py:410
  265.4 25.4 %collective-permute-start.15 = (bf16[4,32,4096]{2,1,0:T(8,128)(2,1)S(1)}, bf16[4,32,4096]{2,1,0:T(8,128)(2,1)S(1)}, u32[]{:S(2)}, u32[]{:S(2)}) collective-permute-start(bf16[4,32,4096]{2,1,0:T(8,128)(2,1)S(1)} %dynamic-slice_bitcast_fusion.2), channel_id=1, source_target_pairs={{0,4},{2,6},{4,0},{6,2},{8,12},{10,14},{12,8},{14,10},{16,20},{18,... | collective-permute-start | bytes 3145736 | tf_op jit(solution)/shard_map/ppermute | solution.py:410
  267.0 25.1 %collective-permute-start.14 = (bf16[4,2,32,2048]{3,2,0,1:T(8,128)(2,1)S(1)}, bf16[4,2,32,2048]{3,2,0,1:T(8,128)(2,1)S(1)}, u32[]{:S(2)}, u32[]{:S(2)}) collective-permute-start(bf16[4,2,32,2048]{3,2,0,1:T(8,128)(2,1)S(1)} %constant_dynamic-slice_fusion.29), channel_id=1, source_target_pairs={{0,1},{1,0},{2,3},{3,2},{4,5},{5,4},{6,7},{7,6},{8,9},{9,8},{10,11... | collective-permute-start | bytes 3145736 | tf_op jit(solution)/shard_map/ppermute | solution.py:410
  298.8 25.0 %collective-permute-start.18 = (bf16[4,2,64,4096]{3,2,0,1:T(8,128)(2,1)}, bf16[4,2,64,4096]{3,2,0,1:T(8,128)(2,1)S(1)}, u32[]{:S(2)}, u32[]{:S(2)}) collective-permute-start(bf16[4,2,64,4096]{3,2,0,1:T(8,128)(2,1)} %fusion.32), channel_id=1, source_target_pairs={{0,2},{2,0},{4,6},{6,4},{8,10},{10,8},{12,14},{14,12},{16,18},{18,... | collective-permute-start | bytes 12582920 | tf_op jit(solution)/shard_map/ppermute | solution.py:410
  304.7 17.6 %collective-permute-start.17 = (bf16[4,32,2048]{2,1,0:T(8,128)(2,1)S(1)}, bf16[4,32,2048]{2,1,0:T(8,128)(2,1)}, u32[]{:S(2)}, u32[]{:S(2)}) collective-permute-start(bf16[4,32,2048]{2,1,0:T(8,128)(2,1)S(1)} %constant_dynamic-slice_fusion.28), channel_id=1, source_target_pairs={{0,1},{1,0},{2,3},{3,2},{4,5},{5,4},{6,7},{7,6},{8,9},{9,8},{10,11... | collective-permute-start | bytes 1572872 | tf_op jit(solution)/shard_map/ppermute | solution.py:410
  306.2 17.3 %collective-permute-start.16 = (bf16[4,32,2048]{2,1,0:T(8,128)(2,1)}, bf16[4,32,2048]{2,1,0:T(8,128)(2,1)S(1)}, u32[]{:S(2)}, u32[]{:S(2)}) collective-permute-start(bf16[4,32,2048]{2,1,0:T(8,128)(2,1)} %dynamic-slice_bitcast_fusion.5), channel_id=1, source_target_pairs={{0,4},{2,6},{4,0},{6,2},{8,12},{10,14},{12,8},{14,10},{16,20},{18,... | collective-permute-start | bytes 1572872 | tf_op jit(solution)/shard_map/ppermute | solution.py:410
  346.0 25.2 %collective-permute-start.23 = (bf16[4,32,4096]{2,1,0:T(8,128)(2,1)}, bf16[4,32,4096]{2,1,0:T(8,128)(2,1)}, u32[]{:S(2)}, u32[]{:S(2)}) collective-permute-start(bf16[4,32,4096]{2,1,0:T(8,128)(2,1)} %dynamic-slice_bitcast_fusion.1), channel_id=1, source_target_pairs={{0,4},{2,6},{4,0},{6,2},{8,12},{10,14},{12,8},{14,10},{16,20},{18,... | collective-permute-start | bytes 3145736 | tf_op jit(solution)/shard_map/ppermute | solution.py:410
  346.7 12.0 %collective-permute-start.19 = (bf16[64,2048]{1,0:T(8,128)(2,1)S(1)}, bf16[64,2048]{1,0:T(8,128)(2,1)}, u32[]{:S(2)}, u32[]{:S(2)}) collective-permute-start(bf16[64,2048]{1,0:T(8,128)(2,1)S(1)} %get-tuple-element.233), channel_id=1, source_target_pairs={{0,8},{2,10},{4,12},{6,14},{8,16},{10,18},{12,20},{14,22},{16,24},... | collective-permute-start | bytes 786440 | tf_op jit(solution)/shard_map/ppermute | solution.py:415
  348.2 19.5 %collective-permute-start.20 = (bf16[64,2048]{1,0:T(8,128)(2,1)S(1)}, bf16[64,2048]{1,0:T(8,128)(2,1)}, u32[]{:S(2)}, u32[]{:S(2)}) collective-permute-start(bf16[64,2048]{1,0:T(8,128)(2,1)S(1)} %get-tuple-element.235), channel_id=1, source_target_pairs={{0,16},{2,18},{4,20},{6,22},{8,24},{10,26},{12,28},{14,30},{16,0},... | collective-permute-start | bytes 786440 | tf_op jit(solution)/shard_map/ppermute | solution.py:415
  349.2 18.6 %collective-permute-start.21 = (bf16[64,2048]{1,0:T(8,128)(2,1)S(1)}, bf16[64,2048]{1,0:T(8,128)(2,1)}, u32[]{:S(2)}, u32[]{:S(2)}) collective-permute-start(bf16[64,2048]{1,0:T(8,128)(2,1)S(1)} %get-tuple-element.234), channel_id=1, source_target_pairs={{0,24},{2,26},{4,28},{6,30},{8,0},{10,2},{12,4},{14,6},{16,8},{18,... | collective-permute-start | bytes 786440 | tf_op jit(solution)/shard_map/ppermute | solution.py:415
  355.8 24.0 %collective-permute-start.22 = (bf16[4,2,32,2048]{3,2,0,1:T(8,128)(2,1)}, bf16[4,2,32,2048]{3,2,0,1:T(8,128)(2,1)}, u32[]{:S(2)}, u32[]{:S(2)}) collective-permute-start(bf16[4,2,32,2048]{3,2,0,1:T(8,128)(2,1)} %constant_dynamic-slice_fusion.26), channel_id=1, source_target_pairs={{0,1},{1,0},{2,3},{3,2},{4,5},{5,4},{6,7},{7,6},{8,9},{9,8},{10,11... | collective-permute-start | bytes 3145736 | tf_op jit(solution)/shard_map/ppermute | solution.py:410
  401.2 55.1 %collective-permute-start.28 = (bf16[4,2,64,1024]{3,2,0,1:T(8,128)(2,1)}, bf16[4,2,64,1024]{3,2,0,1:T(8,128)(2,1)S(1)}, u32[]{:S(2)}, u32[]{:S(2)}) collective-permute-start(bf16[4,2,64,1024]{3,2,0,1:T(8,128)(2,1)} %fusion.55), channel_id=1, source_target_pairs={{0,2},{2,0},{4,6},{6,4},{8,10},{10,8},{12,14},{14,12},{16,18},{18,... | collective-permute-start | bytes 3145736 | tf_op jit(solution)/shard_map/ppermute | solution.py:410
  401.2 53.4 %collective-permute-start.27 = (bf16[4,32,2048]{2,1,0:T(8,128)(2,1)S(1)}, bf16[4,32,2048]{2,1,0:T(8,128)(2,1)S(1)}, u32[]{:S(2)}, u32[]{:S(2)}) collective-permute-start(bf16[4,32,2048]{2,1,0:T(8,128)(2,1)S(1)} %constant_dynamic-slice_fusion.25), channel_id=1, source_target_pairs={{0,1},{1,0},{2,3},{3,2},{4,5},{5,4},{6,7},{7,6},{8,9},{9,8},{10,11... | collective-permute-start | bytes 1572872 | tf_op jit(solution)/shard_map/ppermute | solution.py:410
  403.8 51.0 %collective-permute-start.26 = (bf16[4,32,2048]{2,1,0:T(8,128)(2,1)S(1)}, bf16[4,32,2048]{2,1,0:T(8,128)(2,1)S(1)}, u32[]{:S(2)}, u32[]{:S(2)}) collective-permute-start(bf16[4,32,2048]{2,1,0:T(8,128)(2,1)S(1)} %dynamic-slice_bitcast_fusion.4), channel_id=1, source_target_pairs={{0,4},{2,6},{4,0},{6,2},{8,12},{10,14},{12,8},{14,10},{16,20},{18,... | collective-permute-start | bytes 1572872 | tf_op jit(solution)/shard_map/ppermute | solution.py:410
  404.8 50.2 %collective-permute-start.24 = (bf16[2,160,1024]{2,1,0:T(8,128)(2,1)S(1)}, bf16[2,160,1024]{2,1,0:T(8,128)(2,1)S(1)}, u32[]{:S(2)}, u32[]{:S(2)}) collective-permute-start(bf16[2,160,1024]{2,1,0:T(8,128)(2,1)S(1)} %get-tuple-element.226), channel_id=1, source_target_pairs={{0,1},{1,0},{2,3},{3,2},{4,5},{5,4},{6,7},{7,6},{8,9},{9,8},{10,11... | collective-permute-start | bytes 1966088 | tf_op jit(solution)/shard_map/ppermute | solution.py:410
  406.3 48.6 %collective-permute-start.25 = (bf16[2,160,1024]{2,1,0:T(8,128)(2,1)S(1)}, bf16[2,160,1024]{2,1,0:T(8,128)(2,1)S(1)}, u32[]{:S(2)}, u32[]{:S(2)}) collective-permute-start(bf16[2,160,1024]{2,1,0:T(8,128)(2,1)S(1)} %get-tuple-element.227), channel_id=1, source_target_pairs={{0,1},{1,0},{2,3},{3,2},{4,5},{5,4},{6,7},{7,6},{8,9},{9,8},{10,11... | collective-permute-start | bytes 1966088 | tf_op jit(solution)/shard_map/ppermute | solution.py:410
  473.1 44.5 %collective-permute-start.36 = (bf16[4,2,64,3072]{3,2,0,1:T(8,128)(2,1)S(1)}, bf16[4,2,64,3072]{3,2,0,1:T(8,128)(2,1)}, u32[]{:S(2)}, u32[]{:S(2)}) collective-permute-start(bf16[4,2,64,3072]{3,2,0,1:T(8,128)(2,1)S(1)} %fusion.33), channel_id=1, source_target_pairs={{0,2},{2,0},{4,6},{6,4},{8,10},{10,8},{12,14},{14,12},{16,18},{18,... | collective-permute-start | bytes 9437192 | tf_op jit(solution)/shard_map/ppermute | solution.py:410
  473.3 11.4 %collective-permute-start.29 = (bf16[64,2048]{1,0:T(8,128)(2,1)S(1)}, bf16[64,2048]{1,0:T(8,128)(2,1)S(1)}, u32[]{:S(2)}, u32[]{:S(2)}) collective-permute-start(bf16[64,2048]{1,0:T(8,128)(2,1)S(1)} %get-tuple-element.230), channel_id=1, source_target_pairs={{0,8},{2,10},{4,12},{6,14},{8,16},{10,18},{12,20},{14,22},{16,24},... | collective-permute-start | bytes 786440 | tf_op jit(solution)/shard_map/ppermute | solution.py:415
  473.4 21.3 %collective-permute-start.30 = (bf16[64,2048]{1,0:T(8,128)(2,1)S(1)}, bf16[64,2048]{1,0:T(8,128)(2,1)S(1)}, u32[]{:S(2)}, u32[]{:S(2)}) collective-permute-start(bf16[64,2048]{1,0:T(8,128)(2,1)S(1)} %get-tuple-element.232), channel_id=1, source_target_pairs={{0,16},{2,18},{4,20},{6,22},{8,24},{10,26},{12,28},{14,30},{16,0},... | collective-permute-start | bytes 786440 | tf_op jit(solution)/shard_map/ppermute | solution.py:415
  475.0 19.7 %collective-permute-start.31 = (bf16[64,2048]{1,0:T(8,128)(2,1)S(1)}, bf16[64,2048]{1,0:T(8,128)(2,1)S(1)}, u32[]{:S(2)}, u32[]{:S(2)}) collective-permute-start(bf16[64,2048]{1,0:T(8,128)(2,1)S(1)} %get-tuple-element.231), channel_id=1, source_target_pairs={{0,24},{2,26},{4,28},{6,30},{8,0},{10,2},{12,4},{14,6},{16,8},{18,... | collective-permute-start | bytes 786440 | tf_op jit(solution)/shard_map/ppermute | solution.py:415
  477.5 18.2 %collective-permute-start.33 = (bf16[4,32,1024]{2,1,0:T(8,128)(2,1)S(1)}, bf16[4,32,1024]{2,1,0:T(8,128)(2,1)S(1)}, u32[]{:S(2)}, u32[]{:S(2)}) collective-permute-start(bf16[4,32,1024]{2,1,0:T(8,128)(2,1)S(1)} %dynamic-slice_bitcast_fusion.7), channel_id=1, source_target_pairs={{0,4},{2,6},{4,0},{6,2},{8,12},{10,14},{12,8},{14,10},{16,20},{18,... | collective-permute-start | bytes 786440 | tf_op jit(solution)/shard_map/ppermute | solution.py:410
  484.7 11.0 %collective-permute-start.32 = (bf16[4,2,32,512]{3,2,0,1:T(8,128)(2,1)S(1)}, bf16[4,2,32,512]{3,2,0,1:T(8,128)(2,1)S(1)}, u32[]{:S(2)}, u32[]{:S(2)}) collective-permute-start(bf16[4,2,32,512]{3,2,0,1:T(8,128)(2,1)S(1)} %constant_dynamic-slice_fusion.23), channel_id=1, source_target_pairs={{0,1},{1,0},{2,3},{3,2},{4,5},{5,4},{6,7},{7,6},{8,9},{9,8},{10,11... | collective-permute-start | bytes 786440 | tf_op jit(solution)/shard_map/ppermute | solution.py:410
  496.6 19.7 %collective-permute-start.35 = (bf16[4,32,512]{2,1,0:T(8,128)(2,1)}, bf16[4,32,512]{2,1,0:T(8,128)(2,1)S(1)}, u32[]{:S(2)}, u32[]{:S(2)}) collective-permute-start(bf16[4,32,512]{2,1,0:T(8,128)(2,1)} %constant_dynamic-slice_fusion.22), channel_id=1, source_target_pairs={{0,1},{1,0},{2,3},{3,2},{4,5},{5,4},{6,7},{7,6},{8,9},{9,8},{10,11... | collective-permute-start | bytes 393224 | tf_op jit(solution)/shard_map/ppermute | solution.py:410
  522.9 19.3 %collective-permute-start.41 = (bf16[4,32,3072]{2,1,0:T(8,128)(2,1)S(1)}, bf16[4,32,3072]{2,1,0:T(8,128)(2,1)S(1)}, u32[]{:S(2)}, u32[]{:S(2)}) collective-permute-start(bf16[4,32,3072]{2,1,0:T(8,128)(2,1)S(1)} %dynamic-slice_bitcast_fusion.3), channel_id=1, source_target_pairs={{0,4},{2,6},{4,0},{6,2},{8,12},{10,14},{12,8},{14,10},{16,20},{18,... | collective-permute-start | bytes 2359304 | tf_op jit(solution)/shard_map/ppermute | solution.py:410
  524.5 18.0 %collective-permute-start.40 = (bf16[4,2,32,1536]{3,2,0,1:T(8,128)(2,1)S(1)}, bf16[4,2,32,1536]{3,2,0,1:T(8,128)(2,1)S(1)}, u32[]{:S(2)}, u32[]{:S(2)}) collective-permute-start(bf16[4,2,32,1536]{3,2,0,1:T(8,128)(2,1)S(1)} %constant_dynamic-slice_fusion.19), channel_id=1, source_target_pairs={{0,1},{1,0},{2,3},{3,2},{4,5},{5,4},{6,7},{7,6},{8,9},{9,8},{10,11... | collective-permute-start | bytes 2359304 | tf_op jit(solution)/shard_map/ppermute | solution.py:410
  525.2 16.2 %collective-permute-start.37 = (bf16[64,512]{1,0:T(8,128)(2,1)S(1)}, bf16[64,512]{1,0:T(8,128)(2,1)S(1)}, u32[]{:S(2)}, u32[]{:S(2)}) collective-permute-start(bf16[64,512]{1,0:T(8,128)(2,1)S(1)} %get-tuple-element.243), channel_id=1, source_target_pairs={{0,8},{2,10},{4,12},{6,14},{8,16},{10,18},{12,20},{14,22},{16,24},... | collective-permute-start | bytes 196616 | tf_op jit(solution)/shard_map/ppermute | solution.py:415
  531.1 10.4 %collective-permute-start.38 = (bf16[64,512]{1,0:T(8,128)(2,1)S(1)}, bf16[64,512]{1,0:T(8,128)(2,1)S(1)}, u32[]{:S(2)}, u32[]{:S(2)}) collective-permute-start(bf16[64,512]{1,0:T(8,128)(2,1)S(1)} %get-tuple-element.245), channel_id=1, source_target_pairs={{0,16},{2,18},{4,20},{6,22},{8,24},{10,26},{12,28},{14,30},{16,0},... | collective-permute-start | bytes 196616 | tf_op jit(solution)/shard_map/ppermute | solution.py:415
  542.8 9.7 %collective-permute-start.45 = (bf16[4,32,1536]{2,1,0:T(8,128)(2,1)S(1)}, bf16[4,32,1536]{2,1,0:T(8,128)(2,1)S(1)}, u32[]{:S(2)}, u32[]{:S(2)}) collective-permute-start(bf16[4,32,1536]{2,1,0:T(8,128)(2,1)S(1)} %constant_dynamic-slice_fusion.17), channel_id=1, source_target_pairs={{0,1},{1,0},{2,3},{3,2},{4,5},{5,4},{6,7},{7,6},{8,9},{9,8},{10,11... | collective-permute-start | bytes 1179656 | tf_op jit(solution)/shard_map/ppermute | solution.py:410
  547.8 18.0 %collective-permute-start.42 = (bf16[2,160,1024]{2,1,0:T(8,128)(2,1)S(1)}, bf16[2,160,1024]{2,1,0:T(8,128)(2,1)S(1)}, u32[]{:S(2)}, u32[]{:S(2)}) collective-permute-start(bf16[2,160,1024]{2,1,0:T(8,128)(2,1)S(1)} %get-tuple-element.225), channel_id=1, source_target_pairs={{0,1},{1,0},{2,3},{3,2},{4,5},{5,4},{6,7},{7,6},{8,9},{9,8},{10,11... | collective-permute-start | bytes 1966088 | tf_op jit(solution)/shard_map/ppermute | solution.py:410
  565.9 13.4 %collective-permute-start.49 = (bf16[64,1536]{1,0:T(8,128)(2,1)S(1)}, bf16[64,1536]{1,0:T(8,128)(2,1)S(1)}, u32[]{:S(2)}, u32[]{:S(2)}) collective-permute-start(bf16[64,1536]{1,0:T(8,128)(2,1)S(1)} %get-tuple-element.240), channel_id=1, source_target_pairs={{0,8},{2,10},{4,12},{6,14},{8,16},{10,18},{12,20},{14,22},{16,24},... | collective-permute-start | bytes 589832 | tf_op jit(solution)/shard_map/ppermute | solution.py:415
  572.2 13.2 %collective-permute-start.50 = (bf16[64,1536]{1,0:T(8,128)(2,1)S(1)}, bf16[64,1536]{1,0:T(8,128)(2,1)S(1)}, u32[]{:S(2)}, u32[]{:S(2)}) collective-permute-start(bf16[64,1536]{1,0:T(8,128)(2,1)S(1)} %get-tuple-element.242), channel_id=1, source_target_pairs={{0,16},{2,18},{4,20},{6,22},{8,24},{10,26},{12,28},{14,30},{16,0},... | collective-permute-start | bytes 589832 | tf_op jit(solution)/shard_map/ppermute | solution.py:415
  573.1 12.3 %collective-permute-start.51 = (bf16[64,1536]{1,0:T(8,128)(2,1)S(1)}, bf16[64,1536]{1,0:T(8,128)(2,1)S(1)}, u32[]{:S(2)}, u32[]{:S(2)}) collective-permute-start(bf16[64,1536]{1,0:T(8,128)(2,1)S(1)} %get-tuple-element.241), channel_id=1, source_target_pairs={{0,24},{2,26},{4,28},{6,30},{8,0},{10,2},{12,4},{14,6},{16,8},{18,... | collective-permute-start | bytes 589832 | tf_op jit(solution)/shard_map/ppermute | solution.py:415
  578.5 14.5 %collective-permute-start.46 = (bf16[2,160,1024]{2,1,0:T(8,128)(2,1)S(1)}, bf16[2,160,1024]{2,1,0:T(8,128)(2,1)S(1)}, u32[]{:S(2)}, u32[]{:S(2)}) collective-permute-start(bf16[2,160,1024]{2,1,0:T(8,128)(2,1)S(1)} %get-tuple-element.145), channel_id=1, source_target_pairs={{0,1},{1,0},{2,3},{3,2},{4,5},{5,4},{6,7},{7,6},{8,9},{9,8},{10,11... | collective-permute-start | bytes 1966088 | tf_op jit(solution)/shard_map/ppermute | solution.py:410
  597.4 11.9 %collective-permute-start.54 = (f32[2,192]{1,0:T(2,128)S(1)}, f32[2,192]{1,0:T(2,128)S(1)}, u32[]{:S(2)}, u32[]{:S(2)}) collective-permute-start(f32[2,192]{1,0:T(2,128)S(1)} %get-tuple-element.258), channel_id=1, source_target_pairs={{0,8},{2,10},{4,12},{6,14},{8,16},{10,18},{12,20},{14,22},{16,24},... | collective-permute-start | bytes 4616 | tf_op jit(solution)/shard_map/ppermute | solution.py:415
  597.6 11.7 %collective-permute-start.55 = (f32[2,192]{1,0:T(2,128)S(1)}, f32[2,192]{1,0:T(2,128)S(1)}, u32[]{:S(2)}, u32[]{:S(2)}) collective-permute-start(f32[2,192]{1,0:T(2,128)S(1)} %get-tuple-element.259), channel_id=1, source_target_pairs={{0,16},{2,18},{4,20},{6,22},{8,24},{10,26},{12,28},{14,30},{16,0},... | collective-permute-start | bytes 4616 | tf_op jit(solution)/shard_map/ppermute | solution.py:415
  (88 other events, 1032.6 us)
Sparse Core Ops, SparseCore 0:
  48.4 93.5 all-gather.2
  144.8 75.3 all-gather.4

commit v4 on v3

--- a/solution.py
+++ b/solution.py
@@ -715,11 +715,10 @@
     down_full = beside(last.reshape(2, width, -1), 0, hidden)
     act_grad = product("bsd,df->bsf", out_low, down_full)
     up_grad = (act_grad * slope).astype(BF16)
-    up_grad, normed_two = advance([down], up_grad, normed_two)
     up = Sum(product("bsd,bsf->df", normed_two, up_grad), coords)
     up_shift_grad = token_sum(up_grad)
     down.step()
-    (up_grad,), (down.state, up.state) = lax.optimization_barrier(((up_grad,), (down.state, up.state)))
+    up_grad, down.state, up.state = lax.optimization_barrier((up_grad, down.state, up.state))
     normed_two_grad = product("bsf,df->bsd", up_grad, up_full)
     normed_two_grad = advance([down, up], normed_two_grad)
     gain_two_grad = token_sum(normed_two_grad * unit_two)
@@ -729,11 +728,13 @@
     proj_low = after_attn_grad.astype(BF16)
     out = Sum(product("bsd,bsc->dc", proj_low, attended), coords)
     attended_grad = product("bsd,dc->bsc", proj_low, out_full).astype(BF16)
-    attended_grad, act = advance([down, up], attended_grad, act)
+    attended_grad, act = advance([down], attended_grad, act)
     mlp_out = product("bsf,df->bsd", act, down_full)
     finished = (after_attn + mlp_out + down_shift) * kept
-    (attended_grad, qkv), (finished, out.state) = lax.optimization_barrier(
-        ((attended_grad, qkv), (finished, out.state))
+    down.step()
+    up.step()
+    attended_grad, qkv, finished, out.state, down.state, up.state = lax.optimization_barrier(
+        (attended_grad, qkv, finished, out.state, down.state, up.state)
     )
     qkv_grad = attention_backward(lengths, qkv, lse, attended_grad)
     held, near, far = split_slots(finished, slots)

time: 625 us -> 612 us (0.979)
  waiting for transfers between devices: 127 us -> 117 us
  starting transfers between devices: 70.6 us -> 60.7 us
  local copies, waits for them, and re-layouts: 94.6 us -> 104 us
    ppermute x18, starting transfers between devices: 35.5 us -> 22.2 us  [shift(): lax.ppermute(array, 'dp', [(n, (n + 4 * by) % count) for n in range(count)])]
    reduce_sum x6 -> x5, other arithmetic: 22.9 us -> 17 us  [token_sum(): return jnp.sum(values.astype(F32), axis=(0, 1))]
    unnamed x161 -> x137, local copies, waits for them, and re-layouts: 35.5 us -> 37.5 us
  transfers between devices with their start and end apart: 59 -> 59, of which waited for: 23 -> 22; matrix products, arithmetic and copies ran while one was open for 32% -> 38% of each run, Pallas kernels for 14% -> 14%
where the time goes in v4:
time: 612 us; the launch traced here: 605 us
  matrix products  146 us (24%)
  waiting for transfers between devices  117 us (19%)
  local copies, waits for them, and re-layouts  104 us (17%)
  Pallas kernels  88.7 us (14%)
  other arithmetic  72.1 us (12%)
  starting transfers between devices  60.7 us (10%)
  between operations  16 us (3%)
    ppermute x37, waiting for transfers between devices, swap(): lax.ppermute(array, axis, [(n, n ^ step) for n in range(lax.axis_size(axi...  78.6 us
    pallas_call x1, Pallas kernels, attention_backward(): pl.pallas_call(functools.partial(attention_backward_kernel, key_rows=key_...  47.7 us
    unnamed x137, local copies, waits for them, and re-layouts  37.5 us
    ppermute x37, starting transfers between devices, swap(): lax.ppermute(array, axis, [(n, n ^ step) for n in range(lax.axis_size(axi...  32.2 us
    pallas_call x1, Pallas kernels, attention_forward(): pl.pallas_call(functools.partial(attention_forward_kernel, key_rows=key_c...  32 us
    ppermute x18, waiting for transfers between devices, shift(): lax.ppermute(array, 'dp', [(n, (n + 4 * by) % count) for n in range(count)])  27 us
    convert_element_type x12, other arithmetic, over_pair(): return (take(array, mine, dim).astype(F32) + came).astype(self.sent)  24.8 us
    ppermute x18, starting transfers between devices, shift(): lax.ppermute(array, 'dp', [(n, (n + 4 * by) % count) for n in range(count)])  22.2 us
  transfers between devices with their start and end apart: 59, of which 22 were waited for; matrix products, arithmetic and copies ran while one was open for 38% of the time, Pallas kernels for 14%

profile of v4, /device:TPU:0, one launch (start us, length us, event | category | flops | bytes accessed | tf_op | source)
XLA Modules:
  0.0 605.0 jit_solution(17300521305633166964)
XLA Ops:
  7.3 5.3 constant_dynamic-slice_fusion.31
  13.0 3.0 collective-permute-start.3
  16.8 3.7 collective-permute-start.2
  26.1 12.2 %collective-permute-done.1 = bf16[64,1664]{1,0:T(8,128)(2,1)} collective-permute-done((bf16[64,1664]{1,0:T(8,128)(2,1)S(1)}, bf16[64,1664]{1,0:T(8,128)(2,1)}, u32[]{:S(2)}, u32[]{:S(2)}) %collective-permute-start.1) | collective-permute-done | bytes 213024 | tf_op jit(solution)/shard_map/ppermute | solution.py:415
  39.5 5.4 collective-permute-done.3
  52.4 7.8 %collective-permute-done.4 = bf16[4,32,1664]{2,1,0:T(8,128)(2,1)S(1)} collective-permute-done((bf16[4,32,1664]{2,1,0:T(8,128)(2,1)S(1)}, bf16[4,32,1664]{2,1,0:T(8,128)(2,1)S(1)}, u32[]{:S(2)}, u32[]{:S(2)}) %collective-permute-start.4) | collective-permute-done | bytes 426016 | tf_op jit(solution)/shard_map/ppermute | solution.py:410
  65.3 19.9 %collective-permute-done.5.refs_1_ = bf16[2,4,32,1664]{3,2,1,0:T(8,128)(2,1)S(1)} collective-permute-done((bf16[2,4,32,1664]{3,2,1,0:T(8,128)(2,1)S(1)}, bf16[2,4,32,1664]{3,2,1,0:T(8,128)(2,1)S(1)}, u32[]{:S(2)}, u32[]{:S(2)}) %collective-permute-start.5) | collective-permute-done | bytes 852000 | tf_op jit(solution)/shard_map/ppermute | solution.py:410
  90.3 4.4 assemble.1
  101.1 14.1 %add_convert_fusion.q_ref.k_ref.v_ref = bf16[2,592,3072]{2,1,0:T(8,128)(2,1)} fusion(f32[3072]{0:T(1024)S(1)} %add.407, bf16[2,592,1024]{2,1,0:T(8,128)(2,1)S(1)} %fusion.23, bf16[1024,3072,1]{1,0,2:T(8,128)(2,1)} %bitcast.256), kind=kOutput, calls=%fused_computation.11 | convolution fusion | flops 7456358400 | bytes 16003072 | tf_op jit(solution)/shard_map/bsd,dc->bsc/dot_general | solution.py:700
  119.1 3.2 collective-permute-start.12
  122.5 3.6 multiply_reduce_fusion
  128.3 3.1 copy-done
  131.4 32.0 %attention_forward.1 = (bf16[2,592,1024]{2,1,0:T(8,128)(2,1)S(1)}, f32[2,8,2,592]{3,2,1,0:T(2,128)S(1)}) custom-call(s32[2]{0:T(128)S(1)} %fusion.75.lengths, bf16[2,592,3072]{2,1,0:T(8,128)(2,1)S(1)} %copy-done, bf16[2,592,3072]{2,1,0:T(8,128)(2,1)S(1)} %copy-done, bf16[2,592,3072]{2,1,0:T(8,128)(2,1)S(1)} %copy-done), custom_call_target="tpu_custom_call" | custom-call | flops 5742002176 | bytes 9699328 | tf_op jit(solution)/shard_map/attention_forward/pallas_call | solution.py:357
  169.1 4.2 copy-done.1
  176.0 6.6 %fusion.100 = (f32[2,592]{1,0:T(2,128)S(1)}, f32[2,592,1024]{2,1,0:T(8,128)S(1)}) fusion(f32[1024]{0:T(1024)S(1)} %add.411, bf16[2,592,1024]{2,1,0:T(8,128)(2,1)S(1)} %get-tuple-element.98, bf16[1024,1024]{1,0:T(8,128)(2,1)S(1)} %beside.3, bf16[2,640,1024]{2,1,0:T(8,128)(2,1)} %constant_dynamic-update-slice_fusion.1), kind=kOutput, calls=%fused_computation.253 | convolution fusion | flops 2487876352 | bytes 11805312 | tf_op jit(solution)/shard_map/bsc,dc->bsd/dot_general | solution.py:704
  183.4 15.3 %multiply_convert_fusion = (bf16[2,592,4096]{2,1,0:T(8,128)(2,1)S(1)}, f32[2,592,4096]{2,1,0:T(8,128)}) fusion(f32[4096]{0:T(1024)S(1)} %bitcast.290, bf16[1024,4096]{1,0:T(8,128)(2,1)S(1)} %beside.4, f32[2,592,1024]{2,1,0:T(8,128)S(1)} %get-tuple-element.266, f32[1024]{0:T(1024)S(1)} %add.415, f32[1024]{0:T(1024)S(1)} %mul.225, ...), kind=kOutput, calls=%fused_computation.8 | convolution fusion | flops 9967271936 | bytes 42370304 | tf_op jit(solution)/shard_map/bsd,df->bsf/dot_general | solution.py:708
  198.6 3.7 copy-done.50
  202.4 14.3 %fusion.101 = f32[1024,4096,1]{1,0,2:T(8,128)} fusion(bf16[2,592,1024]{2,1,0:T(8,128)(2,1)S(1)} %copy-done.25, bf16[2,592,4096]{2,1,0:T(8,128)(2,1)S(1)} %get-tuple-element.112), kind=kOutput, calls=%fused_computation.254 | convolution fusion | flops 9932111872 | bytes 28901376 | tf_op jit(solution)/shard_map/bsd,bsf->df/dot_general | solution.py:713
  216.6 5.3 all-gather.5.cloned.1.call-done
  221.9 3.4 copy-done.2
  227.3 9.1 %fusion.31 = bf16[4,2,64,4096]{3,2,0,1:T(8,128)(2,1)} fusion(s32[]{:T(128)S(6)} %select_n.187, f32[4,2,2,64,4096]{4,3,2,1,0:T(8,128)} %bitcast.272), kind=kLoop, calls=%fused_computation.64 | loop fusion | bytes 8388612 | tf_op jit(solution)/shard_map/convert_element_type | solution.py:540
  236.7 21.6 %convert_reduce_fusion = (f32[4096]{0:T(1024)}, bf16[2,592,4096]{2,1,0:T(8,128)(2,1)}) fusion(f32[2,592,4096]{2,1,0:T(8,128)} %get-tuple-element.268, f32[4096]{0:T(1024)S(1)} %bitcast.291, bf16[2,592,1024]{2,1,0:T(8,128)(2,1)S(1)} %copy-done.25, bf16[1024,4096]{1,0:T(8,128)(2,1)S(1)} %beside.5), kind=kOutput, calls=%fused_computation.7 | convolution fusion | flops 9995153408 | bytes 39944192 | tf_op jit(solution)/shard_map/bsd,df->bsf/dot_general | solution.py:716
  258.3 18.3 %fusion.69 = f32[1024,4096,1]{1,0,2:T(8,128)} fusion(bf16[2,592,4096]{2,1,0:T(8,128)(2,1)} %get-tuple-element.105, f32[2,592,1024]{2,1,0:T(8,128)S(1)} %bitcast.261, f32[1024]{0:T(1024)S(1)} %add.415, f32[1024]{0:T(1024)S(1)} %mul.225, f32[2,592]{1,0:T(2,128)S(1)} %add_rsqrt_fusion, f32[2,592]{1,0:T(2,128)S(1)} %broadcast_multiply_fusion.4), kind=kOutput, calls=%fused_computation.154 | convolution fusion | flops 9938173952 | bytes 31343872 | tf_op jit(solution)/shard_map/bsd,bsf->df/dot_general | solution.py:718
  276.6 4.9 fusion.7
  283.7 6.3 %fusion.32 = bf16[4,2,64,4096]{3,2,0,1:T(8,128)(2,1)} fusion(s32[]{:T(128)S(6)} %select_n.187, f32[4,2,2,64,4096]{4,3,2,1,0:T(8,128)} %bitcast.270), kind=kLoop, calls=%fused_computation.65 | loop fusion | bytes 8388612 | tf_op jit(solution)/shard_map/convert_element_type | solution.py:540
  291.1 14.4 %fusion.11 = f32[2,592,1024]{2,1,0:T(8,128)} fusion(bf16[2,592,4096]{2,1,0:T(8,128)(2,1)} %get-tuple-element.105, bf16[1024,4096]{1,0:T(8,128)(2,1)S(1)} %bitcast.255), kind=kOutput, calls=%fused_computation.19 | convolution fusion | flops 9932111872 | bytes 22937600 | tf_op jit(solution)/shard_map/bsf,df->bsd/dot_general | solution.py:722
  308.9 7.0 %collective-permute-done.15 = bf16[4,32,4096]{2,1,0:T(8,128)(2,1)} collective-permute-done((bf16[4,32,4096]{2,1,0:T(8,128)(2,1)S(1)}, bf16[4,32,4096]{2,1,0:T(8,128)(2,1)}, u32[]{:S(2)}, u32[]{:S(2)}) %collective-permute-start.15) | collective-permute-done | bytes 1048608 | tf_op jit(solution)/shard_map/ppermute | solution.py:410
  317.5 8.4 %fusion.6 = bf16[4,2,64,4096]{3,2,0,1:T(8,128)(2,1)} fusion(bf16[4,2,64,4096]{3,2,0,1:T(8,128)(2,1)} %collective-permute-done.16, f32[4,2,2,64,4096]{4,3,2,1,0:T(8,128)} %bitcast.271, s32[]{:T(128)S(6)} %select_n.186), kind=kLoop, calls=%fused_computation.13 | loop fusion | flops 6291456 | bytes 16777220 | tf_op jit(solution)/shard_map/convert_element_type | solution.py:541
  325.9 3.8 multiply_reduce_fusion.1
  329.8 4.5 fusion.90
  334.3 2.9 fusion.45.g_ref
  337.7 4.4 fusion.52
  352.7 5.5 collective-permute-done.17
  365.5 16.0 %add_multiply_fusion.1 = f32[2,592,1024]{2,1,0:T(8,128)S(1)} fusion(f32[2,592,1024]{2,1,0:T(8,128)} %copy-done.12, f32[1024]{0:T(1024)S(1)} %copy-done.41, f32[2,592]{1,0:T(2,128)S(1)} %copy-done.39, bf16[2,592,4096]{2,1,0:T(8,128)(2,1)} %copy-done.50, bf16[1024,4096]{1,0:T(8,128)(2,1)} %copy-done.3), kind=kOutput, calls=%fused_computation.55 | convolution fusion | flops 9935749120 | bytes 27796096 | tf_op jit(solution)/shard_map/bsf,df->bsd/dot_general | solution.py:732
  397.1 47.7 %attention_backward.1 = bf16[2,592,3072]{2,1,0:T(8,128)(2,1)S(1)} custom-call(s32[2]{0:T(128)S(1)} %fusion.75.lengths, bf16[2,592,3072]{2,1,0:T(8,128)(2,1)} %add_convert_fusion.q_ref.k_ref.v_ref, bf16[2,592,3072]{2,1,0:T(8,128)(2,1)} %add_convert_fusion.q_ref.k_ref.v_ref, bf16[2,592,3072]{2,1,0:T(8,128)(2,1)} %add_convert_fusion.q_ref.k_ref.v_ref, ...), custom_call_target="tpu_custom_call" | custom-call | flops 14355005440 | bytes 16973824 | tf_op jit(solution)/shard_map/attention_backward/pallas_call | solution.py:386
  449.6 5.7 copy.74
  462.1 8.5 %fusion.103 = f32[1024,3072,1]{1,0,2:T(8,128)S(1)} fusion(bf16[2,592,1024]{2,1,0:T(8,128)(2,1)S(1)} %copy-done.24, bf16[2,592,3072]{2,1,0:T(8,128)(2,1)S(1)} %attention_backward.1), kind=kOutput, calls=%fused_computation.256 | convolution fusion | flops 7449083904 | bytes 22282240 | tf_op jit(solution)/shard_map/bsd,bsc->dc/dot_general | solution.py:743
  470.6 4.6 copy-done.20
  477.3 4.0 collective-permute-done.30
  485.3 9.7 %fusion.102 = f32[2,592,1024]{2,1,0:T(8,128)} fusion(bf16[2,592,3072]{2,1,0:T(8,128)(2,1)S(1)} %attention_backward.1, bf16[1024,3072,1]{1,0,2:T(8,128)(2,1)S(1)} %bitcast.259), kind=kOutput, calls=%fused_computation.255 | convolution fusion | flops 7449083904 | bytes 18415616 | tf_op jit(solution)/shard_map/bsc,dc->bsd/dot_general | solution.py:745
  502.3 4.1 fusion.15
  506.4 4.0 fusion.28
  516.3 3.5 fusion.27
  520.6 11.8 %collective-permute-done.41 = bf16[4,32,3072]{2,1,0:T(8,128)(2,1)S(1)} collective-permute-done((bf16[4,32,3072]{2,1,0:T(8,128)(2,1)S(1)}, bf16[4,32,3072]{2,1,0:T(8,128)(2,1)S(1)}, u32[]{:S(2)}, u32[]{:S(2)}) %collective-permute-start.41) | collective-permute-done | bytes 786464 | tf_op jit(solution)/shard_map/ppermute | solution.py:410
  547.1 8.6 %collective-permute-done.44 = bf16[4,32,1536]{2,1,0:T(8,128)(2,1)S(1)} collective-permute-done((bf16[4,32,1536]{2,1,0:T(8,128)(2,1)S(1)}, bf16[4,32,1536]{2,1,0:T(8,128)(2,1)S(1)}, u32[]{:S(2)}, u32[]{:S(2)}) %collective-permute-start.44) | collective-permute-done | bytes 393248 | tf_op jit(solution)/shard_map/ppermute | solution.py:410
  562.3 10.6 %collective-permute-done.47 = f32[4,2,1,192]{3,2,1,0:T(1,128)S(1)} collective-permute-done((f32[4,2,1,192]{3,2,1,0:T(1,128)S(1)}, f32[4,2,1,192]{3,2,1,0:T(1,128)S(1)}, u32[]{:S(2)}, u32[]{:S(2)}) %collective-permute-start.47) | collective-permute-done | bytes 6176 | tf_op jit(solution)/shard_map/ppermute | solution.py:410
  574.3 6.1 %collective-permute-done.49 = bf16[64,1536]{1,0:T(8,128)(2,1)S(1)} collective-permute-done((bf16[64,1536]{1,0:T(8,128)(2,1)S(1)}, bf16[64,1536]{1,0:T(8,128)(2,1)S(1)}, u32[]{:S(2)}, u32[]{:S(2)}) %collective-permute-start.49) | collective-permute-done | bytes 196640 | tf_op jit(solution)/shard_map/ppermute | solution.py:415
  589.0 5.7 copy.75
  (391 shorter events, 157.2 us)
Async XLA Ops:
  7.3 161.9 %all-gather.3.cloned.1.call-start = ((), (), s32[]{:S(2)}) async-start(), calls=%async_computation | async-start | bytes 10813440 | tf_op jit(solution)/shard_map/all_gather | solution.py:687
  13.0 31.9 %collective-permute-start.3 = (bf16[2,320,1024]{2,1,0:T(8,128)(2,1)S(1)}, bf16[2,320,1024]{2,1,0:T(8,128)(2,1)}, u32[]{:S(2)}, u32[]{:S(2)}) collective-permute-start(bf16[2,320,1024]{2,1,0:T(8,128)(2,1)S(1)} %bitcast.279), channel_id=1, source_target_pairs={{0,1},{1,0},{2,3},{3,2},{4,5},{5,4},{6,7},{7,6},{8,9},{9,8},{10,11... | collective-permute-start | bytes 3932168 | tf_op jit(solution)/shard_map/ppermute | solution.py:587
  16.8 9.4 %collective-permute-start.2 = (bf16[64,1664]{1,0:T(8,128)(2,1)S(1)}, bf16[64,1664]{1,0:T(8,128)(2,1)S(1)}, u32[]{:S(2)}, u32[]{:S(2)}) collective-permute-start(bf16[64,1664]{1,0:T(8,128)(2,1)S(1)} %get-tuple-element.243), channel_id=1, source_target_pairs={{0,24},{2,26},{4,28},{6,30},{8,0},{10,2},{12,4},{14,6},{16,8},{18,... | collective-permute-start | bytes 638984 | tf_op jit(solution)/shard_map/ppermute | solution.py:415
  20.4 17.9 %collective-permute-start.1 = (bf16[64,1664]{1,0:T(8,128)(2,1)S(1)}, bf16[64,1664]{1,0:T(8,128)(2,1)}, u32[]{:S(2)}, u32[]{:S(2)}) collective-permute-start(bf16[64,1664]{1,0:T(8,128)(2,1)S(1)} %get-tuple-element.243), channel_id=1, source_target_pairs={{0,16},{2,18},{4,20},{6,22},{8,24},{10,26},{12,28},{14,30},{16,0},... | collective-permute-start | bytes 638984 | tf_op jit(solution)/shard_map/ppermute | solution.py:415
  20.4 17.9 %collective-permute-start = (bf16[64,1664]{1,0:T(8,128)(2,1)S(1)}, bf16[64,1664]{1,0:T(8,128)(2,1)}, u32[]{:S(2)}, u32[]{:S(2)}) collective-permute-start(bf16[64,1664]{1,0:T(8,128)(2,1)S(1)} %get-tuple-element.243), channel_id=1, source_target_pairs={{0,8},{2,10},{4,12},{6,14},{8,16},{10,18},{12,20},{14,22},{16,24},... | collective-permute-start | bytes 638984 | tf_op jit(solution)/shard_map/ppermute | solution.py:415
  48.2 173.7 %all-gather.5.cloned.1.call-start = ((), (), s32[]{:S(2)}) async-start(), calls=%async_computation.1 | async-start | bytes 8650752 | tf_op jit(solution)/shard_map/all_gather | solution.py:690
  49.1 11.1 %collective-permute-start.4 = (bf16[4,32,1664]{2,1,0:T(8,128)(2,1)S(1)}, bf16[4,32,1664]{2,1,0:T(8,128)(2,1)S(1)}, u32[]{:S(2)}, u32[]{:S(2)}) collective-permute-start(bf16[4,32,1664]{2,1,0:T(8,128)(2,1)S(1)} %get-tuple-element.235), channel_id=1, source_target_pairs={{0,4},{2,6},{4,0},{6,2},{8,12},{10,14},{12,8},{14,10},{16,20},{18,... | collective-permute-start | bytes 1277960 | tf_op jit(solution)/shard_map/ppermute | solution.py:410
  50.9 12.9 %collective-permute-start.6 = (bf16[4,32,1664]{2,1,0:T(8,128)(2,1)S(1)}, bf16[4,32,1664]{2,1,0:T(8,128)(2,1)S(1)}, u32[]{:S(2)}, u32[]{:S(2)}) collective-permute-start(bf16[4,32,1664]{2,1,0:T(8,128)(2,1)S(1)} %get-tuple-element.234), channel_id=1, source_target_pairs={{0,1},{1,0},{2,3},{3,2},{4,5},{5,4},{6,7},{7,6},{8,9},{9,8},{10,11... | collective-permute-start | bytes 1277960 | tf_op jit(solution)/shard_map/ppermute | solution.py:410
  60.3 24.9 %collective-permute-start.5 = (bf16[2,4,32,1664]{3,2,1,0:T(8,128)(2,1)S(1)}, bf16[2,4,32,1664]{3,2,1,0:T(8,128)(2,1)S(1)}, u32[]{:S(2)}, u32[]{:S(2)}) collective-permute-start(bf16[2,4,32,1664]{3,2,1,0:T(8,128)(2,1)S(1)} %pad_maximum_fusion.3.refs_0_), channel_id=1, source_target_pairs={{0,1},{1,0},{2,3},{3,2},{4,5},{5,4},{6,7},{7,6},{8,9},{9,8},{10,11... | collective-permute-start | bytes 2555912 | tf_op jit(solution)/shard_map/ppermute | solution.py:410
  63.9 21.3 %collective-permute-start.7 = (bf16[2,4,32,1664]{3,2,1,0:T(8,128)(2,1)S(1)}, bf16[2,4,32,1664]{3,2,1,0:T(8,128)(2,1)S(1)}, u32[]{:S(2)}, u32[]{:S(2)}) collective-permute-start(bf16[2,4,32,1664]{3,2,1,0:T(8,128)(2,1)S(1)} %pad_maximum_fusion.4.refs_2_), channel_id=1, source_target_pairs={{0,4},{2,6},{4,0},{6,2},{8,12},{10,14},{12,8},{14,10},{16,20},{18,... | collective-permute-start | bytes 2555912 | tf_op jit(solution)/shard_map/ppermute | solution.py:410
  64.7 25.5 %collective-permute-start.8 = (bf16[2,4,32,1664]{3,2,1,0:T(8,128)(2,1)S(1)}, bf16[2,4,32,1664]{3,2,1,0:T(8,128)(2,1)S(1)}, u32[]{:S(2)}, u32[]{:S(2)}) collective-permute-start(bf16[2,4,32,1664]{3,2,1,0:T(8,128)(2,1)S(1)} %pad_maximum_fusion.3.refs_0_), channel_id=1, source_target_pairs={{0,2},{2,0},{4,6},{6,4},{8,10},{10,8},{12,14},{14,12},{16,18},{18,... | collective-permute-start | bytes 2555912 | tf_op jit(solution)/shard_map/ppermute | solution.py:410
  64.8 25.5 %collective-permute-start.10 = (bf16[2,4,32,1664]{3,2,1,0:T(8,128)(2,1)S(1)}, bf16[2,4,32,1664]{3,2,1,0:T(8,128)(2,1)S(1)}, u32[]{:S(2)}, u32[]{:S(2)}) collective-permute-start(bf16[2,4,32,1664]{3,2,1,0:T(8,128)(2,1)S(1)} %pad_maximum_fusion.4.refs_2_), channel_id=1, source_target_pairs={{0,2},{2,0},{4,6},{6,4},{8,10},{10,8},{12,14},{14,12},{16,18},{18,... | collective-permute-start | bytes 2555912 | tf_op jit(solution)/shard_map/ppermute | solution.py:410
  119.1 44.2 %collective-permute-start.12 = (bf16[2,320,1024]{2,1,0:T(8,128)(2,1)}, bf16[2,320,1024]{2,1,0:T(8,128)(2,1)}, u32[]{:S(2)}, u32[]{:S(2)}) collective-permute-start(bf16[2,320,1024]{2,1,0:T(8,128)(2,1)} %dynamic-slice_bitcast_fusion), channel_id=1, source_target_pairs={{0,1},{1,0},{2,3},{3,2},{4,5},{5,4},{6,7},{7,6},{8,9},{9,8},{10,11... | collective-permute-start | bytes 3932168 | tf_op jit(solution)/shard_map/ppermute | solution.py:587
  236.4 40.2 %collective-permute-start.13 = (bf16[4,2,64,4096]{3,2,0,1:T(8,128)(2,1)}, bf16[4,2,64,4096]{3,2,0,1:T(8,128)(2,1)S(1)}, u32[]{:S(2)}, u32[]{:S(2)}) collective-permute-start(bf16[4,2,64,4096]{3,2,0,1:T(8,128)(2,1)} %fusion.31), channel_id=1, source_target_pairs={{0,2},{2,0},{4,6},{6,4},{8,10},{10,8},{12,14},{14,12},{16,18},{18,... | collective-permute-start | bytes 12582920 | tf_op jit(solution)/shard_map/ppermute | solution.py:410
  282.1 25.4 %collective-permute-start.14 = (bf16[4,2,32,2048]{3,2,0,1:T(8,128)(2,1)S(1)}, bf16[4,2,32,2048]{3,2,0,1:T(8,128)(2,1)S(1)}, u32[]{:S(2)}, u32[]{:S(2)}) collective-permute-start(bf16[4,2,32,2048]{3,2,0,1:T(8,128)(2,1)S(1)} %constant_dynamic-slice_fusion.29), channel_id=1, source_target_pairs={{0,1},{1,0},{2,3},{3,2},{4,5},{5,4},{6,7},{7,6},{8,9},{9,8},{10,11... | collective-permute-start | bytes 3145736 | tf_op jit(solution)/shard_map/ppermute | solution.py:410
  290.0 27.5 %collective-permute-start.16 = (bf16[4,2,64,4096]{3,2,0,1:T(8,128)(2,1)}, bf16[4,2,64,4096]{3,2,0,1:T(8,128)(2,1)}, u32[]{:S(2)}, u32[]{:S(2)}) collective-permute-start(bf16[4,2,64,4096]{3,2,0,1:T(8,128)(2,1)} %fusion.32), channel_id=1, source_target_pairs={{0,2},{2,0},{4,6},{6,4},{8,10},{10,8},{12,14},{14,12},{16,18},{18,... | collective-permute-start | bytes 12582920 | tf_op jit(solution)/shard_map/ppermute | solution.py:410
  290.3 25.5 %collective-permute-start.15 = (bf16[4,32,4096]{2,1,0:T(8,128)(2,1)S(1)}, bf16[4,32,4096]{2,1,0:T(8,128)(2,1)}, u32[]{:S(2)}, u32[]{:S(2)}) collective-permute-start(bf16[4,32,4096]{2,1,0:T(8,128)(2,1)S(1)} %dynamic-slice_bitcast_fusion.2), channel_id=1, source_target_pairs={{0,4},{2,6},{4,0},{6,2},{8,12},{10,14},{12,8},{14,10},{16,20},{18,... | collective-permute-start | bytes 3145736 | tf_op jit(solution)/shard_map/ppermute | solution.py:410
  343.0 15.2 %collective-permute-start.17 = (bf16[4,32,2048]{2,1,0:T(8,128)(2,1)}, bf16[4,32,2048]{2,1,0:T(8,128)(2,1)}, u32[]{:S(2)}, u32[]{:S(2)}) collective-permute-start(bf16[4,32,2048]{2,1,0:T(8,128)(2,1)} %dynamic-slice_bitcast_fusion.5), channel_id=1, source_target_pairs={{0,4},{2,6},{4,0},{6,2},{8,12},{10,14},{12,8},{14,10},{16,20},{18,... | collective-permute-start | bytes 1572872 | tf_op jit(solution)/shard_map/ppermute | solution.py:410
  344.7 15.1 %collective-permute-start.18 = (bf16[4,32,2048]{2,1,0:T(8,128)(2,1)}, bf16[4,32,2048]{2,1,0:T(8,128)(2,1)S(1)}, u32[]{:S(2)}, u32[]{:S(2)}) collective-permute-start(bf16[4,32,2048]{2,1,0:T(8,128)(2,1)} %constant_dynamic-slice_fusion.27), channel_id=1, source_target_pairs={{0,1},{1,0},{2,3},{3,2},{4,5},{5,4},{6,7},{7,6},{8,9},{9,8},{10,11... | collective-permute-start | bytes 1572872 | tf_op jit(solution)/shard_map/ppermute | solution.py:410
  347.6 38.7 %collective-permute-start.22 = (bf16[4,2,32,2048]{3,2,0,1:T(8,128)(2,1)}, bf16[4,2,32,2048]{3,2,0,1:T(8,128)(2,1)}, u32[]{:S(2)}, u32[]{:S(2)}) collective-permute-start(bf16[4,2,32,2048]{3,2,0,1:T(8,128)(2,1)} %constant_dynamic-slice_fusion.26), channel_id=1, source_target_pairs={{0,1},{1,0},{2,3},{3,2},{4,5},{5,4},{6,7},{7,6},{8,9},{9,8},{10,11... | collective-permute-start | bytes 3145736 | tf_op jit(solution)/shard_map/ppermute | solution.py:410
  349.5 38.6 %collective-permute-start.23 = (bf16[4,32,4096]{2,1,0:T(8,128)(2,1)}, bf16[4,32,4096]{2,1,0:T(8,128)(2,1)}, u32[]{:S(2)}, u32[]{:S(2)}) collective-permute-start(bf16[4,32,4096]{2,1,0:T(8,128)(2,1)} %dynamic-slice_bitcast_fusion.1), channel_id=1, source_target_pairs={{0,4},{2,6},{4,0},{6,2},{8,12},{10,14},{12,8},{14,10},{16,20},{18,... | collective-permute-start | bytes 3145736 | tf_op jit(solution)/shard_map/ppermute | solution.py:410
  361.1 20.3 %collective-permute-start.21 = (bf16[64,2048]{1,0:T(8,128)(2,1)S(1)}, bf16[64,2048]{1,0:T(8,128)(2,1)S(1)}, u32[]{:S(2)}, u32[]{:S(2)}) collective-permute-start(bf16[64,2048]{1,0:T(8,128)(2,1)S(1)} %get-tuple-element.230), channel_id=1, source_target_pairs={{0,24},{2,26},{4,28},{6,30},{8,0},{10,2},{12,4},{14,6},{16,8},{18,... | collective-permute-start | bytes 786440 | tf_op jit(solution)/shard_map/ppermute | solution.py:415
  363.1 21.2 %collective-permute-start.20 = (bf16[64,2048]{1,0:T(8,128)(2,1)S(1)}, bf16[64,2048]{1,0:T(8,128)(2,1)}, u32[]{:S(2)}, u32[]{:S(2)}) collective-permute-start(bf16[64,2048]{1,0:T(8,128)(2,1)S(1)} %get-tuple-element.231), channel_id=1, source_target_pairs={{0,16},{2,18},{4,20},{6,22},{8,24},{10,26},{12,28},{14,30},{16,0},... | collective-permute-start | bytes 786440 | tf_op jit(solution)/shard_map/ppermute | solution.py:415
  364.1 20.2 %collective-permute-start.19 = (bf16[64,2048]{1,0:T(8,128)(2,1)S(1)}, bf16[64,2048]{1,0:T(8,128)(2,1)}, u32[]{:S(2)}, u32[]{:S(2)}) collective-permute-start(bf16[64,2048]{1,0:T(8,128)(2,1)S(1)} %get-tuple-element.229), channel_id=1, source_target_pairs={{0,8},{2,10},{4,12},{6,14},{8,16},{10,18},{12,20},{14,22},{16,24},... | collective-permute-start | bytes 786440 | tf_op jit(solution)/shard_map/ppermute | solution.py:415
  390.0 55.1 %collective-permute-start.25 = (bf16[2,160,1024]{2,1,0:T(8,128)(2,1)S(1)}, bf16[2,160,1024]{2,1,0:T(8,128)(2,1)S(1)}, u32[]{:S(2)}, u32[]{:S(2)}) collective-permute-start(bf16[2,160,1024]{2,1,0:T(8,128)(2,1)S(1)} %get-tuple-element.223), channel_id=1, source_target_pairs={{0,1},{1,0},{2,3},{3,2},{4,5},{5,4},{6,7},{7,6},{8,9},{9,8},{10,11... | collective-permute-start | bytes 1966088 | tf_op jit(solution)/shard_map/ppermute | solution.py:410
  391.2 53.9 %collective-permute-start.24 = (bf16[2,160,1024]{2,1,0:T(8,128)(2,1)S(1)}, bf16[2,160,1024]{2,1,0:T(8,128)(2,1)S(1)}, u32[]{:S(2)}, u32[]{:S(2)}) collective-permute-start(bf16[2,160,1024]{2,1,0:T(8,128)(2,1)S(1)} %get-tuple-element.222), channel_id=1, source_target_pairs={{0,1},{1,0},{2,3},{3,2},{4,5},{5,4},{6,7},{7,6},{8,9},{9,8},{10,11... | collective-permute-start | bytes 1966088 | tf_op jit(solution)/shard_map/ppermute | solution.py:410
  392.1 52.6 %collective-permute-start.26 = (bf16[4,32,2048]{2,1,0:T(8,128)(2,1)S(1)}, bf16[4,32,2048]{2,1,0:T(8,128)(2,1)S(1)}, u32[]{:S(2)}, u32[]{:S(2)}) collective-permute-start(bf16[4,32,2048]{2,1,0:T(8,128)(2,1)S(1)} %dynamic-slice_bitcast_fusion.4), channel_id=1, source_target_pairs={{0,4},{2,6},{4,0},{6,2},{8,12},{10,14},{12,8},{14,10},{16,20},{18,... | collective-permute-start | bytes 1572872 | tf_op jit(solution)/shard_map/ppermute | solution.py:410
  393.4 51.5 %collective-permute-start.27 = (bf16[4,32,2048]{2,1,0:T(8,128)(2,1)S(1)}, bf16[4,32,2048]{2,1,0:T(8,128)(2,1)S(1)}, u32[]{:S(2)}, u32[]{:S(2)}) collective-permute-start(bf16[4,32,2048]{2,1,0:T(8,128)(2,1)S(1)} %constant_dynamic-slice_fusion.25), channel_id=1, source_target_pairs={{0,1},{1,0},{2,3},{3,2},{4,5},{5,4},{6,7},{7,6},{8,9},{9,8},{10,11... | collective-permute-start | bytes 1572872 | tf_op jit(solution)/shard_map/ppermute | solution.py:410
  397.1 49.2 %collective-permute-start.28 = (bf16[4,2,64,1024]{3,2,0,1:T(8,128)(2,1)}, bf16[4,2,64,1024]{3,2,0,1:T(8,128)(2,1)}, u32[]{:S(2)}, u32[]{:S(2)}) collective-permute-start(bf16[4,2,64,1024]{3,2,0,1:T(8,128)(2,1)} %fusion.55), channel_id=1, source_target_pairs={{0,2},{2,0},{4,6},{6,4},{8,10},{10,8},{12,14},{14,12},{16,18},{18,... | collective-permute-start | bytes 3145736 | tf_op jit(solution)/shard_map/ppermute | solution.py:410
  455.6 21.8 %collective-permute-start.31 = (bf16[64,2048]{1,0:T(8,128)(2,1)S(1)}, bf16[64,2048]{1,0:T(8,128)(2,1)S(1)}, u32[]{:S(2)}, u32[]{:S(2)}) collective-permute-start(bf16[64,2048]{1,0:T(8,128)(2,1)S(1)} %get-tuple-element.227), channel_id=1, source_target_pairs={{0,24},{2,26},{4,28},{6,30},{8,0},{10,2},{12,4},{14,6},{16,8},{18,... | collective-permute-start | bytes 786440 | tf_op jit(solution)/shard_map/ppermute | solution.py:415
  455.8 25.5 %collective-permute-start.30 = (bf16[64,2048]{1,0:T(8,128)(2,1)S(1)}, bf16[64,2048]{1,0:T(8,128)(2,1)S(1)}, u32[]{:S(2)}, u32[]{:S(2)}) collective-permute-start(bf16[64,2048]{1,0:T(8,128)(2,1)S(1)} %get-tuple-element.228), channel_id=1, source_target_pairs={{0,16},{2,18},{4,20},{6,22},{8,24},{10,26},{12,28},{14,30},{16,0},... | collective-permute-start | bytes 786440 | tf_op jit(solution)/shard_map/ppermute | solution.py:415
  457.6 23.8 %collective-permute-start.29 = (bf16[64,2048]{1,0:T(8,128)(2,1)S(1)}, bf16[64,2048]{1,0:T(8,128)(2,1)S(1)}, u32[]{:S(2)}, u32[]{:S(2)}) collective-permute-start(bf16[64,2048]{1,0:T(8,128)(2,1)S(1)} %get-tuple-element.226), channel_id=1, source_target_pairs={{0,8},{2,10},{4,12},{6,14},{8,16},{10,18},{12,20},{14,22},{16,24},... | collective-permute-start | bytes 786440 | tf_op jit(solution)/shard_map/ppermute | solution.py:415
  459.8 22.6 %collective-permute-start.32 = (bf16[4,2,32,512]{3,2,0,1:T(8,128)(2,1)S(1)}, bf16[4,2,32,512]{3,2,0,1:T(8,128)(2,1)S(1)}, u32[]{:S(2)}, u32[]{:S(2)}) collective-permute-start(bf16[4,2,32,512]{3,2,0,1:T(8,128)(2,1)S(1)} %constant_dynamic-slice_fusion.23), channel_id=1, source_target_pairs={{0,1},{1,0},{2,3},{3,2},{4,5},{5,4},{6,7},{7,6},{8,9},{9,8},{10,11... | collective-permute-start | bytes 786440 | tf_op jit(solution)/shard_map/ppermute | solution.py:410
  461.1 21.1 %collective-permute-start.33 = (bf16[4,32,1024]{2,1,0:T(8,128)(2,1)S(1)}, bf16[4,32,1024]{2,1,0:T(8,128)(2,1)S(1)}, u32[]{:S(2)}, u32[]{:S(2)}) collective-permute-start(bf16[4,32,1024]{2,1,0:T(8,128)(2,1)S(1)} %dynamic-slice_bitcast_fusion.7), channel_id=1, source_target_pairs={{0,4},{2,6},{4,0},{6,2},{8,12},{10,14},{12,8},{14,10},{16,20},{18,... | collective-permute-start | bytes 786440 | tf_op jit(solution)/shard_map/ppermute | solution.py:410
  477.3 24.9 %collective-permute-start.36 = (bf16[4,2,64,3072]{3,2,0,1:T(8,128)(2,1)}, bf16[4,2,64,3072]{3,2,0,1:T(8,128)(2,1)S(1)}, u32[]{:S(2)}, u32[]{:S(2)}) collective-permute-start(bf16[4,2,64,3072]{3,2,0,1:T(8,128)(2,1)} %fusion.33), channel_id=1, source_target_pairs={{0,2},{2,0},{4,6},{6,4},{8,10},{10,8},{12,14},{14,12},{16,18},{18,... | collective-permute-start | bytes 9437192 | tf_op jit(solution)/shard_map/ppermute | solution.py:410
  483.1 16.5 %collective-permute-start.34 = (bf16[4,32,512]{2,1,0:T(8,128)(2,1)}, bf16[4,32,512]{2,1,0:T(8,128)(2,1)S(1)}, u32[]{:S(2)}, u32[]{:S(2)}) collective-permute-start(bf16[4,32,512]{2,1,0:T(8,128)(2,1)} %dynamic-slice_bitcast_fusion.17), channel_id=1, source_target_pairs={{0,4},{2,6},{4,0},{6,2},{8,12},{10,14},{12,8},{14,10},{16,20},{18,... | collective-permute-start | bytes 393224 | tf_op jit(solution)/shard_map/ppermute | solution.py:410
  510.5 9.3 %collective-permute-start.39 = (bf16[64,512]{1,0:T(8,128)(2,1)S(1)}, bf16[64,512]{1,0:T(8,128)(2,1)S(1)}, u32[]{:S(2)}, u32[]{:S(2)}) collective-permute-start(bf16[64,512]{1,0:T(8,128)(2,1)S(1)} %get-tuple-element.240), channel_id=1, source_target_pairs={{0,24},{2,26},{4,28},{6,30},{8,0},{10,2},{12,4},{14,6},{16,8},{18,... | collective-permute-start | bytes 196616 | tf_op jit(solution)/shard_map/ppermute | solution.py:415
  514.1 18.5 %collective-permute-start.40 = (bf16[4,2,32,1536]{3,2,0,1:T(8,128)(2,1)S(1)}, bf16[4,2,32,1536]{3,2,0,1:T(8,128)(2,1)S(1)}, u32[]{:S(2)}, u32[]{:S(2)}) collective-permute-start(bf16[4,2,32,1536]{3,2,0,1:T(8,128)(2,1)S(1)} %constant_dynamic-slice_fusion.19), channel_id=1, source_target_pairs={{0,1},{1,0},{2,3},{3,2},{4,5},{5,4},{6,7},{7,6},{8,9},{9,8},{10,11... | collective-permute-start | bytes 2359304 | tf_op jit(solution)/shard_map/ppermute | solution.py:410
  515.1 17.3 %collective-permute-start.41 = (bf16[4,32,3072]{2,1,0:T(8,128)(2,1)S(1)}, bf16[4,32,3072]{2,1,0:T(8,128)(2,1)S(1)}, u32[]{:S(2)}, u32[]{:S(2)}) collective-permute-start(bf16[4,32,3072]{2,1,0:T(8,128)(2,1)S(1)} %dynamic-slice_bitcast_fusion.3), channel_id=1, source_target_pairs={{0,4},{2,6},{4,0},{6,2},{8,12},{10,14},{12,8},{14,10},{16,20},{18,... | collective-permute-start | bytes 2359304 | tf_op jit(solution)/shard_map/ppermute | solution.py:410
  533.2 23.4 %collective-permute-start.42 = (bf16[2,160,1024]{2,1,0:T(8,128)(2,1)S(1)}, bf16[2,160,1024]{2,1,0:T(8,128)(2,1)S(1)}, u32[]{:S(2)}, u32[]{:S(2)}) collective-permute-start(bf16[2,160,1024]{2,1,0:T(8,128)(2,1)S(1)} %get-tuple-element.221), channel_id=1, source_target_pairs={{0,1},{1,0},{2,3},{3,2},{4,5},{5,4},{6,7},{7,6},{8,9},{9,8},{10,11... | collective-permute-start | bytes 1966088 | tf_op jit(solution)/shard_map/ppermute | solution.py:410
  544.1 11.6 %collective-permute-start.44 = (bf16[4,32,1536]{2,1,0:T(8,128)(2,1)S(1)}, bf16[4,32,1536]{2,1,0:T(8,128)(2,1)S(1)}, u32[]{:S(2)}, u32[]{:S(2)}) collective-permute-start(bf16[4,32,1536]{2,1,0:T(8,128)(2,1)S(1)} %dynamic-slice_bitcast_fusion.6), channel_id=1, source_target_pairs={{0,4},{2,6},{4,0},{6,2},{8,12},{10,14},{12,8},{14,10},{16,20},{18,... | collective-permute-start | bytes 1179656 | tf_op jit(solution)/shard_map/ppermute | solution.py:410
  545.2 11.3 %collective-permute-start.45 = (bf16[4,32,1536]{2,1,0:T(8,128)(2,1)S(1)}, bf16[4,32,1536]{2,1,0:T(8,128)(2,1)S(1)}, u32[]{:S(2)}, u32[]{:S(2)}) collective-permute-start(bf16[4,32,1536]{2,1,0:T(8,128)(2,1)S(1)} %constant_dynamic-slice_fusion.17), channel_id=1, source_target_pairs={{0,1},{1,0},{2,3},{3,2},{4,5},{5,4},{6,7},{7,6},{8,9},{9,8},{10,11... | collective-permute-start | bytes 1179656 | tf_op jit(solution)/shard_map/ppermute | solution.py:410
  556.6 23.8 %collective-permute-start.46 = (bf16[2,160,1024]{2,1,0:T(8,128)(2,1)S(1)}, bf16[2,160,1024]{2,1,0:T(8,128)(2,1)S(1)}, u32[]{:S(2)}, u32[]{:S(2)}) collective-permute-start(bf16[2,160,1024]{2,1,0:T(8,128)(2,1)S(1)} %get-tuple-element.141), channel_id=1, source_target_pairs={{0,1},{1,0},{2,3},{3,2},{4,5},{5,4},{6,7},{7,6},{8,9},{9,8},{10,11... | collective-permute-start | bytes 1966088 | tf_op jit(solution)/shard_map/ppermute | solution.py:410
  557.9 15.0 %collective-permute-start.47 = (f32[4,2,1,192]{3,2,1,0:T(1,128)S(1)}, f32[4,2,1,192]{3,2,1,0:T(1,128)S(1)}, u32[]{:S(2)}, u32[]{:S(2)}) collective-permute-start(f32[4,2,1,192]{3,2,1,0:T(1,128)S(1)} %constant_dynamic-slice_fusion.15), channel_id=1, source_target_pairs={{0,1},{1,0},{2,3},{3,2},{4,5},{5,4},{6,7},{7,6},{8,9},{9,8},{10,11... | collective-permute-start | bytes 18440 | tf_op jit(solution)/shard_map/ppermute | solution.py:410
  558.9 14.8 %collective-permute-start.48 = (f32[4,1,384]{2,1,0:T(1,128)S(1)}, f32[4,1,384]{2,1,0:T(1,128)S(1)}, u32[]{:S(2)}, u32[]{:S(2)}) collective-permute-start(f32[4,1,384]{2,1,0:T(1,128)S(1)} %fusion.74), channel_id=1, source_target_pairs={{0,4},{2,6},{4,0},{6,2},{8,12},{10,14},{12,8},{14,10},{16,20},{18,... | collective-permute-start | bytes 18440 | tf_op jit(solution)/shard_map/ppermute | solution.py:410
  560.1 13.6 %collective-permute-start.51 = (bf16[64,1536]{1,0:T(8,128)(2,1)S(1)}, bf16[64,1536]{1,0:T(8,128)(2,1)S(1)}, u32[]{:S(2)}, u32[]{:S(2)}) collective-permute-start(bf16[64,1536]{1,0:T(8,128)(2,1)S(1)} %get-tuple-element.237), channel_id=1, source_target_pairs={{0,24},{2,26},{4,28},{6,30},{8,0},{10,2},{12,4},{14,6},{16,8},{18,... | collective-permute-start | bytes 589832 | tf_op jit(solution)/shard_map/ppermute | solution.py:415
  562.3 12.0 %collective-permute-start.50 = (bf16[64,1536]{1,0:T(8,128)(2,1)S(1)}, bf16[64,1536]{1,0:T(8,128)(2,1)S(1)}, u32[]{:S(2)}, u32[]{:S(2)}) collective-permute-start(bf16[64,1536]{1,0:T(8,128)(2,1)S(1)} %get-tuple-element.238), channel_id=1, source_target_pairs={{0,16},{2,18},{4,20},{6,22},{8,24},{10,26},{12,28},{14,30},{16,0},... | collective-permute-start | bytes 589832 | tf_op jit(solution)/shard_map/ppermute | solution.py:415
  585.2 10.8 %collective-permute-start.56 = (f32[2,192]{1,0:T(2,128)S(1)}, f32[2,192]{1,0:T(2,128)S(1)}, u32[]{:S(2)}, u32[]{:S(2)}) collective-permute-start(f32[2,192]{1,0:T(2,128)S(1)} %get-tuple-element.256), channel_id=1, source_target_pairs={{0,24},{2,26},{4,28},{6,30},{8,0},{10,2},{12,4},{14,6},{16,8},{18,... | collective-permute-start | bytes 4616 | tf_op jit(solution)/shard_map/ppermute | solution.py:415
  (76 other events, 749.1 us)
Sparse Core Ops, SparseCore 0:
  48.3 91.7 all-gather.2
  143.0 78.9 all-gather.4

commit v5 on v4

--- a/solution.py
+++ b/solution.py
@@ -10,6 +10,7 @@
 HD = 64
 PAIR = 2 * HD
 VALID = 577
+SURE = 288
 F32 = jnp.float32
 BF16 = jnp.bfloat16
 
@@ -287,18 +288,23 @@
     return lax.dot_general(a, b, NT, preferred_element_type=F32)
 
 
+def where_key(length, values, filler):
+    rest = values[SURE:]
+    slot = lax.broadcasted_iota(jnp.int32, rest.shape, 0) + SURE
+    return jnp.concatenate([values[:SURE], jnp.where(slot < length, rest, filler)], axis=0)
+
+
 def attention_forward_kernel(lengths, q_ref, k_ref, v_ref, o_ref, lse_ref, *, key_rows):
     length = lengths[pl.program_id(0)]
     queries = q_ref[0] * jnp.asarray(HD**-0.5, BF16)
     keys = k_ref[0, :key_rows]
     values_t = jnp.transpose(v_ref[0, :key_rows].astype(F32)).astype(BF16)
     lane = lax.broadcasted_iota(jnp.int32, (key_rows, PAIR), 1)
-    valid = lax.broadcasted_iota(jnp.int32, (key_rows, q_ref.shape[1]), 0) < length
     outs = []
     for head in range(2):
         own = (lane >= head * HD) & (lane < (head + 1) * HD)
         scores = dot_nt(jnp.where(own, keys, jnp.zeros_like(keys)), queries)
-        scores = jnp.where(valid, scores, masked_score)
+        scores = where_key(length, scores, masked_score)
         top = jnp.max(scores, axis=0, keepdims=True)
         exps = jnp.exp(scores - top)
         total = jnp.sum(exps, axis=0, keepdims=True)
@@ -321,13 +327,12 @@
     grads = g_ref[0]
     keys_t = jnp.transpose(keys.astype(F32)).astype(BF16)
     lane = lax.broadcasted_iota(jnp.int32, (key_rows, PAIR), 1)
-    valid = lax.broadcasted_iota(jnp.int32, (key_rows, slots), 0) < length
     zero = jnp.zeros_like(keys)
     dqs, dks, dvs = [], [], []
     for head in range(2):
         own = (lane >= head * HD) & (lane < (head + 1) * HD)
         scores = dot_nt(jnp.where(own, keys, zero), queries)
-        soft = jnp.where(valid, jnp.exp(scores - lse_ref[0, 0, head : head + 1, :]), 0.0)
+        soft = where_key(length, jnp.exp(scores - lse_ref[0, 0, head : head + 1, :]), 0.0)
         prob_grad = dot_nt(jnp.where(own, values, zero), grads)
         inner = jnp.sum(prob_grad * soft, axis=0, keepdims=True)
         score_grad = (soft * (prob_grad - inner)).astype(BF16)

time: 612 us -> 611 us (level)
  no operation moved by 1% of the time
where the time goes in v5:
time: 611 us; the launch traced here: 604 us
  matrix products  146 us (24%)
  waiting for transfers between devices  119 us (19%)
  local copies, waits for them, and re-layouts  104 us (17%)
  Pallas kernels  86.2 us (14%)
  other arithmetic  72.1 us (12%)
  starting transfers between devices  60.2 us (10%)
  between operations  16 us (3%)
    ppermute x37, waiting for transfers between devices, swap(): lax.ppermute(array, axis, [(n, n ^ step) for n in range(lax.axis_size(axi...  78.8 us
    pallas_call x1, Pallas kernels, attention_backward(): pl.pallas_call(functools.partial(attention_backward_kernel, key_rows=key_...  46.4 us
    unnamed x137, local copies, waits for them, and re-layouts  37.5 us
    ppermute x37, starting transfers between devices, swap(): lax.ppermute(array, axis, [(n, n ^ step) for n in range(lax.axis_size(axi...  31.9 us
    pallas_call x1, Pallas kernels, attention_forward(): pl.pallas_call(functools.partial(attention_forward_kernel, key_rows=key_c...  30.8 us
    ppermute x18, waiting for transfers between devices, shift(): lax.ppermute(array, 'dp', [(n, (n + 4 * by) % count) for n in range(count)])  27.3 us
    convert_element_type x12, other arithmetic, over_pair(): return (take(array, mine, dim).astype(F32) + came).astype(self.sent)  24.8 us
    ppermute x18, starting transfers between devices, shift(): lax.ppermute(array, 'dp', [(n, (n + 4 * by) % count) for n in range(count)])  22.1 us
  transfers between devices with their start and end apart: 59, of which 22 were waited for; matrix products, arithmetic and copies ran while one was open for 38% of the time, Pallas kernels for 14%

profile of v5, /device:TPU:0, one launch (start us, length us, event | category | flops | bytes accessed | tf_op | source)
XLA Modules:
  0.0 603.8 jit_solution(9724519259099759046)
XLA Ops:
  7.3 5.3 constant_dynamic-slice_fusion.31
  13.0 3.0 collective-permute-start.3
  16.8 3.7 collective-permute-start.2
  26.1 12.2 %collective-permute-done.1 = bf16[64,1664]{1,0:T(8,128)(2,1)} collective-permute-done((bf16[64,1664]{1,0:T(8,128)(2,1)S(1)}, bf16[64,1664]{1,0:T(8,128)(2,1)}, u32[]{:S(2)}, u32[]{:S(2)}) %collective-permute-start.1) | collective-permute-done | bytes 213024 | tf_op jit(solution)/shard_map/ppermute | solution.py:420
  39.5 5.4 collective-permute-done.3
  52.4 7.8 %collective-permute-done.4 = bf16[4,32,1664]{2,1,0:T(8,128)(2,1)S(1)} collective-permute-done((bf16[4,32,1664]{2,1,0:T(8,128)(2,1)S(1)}, bf16[4,32,1664]{2,1,0:T(8,128)(2,1)S(1)}, u32[]{:S(2)}, u32[]{:S(2)}) %collective-permute-start.4) | collective-permute-done | bytes 426016 | tf_op jit(solution)/shard_map/ppermute | solution.py:415
  65.3 19.9 %collective-permute-done.5.refs_1_ = bf16[2,4,32,1664]{3,2,1,0:T(8,128)(2,1)S(1)} collective-permute-done((bf16[2,4,32,1664]{3,2,1,0:T(8,128)(2,1)S(1)}, bf16[2,4,32,1664]{3,2,1,0:T(8,128)(2,1)S(1)}, u32[]{:S(2)}, u32[]{:S(2)}) %collective-permute-start.5) | collective-permute-done | bytes 852000 | tf_op jit(solution)/shard_map/ppermute | solution.py:415
  90.3 4.4 assemble.1
  101.1 14.1 %add_convert_fusion.q_ref.k_ref.v_ref = bf16[2,592,3072]{2,1,0:T(8,128)(2,1)} fusion(f32[3072]{0:T(1024)S(1)} %add.407, bf16[2,592,1024]{2,1,0:T(8,128)(2,1)S(1)} %fusion.23, bf16[1024,3072,1]{1,0,2:T(8,128)(2,1)} %bitcast.256), kind=kOutput, calls=%fused_computation.11 | convolution fusion | flops 7456358400 | bytes 16003072 | tf_op jit(solution)/shard_map/bsd,dc->bsc/dot_general | solution.py:705
  119.1 3.2 collective-permute-start.12
  122.5 3.6 multiply_reduce_fusion
  128.3 3.1 copy-done
  131.4 30.8 %attention_forward.1 = (bf16[2,592,1024]{2,1,0:T(8,128)(2,1)S(1)}, f32[2,8,2,592]{3,2,1,0:T(2,128)S(1)}) custom-call(s32[2]{0:T(128)S(1)} %fusion.75.lengths, bf16[2,592,3072]{2,1,0:T(8,128)(2,1)S(1)} %copy-done, bf16[2,592,3072]{2,1,0:T(8,128)(2,1)S(1)} %copy-done, bf16[2,592,3072]{2,1,0:T(8,128)(2,1)S(1)} %copy-done), custom_call_target="tpu_custom_call" | custom-call | flops 5742002176 | bytes 9699328 | tf_op jit(solution)/shard_map/attention_forward/pallas_call | solution.py:362
  167.9 4.2 copy-done.1
  174.8 6.6 %fusion.100 = (f32[2,592]{1,0:T(2,128)S(1)}, f32[2,592,1024]{2,1,0:T(8,128)S(1)}) fusion(f32[1024]{0:T(1024)S(1)} %add.411, bf16[2,592,1024]{2,1,0:T(8,128)(2,1)S(1)} %get-tuple-element.98, bf16[1024,1024]{1,0:T(8,128)(2,1)S(1)} %beside.3, bf16[2,640,1024]{2,1,0:T(8,128)(2,1)} %constant_dynamic-update-slice_fusion.1), kind=kOutput, calls=%fused_computation.253 | convolution fusion | flops 2487876352 | bytes 11805312 | tf_op jit(solution)/shard_map/bsc,dc->bsd/dot_general | solution.py:709
  182.2 15.3 %multiply_convert_fusion = (bf16[2,592,4096]{2,1,0:T(8,128)(2,1)S(1)}, f32[2,592,4096]{2,1,0:T(8,128)}) fusion(f32[4096]{0:T(1024)S(1)} %bitcast.290, bf16[1024,4096]{1,0:T(8,128)(2,1)S(1)} %beside.4, f32[2,592,1024]{2,1,0:T(8,128)S(1)} %get-tuple-element.266, f32[1024]{0:T(1024)S(1)} %add.415, f32[1024]{0:T(1024)S(1)} %mul.225, ...), kind=kOutput, calls=%fused_computation.8 | convolution fusion | flops 9967271936 | bytes 42370304 | tf_op jit(solution)/shard_map/bsd,df->bsf/dot_general | solution.py:713
  197.4 3.7 copy-done.50
  201.2 14.3 %fusion.101 = f32[1024,4096,1]{1,0,2:T(8,128)} fusion(bf16[2,592,1024]{2,1,0:T(8,128)(2,1)S(1)} %copy-done.25, bf16[2,592,4096]{2,1,0:T(8,128)(2,1)S(1)} %get-tuple-element.112), kind=kOutput, calls=%fused_computation.254 | convolution fusion | flops 9932111872 | bytes 28901376 | tf_op jit(solution)/shard_map/bsd,bsf->df/dot_general | solution.py:718
  215.5 6.6 %all-gather.5.cloned.1.call-done = bf16[2048,2048]{1,0:T(8,128)(2,1)} async-done(((bf16[64,2048]{1,0:T(8,128)(2,1)}), bf16[2048,2048]{1,0:T(8,128)(2,1)}) %all-gather.5.cloned.1.call-update) | async-done | bytes 8388624 | tf_op jit(solution)/shard_map/all_gather | solution.py:695
  222.0 3.4 copy-done.2
  227.4 9.1 %fusion.31 = bf16[4,2,64,4096]{3,2,0,1:T(8,128)(2,1)} fusion(s32[]{:T(128)S(6)} %select_n.187, f32[4,2,2,64,4096]{4,3,2,1,0:T(8,128)} %bitcast.272), kind=kLoop, calls=%fused_computation.64 | loop fusion | bytes 8388612 | tf_op jit(solution)/shard_map/convert_element_type | solution.py:545
  236.8 21.6 %convert_reduce_fusion = (f32[4096]{0:T(1024)}, bf16[2,592,4096]{2,1,0:T(8,128)(2,1)}) fusion(f32[2,592,4096]{2,1,0:T(8,128)} %get-tuple-element.268, f32[4096]{0:T(1024)S(1)} %bitcast.291, bf16[2,592,1024]{2,1,0:T(8,128)(2,1)S(1)} %copy-done.25, bf16[1024,4096]{1,0:T(8,128)(2,1)S(1)} %beside.5), kind=kOutput, calls=%fused_computation.7 | convolution fusion | flops 9995153408 | bytes 39944192 | tf_op jit(solution)/shard_map/bsd,df->bsf/dot_general | solution.py:721
  258.4 18.3 %fusion.69 = f32[1024,4096,1]{1,0,2:T(8,128)} fusion(bf16[2,592,4096]{2,1,0:T(8,128)(2,1)} %get-tuple-element.105, f32[2,592,1024]{2,1,0:T(8,128)S(1)} %bitcast.261, f32[1024]{0:T(1024)S(1)} %add.415, f32[1024]{0:T(1024)S(1)} %mul.225, f32[2,592]{1,0:T(2,128)S(1)} %add_rsqrt_fusion, f32[2,592]{1,0:T(2,128)S(1)} %broadcast_multiply_fusion.4), kind=kOutput, calls=%fused_computation.154 | convolution fusion | flops 9938173952 | bytes 31343872 | tf_op jit(solution)/shard_map/bsd,bsf->df/dot_general | solution.py:723
  276.7 4.9 fusion.7
  283.8 6.3 %fusion.32 = bf16[4,2,64,4096]{3,2,0,1:T(8,128)(2,1)} fusion(s32[]{:T(128)S(6)} %select_n.187, f32[4,2,2,64,4096]{4,3,2,1,0:T(8,128)} %bitcast.270), kind=kLoop, calls=%fused_computation.65 | loop fusion | bytes 8388612 | tf_op jit(solution)/shard_map/convert_element_type | solution.py:545
  291.1 14.4 %fusion.11 = f32[2,592,1024]{2,1,0:T(8,128)} fusion(bf16[2,592,4096]{2,1,0:T(8,128)(2,1)} %get-tuple-element.105, bf16[1024,4096]{1,0:T(8,128)(2,1)S(1)} %bitcast.255), kind=kOutput, calls=%fused_computation.19 | convolution fusion | flops 9932111872 | bytes 22937600 | tf_op jit(solution)/shard_map/bsf,df->bsd/dot_general | solution.py:727
  309.0 7.0 %collective-permute-done.15 = bf16[4,32,4096]{2,1,0:T(8,128)(2,1)} collective-permute-done((bf16[4,32,4096]{2,1,0:T(8,128)(2,1)S(1)}, bf16[4,32,4096]{2,1,0:T(8,128)(2,1)}, u32[]{:S(2)}, u32[]{:S(2)}) %collective-permute-start.15) | collective-permute-done | bytes 1048608 | tf_op jit(solution)/shard_map/ppermute | solution.py:415
  317.6 8.4 %fusion.6 = bf16[4,2,64,4096]{3,2,0,1:T(8,128)(2,1)} fusion(bf16[4,2,64,4096]{3,2,0,1:T(8,128)(2,1)} %collective-permute-done.16, f32[4,2,2,64,4096]{4,3,2,1,0:T(8,128)} %bitcast.271, s32[]{:T(128)S(6)} %select_n.186), kind=kLoop, calls=%fused_computation.13 | loop fusion | flops 6291456 | bytes 16777220 | tf_op jit(solution)/shard_map/convert_element_type | solution.py:546
  326.0 3.8 multiply_reduce_fusion.1
  329.8 4.5 fusion.90
  334.4 2.9 fusion.45.g_ref
  337.8 4.4 fusion.52
  352.8 5.5 collective-permute-done.17
  365.5 16.0 %add_multiply_fusion.1 = f32[2,592,1024]{2,1,0:T(8,128)S(1)} fusion(f32[2,592,1024]{2,1,0:T(8,128)} %copy-done.12, f32[1024]{0:T(1024)S(1)} %copy-done.41, f32[2,592]{1,0:T(2,128)S(1)} %copy-done.39, bf16[2,592,4096]{2,1,0:T(8,128)(2,1)} %copy-done.50, bf16[1024,4096]{1,0:T(8,128)(2,1)} %copy-done.3), kind=kOutput, calls=%fused_computation.55 | convolution fusion | flops 9935749120 | bytes 27796096 | tf_op jit(solution)/shard_map/bsf,df->bsd/dot_general | solution.py:737
  397.2 46.4 %attention_backward.1 = bf16[2,592,3072]{2,1,0:T(8,128)(2,1)S(1)} custom-call(s32[2]{0:T(128)S(1)} %fusion.75.lengths, bf16[2,592,3072]{2,1,0:T(8,128)(2,1)} %add_convert_fusion.q_ref.k_ref.v_ref, bf16[2,592,3072]{2,1,0:T(8,128)(2,1)} %add_convert_fusion.q_ref.k_ref.v_ref, bf16[2,592,3072]{2,1,0:T(8,128)(2,1)} %add_convert_fusion.q_ref.k_ref.v_ref, ...), custom_call_target="tpu_custom_call" | custom-call | flops 14355005440 | bytes 16973824 | tf_op jit(solution)/shard_map/attention_backward/pallas_call | solution.py:391
  448.5 5.7 copy.74
  460.9 8.5 %fusion.103 = f32[1024,3072,1]{1,0,2:T(8,128)S(1)} fusion(bf16[2,592,1024]{2,1,0:T(8,128)(2,1)S(1)} %copy-done.24, bf16[2,592,3072]{2,1,0:T(8,128)(2,1)S(1)} %attention_backward.1), kind=kOutput, calls=%fused_computation.256 | convolution fusion | flops 7449083904 | bytes 22282240 | tf_op jit(solution)/shard_map/bsd,bsc->dc/dot_general | solution.py:748
  469.3 4.6 copy-done.20
  476.1 4.1 collective-permute-done.30
  484.2 9.7 %fusion.102 = f32[2,592,1024]{2,1,0:T(8,128)} fusion(bf16[2,592,3072]{2,1,0:T(8,128)(2,1)S(1)} %attention_backward.1, bf16[1024,3072,1]{1,0,2:T(8,128)(2,1)S(1)} %bitcast.259), kind=kOutput, calls=%fused_computation.255 | convolution fusion | flops 7449083904 | bytes 18415616 | tf_op jit(solution)/shard_map/bsc,dc->bsd/dot_general | solution.py:750
  501.2 4.1 fusion.15
  505.3 4.0 fusion.28
  515.2 3.5 fusion.27
  519.4 11.8 %collective-permute-done.41 = bf16[4,32,3072]{2,1,0:T(8,128)(2,1)S(1)} collective-permute-done((bf16[4,32,3072]{2,1,0:T(8,128)(2,1)S(1)}, bf16[4,32,3072]{2,1,0:T(8,128)(2,1)S(1)}, u32[]{:S(2)}, u32[]{:S(2)}) %collective-permute-start.41) | collective-permute-done | bytes 786464 | tf_op jit(solution)/shard_map/ppermute | solution.py:415
  545.9 8.7 %collective-permute-done.44 = bf16[4,32,1536]{2,1,0:T(8,128)(2,1)S(1)} collective-permute-done((bf16[4,32,1536]{2,1,0:T(8,128)(2,1)S(1)}, bf16[4,32,1536]{2,1,0:T(8,128)(2,1)S(1)}, u32[]{:S(2)}, u32[]{:S(2)}) %collective-permute-start.44) | collective-permute-done | bytes 393248 | tf_op jit(solution)/shard_map/ppermute | solution.py:415
  561.2 10.5 %collective-permute-done.47 = f32[4,2,1,192]{3,2,1,0:T(1,128)S(1)} collective-permute-done((f32[4,2,1,192]{3,2,1,0:T(1,128)S(1)}, f32[4,2,1,192]{3,2,1,0:T(1,128)S(1)}, u32[]{:S(2)}, u32[]{:S(2)}) %collective-permute-start.47) | collective-permute-done | bytes 6176 | tf_op jit(solution)/shard_map/ppermute | solution.py:415
  573.1 6.0 %collective-permute-done.49 = bf16[64,1536]{1,0:T(8,128)(2,1)S(1)} collective-permute-done((bf16[64,1536]{1,0:T(8,128)(2,1)S(1)}, bf16[64,1536]{1,0:T(8,128)(2,1)S(1)}, u32[]{:S(2)}, u32[]{:S(2)}) %collective-permute-start.49) | collective-permute-done | bytes 196640 | tf_op jit(solution)/shard_map/ppermute | solution.py:420
  587.8 5.7 copy.75
  (391 shorter events, 156.9 us)
Async XLA Ops:
  7.3 160.7 %all-gather.3.cloned.1.call-start = ((), (), s32[]{:S(2)}) async-start(), calls=%async_computation | async-start | bytes 10813440 | tf_op jit(solution)/shard_map/all_gather | solution.py:692
  13.0 31.9 %collective-permute-start.3 = (bf16[2,320,1024]{2,1,0:T(8,128)(2,1)S(1)}, bf16[2,320,1024]{2,1,0:T(8,128)(2,1)}, u32[]{:S(2)}, u32[]{:S(2)}) collective-permute-start(bf16[2,320,1024]{2,1,0:T(8,128)(2,1)S(1)} %bitcast.279), channel_id=1, source_target_pairs={{0,1},{1,0},{2,3},{3,2},{4,5},{5,4},{6,7},{7,6},{8,9},{9,8},{10,11... | collective-permute-start | bytes 3932168 | tf_op jit(solution)/shard_map/ppermute | solution.py:592
  16.8 9.4 %collective-permute-start.2 = (bf16[64,1664]{1,0:T(8,128)(2,1)S(1)}, bf16[64,1664]{1,0:T(8,128)(2,1)S(1)}, u32[]{:S(2)}, u32[]{:S(2)}) collective-permute-start(bf16[64,1664]{1,0:T(8,128)(2,1)S(1)} %get-tuple-element.243), channel_id=1, source_target_pairs={{0,24},{2,26},{4,28},{6,30},{8,0},{10,2},{12,4},{14,6},{16,8},{18,... | collective-permute-start | bytes 638984 | tf_op jit(solution)/shard_map/ppermute | solution.py:420
  20.4 17.9 %collective-permute-start.1 = (bf16[64,1664]{1,0:T(8,128)(2,1)S(1)}, bf16[64,1664]{1,0:T(8,128)(2,1)}, u32[]{:S(2)}, u32[]{:S(2)}) collective-permute-start(bf16[64,1664]{1,0:T(8,128)(2,1)S(1)} %get-tuple-element.243), channel_id=1, source_target_pairs={{0,16},{2,18},{4,20},{6,22},{8,24},{10,26},{12,28},{14,30},{16,0},... | collective-permute-start | bytes 638984 | tf_op jit(solution)/shard_map/ppermute | solution.py:420
  20.4 17.9 %collective-permute-start = (bf16[64,1664]{1,0:T(8,128)(2,1)S(1)}, bf16[64,1664]{1,0:T(8,128)(2,1)}, u32[]{:S(2)}, u32[]{:S(2)}) collective-permute-start(bf16[64,1664]{1,0:T(8,128)(2,1)S(1)} %get-tuple-element.243), channel_id=1, source_target_pairs={{0,8},{2,10},{4,12},{6,14},{8,16},{10,18},{12,20},{14,22},{16,24},... | collective-permute-start | bytes 638984 | tf_op jit(solution)/shard_map/ppermute | solution.py:420
  48.2 173.8 %all-gather.5.cloned.1.call-start = ((), (), s32[]{:S(2)}) async-start(), calls=%async_computation.1 | async-start | bytes 8650752 | tf_op jit(solution)/shard_map/all_gather | solution.py:695
  49.1 11.1 %collective-permute-start.4 = (bf16[4,32,1664]{2,1,0:T(8,128)(2,1)S(1)}, bf16[4,32,1664]{2,1,0:T(8,128)(2,1)S(1)}, u32[]{:S(2)}, u32[]{:S(2)}) collective-permute-start(bf16[4,32,1664]{2,1,0:T(8,128)(2,1)S(1)} %get-tuple-element.235), channel_id=1, source_target_pairs={{0,4},{2,6},{4,0},{6,2},{8,12},{10,14},{12,8},{14,10},{16,20},{18,... | collective-permute-start | bytes 1277960 | tf_op jit(solution)/shard_map/ppermute | solution.py:415
  50.9 12.9 %collective-permute-start.6 = (bf16[4,32,1664]{2,1,0:T(8,128)(2,1)S(1)}, bf16[4,32,1664]{2,1,0:T(8,128)(2,1)S(1)}, u32[]{:S(2)}, u32[]{:S(2)}) collective-permute-start(bf16[4,32,1664]{2,1,0:T(8,128)(2,1)S(1)} %get-tuple-element.234), channel_id=1, source_target_pairs={{0,1},{1,0},{2,3},{3,2},{4,5},{5,4},{6,7},{7,6},{8,9},{9,8},{10,11... | collective-permute-start | bytes 1277960 | tf_op jit(solution)/shard_map/ppermute | solution.py:415
  60.3 24.9 %collective-permute-start.5 = (bf16[2,4,32,1664]{3,2,1,0:T(8,128)(2,1)S(1)}, bf16[2,4,32,1664]{3,2,1,0:T(8,128)(2,1)S(1)}, u32[]{:S(2)}, u32[]{:S(2)}) collective-permute-start(bf16[2,4,32,1664]{3,2,1,0:T(8,128)(2,1)S(1)} %pad_maximum_fusion.3.refs_0_), channel_id=1, source_target_pairs={{0,1},{1,0},{2,3},{3,2},{4,5},{5,4},{6,7},{7,6},{8,9},{9,8},{10,11... | collective-permute-start | bytes 2555912 | tf_op jit(solution)/shard_map/ppermute | solution.py:415
  63.9 21.3 %collective-permute-start.7 = (bf16[2,4,32,1664]{3,2,1,0:T(8,128)(2,1)S(1)}, bf16[2,4,32,1664]{3,2,1,0:T(8,128)(2,1)S(1)}, u32[]{:S(2)}, u32[]{:S(2)}) collective-permute-start(bf16[2,4,32,1664]{3,2,1,0:T(8,128)(2,1)S(1)} %pad_maximum_fusion.4.refs_2_), channel_id=1, source_target_pairs={{0,4},{2,6},{4,0},{6,2},{8,12},{10,14},{12,8},{14,10},{16,20},{18,... | collective-permute-start | bytes 2555912 | tf_op jit(solution)/shard_map/ppermute | solution.py:415
  64.7 25.5 %collective-permute-start.8 = (bf16[2,4,32,1664]{3,2,1,0:T(8,128)(2,1)S(1)}, bf16[2,4,32,1664]{3,2,1,0:T(8,128)(2,1)S(1)}, u32[]{:S(2)}, u32[]{:S(2)}) collective-permute-start(bf16[2,4,32,1664]{3,2,1,0:T(8,128)(2,1)S(1)} %pad_maximum_fusion.3.refs_0_), channel_id=1, source_target_pairs={{0,2},{2,0},{4,6},{6,4},{8,10},{10,8},{12,14},{14,12},{16,18},{18,... | collective-permute-start | bytes 2555912 | tf_op jit(solution)/shard_map/ppermute | solution.py:415
  64.8 25.5 %collective-permute-start.10 = (bf16[2,4,32,1664]{3,2,1,0:T(8,128)(2,1)S(1)}, bf16[2,4,32,1664]{3,2,1,0:T(8,128)(2,1)S(1)}, u32[]{:S(2)}, u32[]{:S(2)}) collective-permute-start(bf16[2,4,32,1664]{3,2,1,0:T(8,128)(2,1)S(1)} %pad_maximum_fusion.4.refs_2_), channel_id=1, source_target_pairs={{0,2},{2,0},{4,6},{6,4},{8,10},{10,8},{12,14},{14,12},{16,18},{18,... | collective-permute-start | bytes 2555912 | tf_op jit(solution)/shard_map/ppermute | solution.py:415
  119.1 43.0 %collective-permute-start.12 = (bf16[2,320,1024]{2,1,0:T(8,128)(2,1)}, bf16[2,320,1024]{2,1,0:T(8,128)(2,1)}, u32[]{:S(2)}, u32[]{:S(2)}) collective-permute-start(bf16[2,320,1024]{2,1,0:T(8,128)(2,1)} %dynamic-slice_bitcast_fusion), channel_id=1, source_target_pairs={{0,1},{1,0},{2,3},{3,2},{4,5},{5,4},{6,7},{7,6},{8,9},{9,8},{10,11... | collective-permute-start | bytes 3932168 | tf_op jit(solution)/shard_map/ppermute | solution.py:592
  236.5 40.2 %collective-permute-start.13 = (bf16[4,2,64,4096]{3,2,0,1:T(8,128)(2,1)}, bf16[4,2,64,4096]{3,2,0,1:T(8,128)(2,1)S(1)}, u32[]{:S(2)}, u32[]{:S(2)}) collective-permute-start(bf16[4,2,64,4096]{3,2,0,1:T(8,128)(2,1)} %fusion.31), channel_id=1, source_target_pairs={{0,2},{2,0},{4,6},{6,4},{8,10},{10,8},{12,14},{14,12},{16,18},{18,... | collective-permute-start | bytes 12582920 | tf_op jit(solution)/shard_map/ppermute | solution.py:415
  282.2 25.4 %collective-permute-start.14 = (bf16[4,2,32,2048]{3,2,0,1:T(8,128)(2,1)S(1)}, bf16[4,2,32,2048]{3,2,0,1:T(8,128)(2,1)S(1)}, u32[]{:S(2)}, u32[]{:S(2)}) collective-permute-start(bf16[4,2,32,2048]{3,2,0,1:T(8,128)(2,1)S(1)} %constant_dynamic-slice_fusion.29), channel_id=1, source_target_pairs={{0,1},{1,0},{2,3},{3,2},{4,5},{5,4},{6,7},{7,6},{8,9},{9,8},{10,11... | collective-permute-start | bytes 3145736 | tf_op jit(solution)/shard_map/ppermute | solution.py:415
  290.1 27.5 %collective-permute-start.16 = (bf16[4,2,64,4096]{3,2,0,1:T(8,128)(2,1)}, bf16[4,2,64,4096]{3,2,0,1:T(8,128)(2,1)}, u32[]{:S(2)}, u32[]{:S(2)}) collective-permute-start(bf16[4,2,64,4096]{3,2,0,1:T(8,128)(2,1)} %fusion.32), channel_id=1, source_target_pairs={{0,2},{2,0},{4,6},{6,4},{8,10},{10,8},{12,14},{14,12},{16,18},{18,... | collective-permute-start | bytes 12582920 | tf_op jit(solution)/shard_map/ppermute | solution.py:415
  290.4 25.5 %collective-permute-start.15 = (bf16[4,32,4096]{2,1,0:T(8,128)(2,1)S(1)}, bf16[4,32,4096]{2,1,0:T(8,128)(2,1)}, u32[]{:S(2)}, u32[]{:S(2)}) collective-permute-start(bf16[4,32,4096]{2,1,0:T(8,128)(2,1)S(1)} %dynamic-slice_bitcast_fusion.2), channel_id=1, source_target_pairs={{0,4},{2,6},{4,0},{6,2},{8,12},{10,14},{12,8},{14,10},{16,20},{18,... | collective-permute-start | bytes 3145736 | tf_op jit(solution)/shard_map/ppermute | solution.py:415
  343.1 15.2 %collective-permute-start.17 = (bf16[4,32,2048]{2,1,0:T(8,128)(2,1)}, bf16[4,32,2048]{2,1,0:T(8,128)(2,1)}, u32[]{:S(2)}, u32[]{:S(2)}) collective-permute-start(bf16[4,32,2048]{2,1,0:T(8,128)(2,1)} %dynamic-slice_bitcast_fusion.5), channel_id=1, source_target_pairs={{0,4},{2,6},{4,0},{6,2},{8,12},{10,14},{12,8},{14,10},{16,20},{18,... | collective-permute-start | bytes 1572872 | tf_op jit(solution)/shard_map/ppermute | solution.py:415
  344.8 15.1 %collective-permute-start.18 = (bf16[4,32,2048]{2,1,0:T(8,128)(2,1)}, bf16[4,32,2048]{2,1,0:T(8,128)(2,1)S(1)}, u32[]{:S(2)}, u32[]{:S(2)}) collective-permute-start(bf16[4,32,2048]{2,1,0:T(8,128)(2,1)} %constant_dynamic-slice_fusion.27), channel_id=1, source_target_pairs={{0,1},{1,0},{2,3},{3,2},{4,5},{5,4},{6,7},{7,6},{8,9},{9,8},{10,11... | collective-permute-start | bytes 1572872 | tf_op jit(solution)/shard_map/ppermute | solution.py:415
  347.7 38.7 %collective-permute-start.22 = (bf16[4,2,32,2048]{3,2,0,1:T(8,128)(2,1)}, bf16[4,2,32,2048]{3,2,0,1:T(8,128)(2,1)}, u32[]{:S(2)}, u32[]{:S(2)}) collective-permute-start(bf16[4,2,32,2048]{3,2,0,1:T(8,128)(2,1)} %constant_dynamic-slice_fusion.26), channel_id=1, source_target_pairs={{0,1},{1,0},{2,3},{3,2},{4,5},{5,4},{6,7},{7,6},{8,9},{9,8},{10,11... | collective-permute-start | bytes 3145736 | tf_op jit(solution)/shard_map/ppermute | solution.py:415
  349.6 38.7 %collective-permute-start.23 = (bf16[4,32,4096]{2,1,0:T(8,128)(2,1)}, bf16[4,32,4096]{2,1,0:T(8,128)(2,1)}, u32[]{:S(2)}, u32[]{:S(2)}) collective-permute-start(bf16[4,32,4096]{2,1,0:T(8,128)(2,1)} %dynamic-slice_bitcast_fusion.1), channel_id=1, source_target_pairs={{0,4},{2,6},{4,0},{6,2},{8,12},{10,14},{12,8},{14,10},{16,20},{18,... | collective-permute-start | bytes 3145736 | tf_op jit(solution)/shard_map/ppermute | solution.py:415
  361.2 20.4 %collective-permute-start.21 = (bf16[64,2048]{1,0:T(8,128)(2,1)S(1)}, bf16[64,2048]{1,0:T(8,128)(2,1)S(1)}, u32[]{:S(2)}, u32[]{:S(2)}) collective-permute-start(bf16[64,2048]{1,0:T(8,128)(2,1)S(1)} %get-tuple-element.230), channel_id=1, source_target_pairs={{0,24},{2,26},{4,28},{6,30},{8,0},{10,2},{12,4},{14,6},{16,8},{18,... | collective-permute-start | bytes 786440 | tf_op jit(solution)/shard_map/ppermute | solution.py:420
  363.1 21.2 %collective-permute-start.20 = (bf16[64,2048]{1,0:T(8,128)(2,1)S(1)}, bf16[64,2048]{1,0:T(8,128)(2,1)}, u32[]{:S(2)}, u32[]{:S(2)}) collective-permute-start(bf16[64,2048]{1,0:T(8,128)(2,1)S(1)} %get-tuple-element.231), channel_id=1, source_target_pairs={{0,16},{2,18},{4,20},{6,22},{8,24},{10,26},{12,28},{14,30},{16,0},... | collective-permute-start | bytes 786440 | tf_op jit(solution)/shard_map/ppermute | solution.py:420
  364.2 20.2 %collective-permute-start.19 = (bf16[64,2048]{1,0:T(8,128)(2,1)S(1)}, bf16[64,2048]{1,0:T(8,128)(2,1)}, u32[]{:S(2)}, u32[]{:S(2)}) collective-permute-start(bf16[64,2048]{1,0:T(8,128)(2,1)S(1)} %get-tuple-element.229), channel_id=1, source_target_pairs={{0,8},{2,10},{4,12},{6,14},{8,16},{10,18},{12,20},{14,22},{16,24},... | collective-permute-start | bytes 786440 | tf_op jit(solution)/shard_map/ppermute | solution.py:420
  390.1 53.8 %collective-permute-start.25 = (bf16[2,160,1024]{2,1,0:T(8,128)(2,1)S(1)}, bf16[2,160,1024]{2,1,0:T(8,128)(2,1)S(1)}, u32[]{:S(2)}, u32[]{:S(2)}) collective-permute-start(bf16[2,160,1024]{2,1,0:T(8,128)(2,1)S(1)} %get-tuple-element.223), channel_id=1, source_target_pairs={{0,1},{1,0},{2,3},{3,2},{4,5},{5,4},{6,7},{7,6},{8,9},{9,8},{10,11... | collective-permute-start | bytes 1966088 | tf_op jit(solution)/shard_map/ppermute | solution.py:415
  391.3 52.7 %collective-permute-start.24 = (bf16[2,160,1024]{2,1,0:T(8,128)(2,1)S(1)}, bf16[2,160,1024]{2,1,0:T(8,128)(2,1)S(1)}, u32[]{:S(2)}, u32[]{:S(2)}) collective-permute-start(bf16[2,160,1024]{2,1,0:T(8,128)(2,1)S(1)} %get-tuple-element.222), channel_id=1, source_target_pairs={{0,1},{1,0},{2,3},{3,2},{4,5},{5,4},{6,7},{7,6},{8,9},{9,8},{10,11... | collective-permute-start | bytes 1966088 | tf_op jit(solution)/shard_map/ppermute | solution.py:415
  392.2 51.4 %collective-permute-start.26 = (bf16[4,32,2048]{2,1,0:T(8,128)(2,1)S(1)}, bf16[4,32,2048]{2,1,0:T(8,128)(2,1)S(1)}, u32[]{:S(2)}, u32[]{:S(2)}) collective-permute-start(bf16[4,32,2048]{2,1,0:T(8,128)(2,1)S(1)} %dynamic-slice_bitcast_fusion.4), channel_id=1, source_target_pairs={{0,4},{2,6},{4,0},{6,2},{8,12},{10,14},{12,8},{14,10},{16,20},{18,... | collective-permute-start | bytes 1572872 | tf_op jit(solution)/shard_map/ppermute | solution.py:415
  393.5 50.3 %collective-permute-start.27 = (bf16[4,32,2048]{2,1,0:T(8,128)(2,1)S(1)}, bf16[4,32,2048]{2,1,0:T(8,128)(2,1)S(1)}, u32[]{:S(2)}, u32[]{:S(2)}) collective-permute-start(bf16[4,32,2048]{2,1,0:T(8,128)(2,1)S(1)} %constant_dynamic-slice_fusion.25), channel_id=1, source_target_pairs={{0,1},{1,0},{2,3},{3,2},{4,5},{5,4},{6,7},{7,6},{8,9},{9,8},{10,11... | collective-permute-start | bytes 1572872 | tf_op jit(solution)/shard_map/ppermute | solution.py:415
  397.2 48.0 %collective-permute-start.28 = (bf16[4,2,64,1024]{3,2,0,1:T(8,128)(2,1)}, bf16[4,2,64,1024]{3,2,0,1:T(8,128)(2,1)}, u32[]{:S(2)}, u32[]{:S(2)}) collective-permute-start(bf16[4,2,64,1024]{3,2,0,1:T(8,128)(2,1)} %fusion.55), channel_id=1, source_target_pairs={{0,2},{2,0},{4,6},{6,4},{8,10},{10,8},{12,14},{14,12},{16,18},{18,... | collective-permute-start | bytes 3145736 | tf_op jit(solution)/shard_map/ppermute | solution.py:415
  454.4 21.7 %collective-permute-start.31 = (bf16[64,2048]{1,0:T(8,128)(2,1)S(1)}, bf16[64,2048]{1,0:T(8,128)(2,1)S(1)}, u32[]{:S(2)}, u32[]{:S(2)}) collective-permute-start(bf16[64,2048]{1,0:T(8,128)(2,1)S(1)} %get-tuple-element.227), channel_id=1, source_target_pairs={{0,24},{2,26},{4,28},{6,30},{8,0},{10,2},{12,4},{14,6},{16,8},{18,... | collective-permute-start | bytes 786440 | tf_op jit(solution)/shard_map/ppermute | solution.py:420
  454.7 25.5 %collective-permute-start.30 = (bf16[64,2048]{1,0:T(8,128)(2,1)S(1)}, bf16[64,2048]{1,0:T(8,128)(2,1)S(1)}, u32[]{:S(2)}, u32[]{:S(2)}) collective-permute-start(bf16[64,2048]{1,0:T(8,128)(2,1)S(1)} %get-tuple-element.228), channel_id=1, source_target_pairs={{0,16},{2,18},{4,20},{6,22},{8,24},{10,26},{12,28},{14,30},{16,0},... | collective-permute-start | bytes 786440 | tf_op jit(solution)/shard_map/ppermute | solution.py:420
  456.4 23.8 %collective-permute-start.29 = (bf16[64,2048]{1,0:T(8,128)(2,1)S(1)}, bf16[64,2048]{1,0:T(8,128)(2,1)S(1)}, u32[]{:S(2)}, u32[]{:S(2)}) collective-permute-start(bf16[64,2048]{1,0:T(8,128)(2,1)S(1)} %get-tuple-element.226), channel_id=1, source_target_pairs={{0,8},{2,10},{4,12},{6,14},{8,16},{10,18},{12,20},{14,22},{16,24},... | collective-permute-start | bytes 786440 | tf_op jit(solution)/shard_map/ppermute | solution.py:420
  458.6 22.6 %collective-permute-start.32 = (bf16[4,2,32,512]{3,2,0,1:T(8,128)(2,1)S(1)}, bf16[4,2,32,512]{3,2,0,1:T(8,128)(2,1)S(1)}, u32[]{:S(2)}, u32[]{:S(2)}) collective-permute-start(bf16[4,2,32,512]{3,2,0,1:T(8,128)(2,1)S(1)} %constant_dynamic-slice_fusion.23), channel_id=1, source_target_pairs={{0,1},{1,0},{2,3},{3,2},{4,5},{5,4},{6,7},{7,6},{8,9},{9,8},{10,11... | collective-permute-start | bytes 786440 | tf_op jit(solution)/shard_map/ppermute | solution.py:415
  459.9 21.3 %collective-permute-start.33 = (bf16[4,32,1024]{2,1,0:T(8,128)(2,1)S(1)}, bf16[4,32,1024]{2,1,0:T(8,128)(2,1)S(1)}, u32[]{:S(2)}, u32[]{:S(2)}) collective-permute-start(bf16[4,32,1024]{2,1,0:T(8,128)(2,1)S(1)} %dynamic-slice_bitcast_fusion.7), channel_id=1, source_target_pairs={{0,4},{2,6},{4,0},{6,2},{8,12},{10,14},{12,8},{14,10},{16,20},{18,... | collective-permute-start | bytes 786440 | tf_op jit(solution)/shard_map/ppermute | solution.py:415
  476.1 25.1 %collective-permute-start.36 = (bf16[4,2,64,3072]{3,2,0,1:T(8,128)(2,1)}, bf16[4,2,64,3072]{3,2,0,1:T(8,128)(2,1)S(1)}, u32[]{:S(2)}, u32[]{:S(2)}) collective-permute-start(bf16[4,2,64,3072]{3,2,0,1:T(8,128)(2,1)} %fusion.33), channel_id=1, source_target_pairs={{0,2},{2,0},{4,6},{6,4},{8,10},{10,8},{12,14},{14,12},{16,18},{18,... | collective-permute-start | bytes 9437192 | tf_op jit(solution)/shard_map/ppermute | solution.py:415
  482.0 16.3 %collective-permute-start.34 = (bf16[4,32,512]{2,1,0:T(8,128)(2,1)}, bf16[4,32,512]{2,1,0:T(8,128)(2,1)S(1)}, u32[]{:S(2)}, u32[]{:S(2)}) collective-permute-start(bf16[4,32,512]{2,1,0:T(8,128)(2,1)} %dynamic-slice_bitcast_fusion.17), channel_id=1, source_target_pairs={{0,4},{2,6},{4,0},{6,2},{8,12},{10,14},{12,8},{14,10},{16,20},{18,... | collective-permute-start | bytes 393224 | tf_op jit(solution)/shard_map/ppermute | solution.py:415
  509.4 9.3 %collective-permute-start.39 = (bf16[64,512]{1,0:T(8,128)(2,1)S(1)}, bf16[64,512]{1,0:T(8,128)(2,1)S(1)}, u32[]{:S(2)}, u32[]{:S(2)}) collective-permute-start(bf16[64,512]{1,0:T(8,128)(2,1)S(1)} %get-tuple-element.240), channel_id=1, source_target_pairs={{0,24},{2,26},{4,28},{6,30},{8,0},{10,2},{12,4},{14,6},{16,8},{18,... | collective-permute-start | bytes 196616 | tf_op jit(solution)/shard_map/ppermute | solution.py:420
  512.9 18.5 %collective-permute-start.40 = (bf16[4,2,32,1536]{3,2,0,1:T(8,128)(2,1)S(1)}, bf16[4,2,32,1536]{3,2,0,1:T(8,128)(2,1)S(1)}, u32[]{:S(2)}, u32[]{:S(2)}) collective-permute-start(bf16[4,2,32,1536]{3,2,0,1:T(8,128)(2,1)S(1)} %constant_dynamic-slice_fusion.19), channel_id=1, source_target_pairs={{0,1},{1,0},{2,3},{3,2},{4,5},{5,4},{6,7},{7,6},{8,9},{9,8},{10,11... | collective-permute-start | bytes 2359304 | tf_op jit(solution)/shard_map/ppermute | solution.py:415
  514.0 17.3 %collective-permute-start.41 = (bf16[4,32,3072]{2,1,0:T(8,128)(2,1)S(1)}, bf16[4,32,3072]{2,1,0:T(8,128)(2,1)S(1)}, u32[]{:S(2)}, u32[]{:S(2)}) collective-permute-start(bf16[4,32,3072]{2,1,0:T(8,128)(2,1)S(1)} %dynamic-slice_bitcast_fusion.3), channel_id=1, source_target_pairs={{0,4},{2,6},{4,0},{6,2},{8,12},{10,14},{12,8},{14,10},{16,20},{18,... | collective-permute-start | bytes 2359304 | tf_op jit(solution)/shard_map/ppermute | solution.py:415
  532.1 23.4 %collective-permute-start.42 = (bf16[2,160,1024]{2,1,0:T(8,128)(2,1)S(1)}, bf16[2,160,1024]{2,1,0:T(8,128)(2,1)S(1)}, u32[]{:S(2)}, u32[]{:S(2)}) collective-permute-start(bf16[2,160,1024]{2,1,0:T(8,128)(2,1)S(1)} %get-tuple-element.221), channel_id=1, source_target_pairs={{0,1},{1,0},{2,3},{3,2},{4,5},{5,4},{6,7},{7,6},{8,9},{9,8},{10,11... | collective-permute-start | bytes 1966088 | tf_op jit(solution)/shard_map/ppermute | solution.py:415
  543.0 11.6 %collective-permute-start.44 = (bf16[4,32,1536]{2,1,0:T(8,128)(2,1)S(1)}, bf16[4,32,1536]{2,1,0:T(8,128)(2,1)S(1)}, u32[]{:S(2)}, u32[]{:S(2)}) collective-permute-start(bf16[4,32,1536]{2,1,0:T(8,128)(2,1)S(1)} %dynamic-slice_bitcast_fusion.6), channel_id=1, source_target_pairs={{0,4},{2,6},{4,0},{6,2},{8,12},{10,14},{12,8},{14,10},{16,20},{18,... | collective-permute-start | bytes 1179656 | tf_op jit(solution)/shard_map/ppermute | solution.py:415
  544.0 11.3 %collective-permute-start.45 = (bf16[4,32,1536]{2,1,0:T(8,128)(2,1)S(1)}, bf16[4,32,1536]{2,1,0:T(8,128)(2,1)S(1)}, u32[]{:S(2)}, u32[]{:S(2)}) collective-permute-start(bf16[4,32,1536]{2,1,0:T(8,128)(2,1)S(1)} %constant_dynamic-slice_fusion.17), channel_id=1, source_target_pairs={{0,1},{1,0},{2,3},{3,2},{4,5},{5,4},{6,7},{7,6},{8,9},{9,8},{10,11... | collective-permute-start | bytes 1179656 | tf_op jit(solution)/shard_map/ppermute | solution.py:415
  555.4 23.8 %collective-permute-start.46 = (bf16[2,160,1024]{2,1,0:T(8,128)(2,1)S(1)}, bf16[2,160,1024]{2,1,0:T(8,128)(2,1)S(1)}, u32[]{:S(2)}, u32[]{:S(2)}) collective-permute-start(bf16[2,160,1024]{2,1,0:T(8,128)(2,1)S(1)} %get-tuple-element.141), channel_id=1, source_target_pairs={{0,1},{1,0},{2,3},{3,2},{4,5},{5,4},{6,7},{7,6},{8,9},{9,8},{10,11... | collective-permute-start | bytes 1966088 | tf_op jit(solution)/shard_map/ppermute | solution.py:415
  556.7 15.0 %collective-permute-start.47 = (f32[4,2,1,192]{3,2,1,0:T(1,128)S(1)}, f32[4,2,1,192]{3,2,1,0:T(1,128)S(1)}, u32[]{:S(2)}, u32[]{:S(2)}) collective-permute-start(f32[4,2,1,192]{3,2,1,0:T(1,128)S(1)} %constant_dynamic-slice_fusion.15), channel_id=1, source_target_pairs={{0,1},{1,0},{2,3},{3,2},{4,5},{5,4},{6,7},{7,6},{8,9},{9,8},{10,11... | collective-permute-start | bytes 18440 | tf_op jit(solution)/shard_map/ppermute | solution.py:415
  557.7 14.7 %collective-permute-start.48 = (f32[4,1,384]{2,1,0:T(1,128)S(1)}, f32[4,1,384]{2,1,0:T(1,128)S(1)}, u32[]{:S(2)}, u32[]{:S(2)}) collective-permute-start(f32[4,1,384]{2,1,0:T(1,128)S(1)} %fusion.74), channel_id=1, source_target_pairs={{0,4},{2,6},{4,0},{6,2},{8,12},{10,14},{12,8},{14,10},{16,20},{18,... | collective-permute-start | bytes 18440 | tf_op jit(solution)/shard_map/ppermute | solution.py:415
  558.9 13.5 %collective-permute-start.51 = (bf16[64,1536]{1,0:T(8,128)(2,1)S(1)}, bf16[64,1536]{1,0:T(8,128)(2,1)S(1)}, u32[]{:S(2)}, u32[]{:S(2)}) collective-permute-start(bf16[64,1536]{1,0:T(8,128)(2,1)S(1)} %get-tuple-element.237), channel_id=1, source_target_pairs={{0,24},{2,26},{4,28},{6,30},{8,0},{10,2},{12,4},{14,6},{16,8},{18,... | collective-permute-start | bytes 589832 | tf_op jit(solution)/shard_map/ppermute | solution.py:420
  561.1 12.0 %collective-permute-start.50 = (bf16[64,1536]{1,0:T(8,128)(2,1)S(1)}, bf16[64,1536]{1,0:T(8,128)(2,1)S(1)}, u32[]{:S(2)}, u32[]{:S(2)}) collective-permute-start(bf16[64,1536]{1,0:T(8,128)(2,1)S(1)} %get-tuple-element.238), channel_id=1, source_target_pairs={{0,16},{2,18},{4,20},{6,22},{8,24},{10,26},{12,28},{14,30},{16,0},... | collective-permute-start | bytes 589832 | tf_op jit(solution)/shard_map/ppermute | solution.py:420
  584.1 10.8 %collective-permute-start.56 = (f32[2,192]{1,0:T(2,128)S(1)}, f32[2,192]{1,0:T(2,128)S(1)}, u32[]{:S(2)}, u32[]{:S(2)}) collective-permute-start(f32[2,192]{1,0:T(2,128)S(1)} %get-tuple-element.256), channel_id=1, source_target_pairs={{0,24},{2,26},{4,28},{6,30},{8,0},{10,2},{12,4},{14,6},{16,8},{18,... | collective-permute-start | bytes 4616 | tf_op jit(solution)/shard_map/ppermute | solution.py:420
  (76 other events, 747.8 us)
Sparse Core Ops, SparseCore 0:
  48.3 91.7 all-gather.2
  143.0 79.0 all-gather.4
